TPU v7x, 32 devices: a whole 2x2x4 slice. The times are simulated.
32 devices in a mesh: dp: 8 (over z, x), tensor: 4 (over y, core).
Axes of the slice: x: 2, y: 2, z: 4, core: 2. Of those that a mesh axis runs over, the one named last changes fastest.
Arguments:
- block_input: bfloat16 [2, 8192, 1024], P(None, ('dp', 'tensor')), may hold values from -6 to 6
- cotangent: bfloat16 [2, 8192, 1024], P(None, 'dp'), may hold values from -6 to 6
- parent: int32 [2, 2, 16], replicated, may hold values from -1 to 15, as said below
- pre_attn_gain: float32 [1024], replicated, may hold values from 0.25 to 1.75
- qkv_weight: bfloat16 [3, 1024, 1024], P(None, None, 'tensor'), may hold values from -0.1875 to 0.1875
- head_scale: float32 [16], P('tensor'), may hold values from 0.5 to 2
- out_weight: bfloat16 [1024, 1024], P('tensor'), may hold values from -0.1875 to 0.1875
- post_attn_gain: float32 [1024], replicated, may hold values from 0.25 to 1.75
- pre_ffn_gain: float32 [1024], replicated, may hold values from 0.25 to 1.75
- fc1_weight: bfloat16 [1024, 4096], P(None, 'tensor'), may hold values from -0.1875 to 0.1875
- ffn_norm_gain: float32 [4096], P('tensor'), may hold values from 0.25 to 1.75
- fc2_weight: bfloat16 [4096, 1024], P('tensor'), may hold values from -0.09375 to 0.09375
Outputs:
- block_output: bfloat16 [2, 8192, 1024], P(None, ('dp', 'tensor'))
- input_grad: float32 [2, 8192, 1024], P(None, ('dp', 'tensor'))
- pre_attn_gain_grad: float32 [1024], replicated
- qkv_weight_grad: float32 [3, 1024, 1024], P(None, None, 'tensor')
- head_scale_grad: float32 [16], P('tensor')
- out_weight_grad: float32 [1024, 1024], P('tensor')
- post_attn_gain_grad: float32 [1024], replicated
- pre_ffn_gain_grad: float32 [1024], replicated
- fc1_weight_grad: float32 [1024, 4096], P(None, 'tensor')
- ffn_norm_gain_grad: float32 [4096], P('tensor')
- fc2_weight_grad: float32 [4096, 1024], P('tensor')
Inputs may be any that keep to these rules, and one draw needn't show every extreme that they name: In each tree exactly one segment has parent -1; it heads a chain of 4 segments, each the parent of the next; 4 branch segments have the chain's last segment as parent; the other 8 segments are leaves, two under each branch. Which position holds which segment is drawn anew for every tree.
All inputs are finite; a program needn't handle non-finite values.
Results may differ from a plain program's by a relative error of at most 0.017.
The roundings to bfloat16 on the way count: a program that leaves them out, or rounds other values in their place, can miss the bound.
Values may be sent and summed in bfloat16 or wider, within the bound.
A program may use at most 320 MiB of HBM per device.

v0:
```python
from functools import partial

import jax
import jax.numpy as jnp
from jax import lax
from jax.sharding import PartitionSpec as P

HEAD_DIM = 64
FFN = 4096
SEG_LEN = 256
SEGS = 16
GROUP = 4
MICRO = 2


EPSILON = 1e-05
NEGATIVE = -1e30


def from_partner(value, axis, distance):
    mask = 2**distance
    pairs = [(source, source ^ mask) for source in range(lax.axis_size(axis))]
    return lax.ppermute(value, axis, pairs)


def normalize(values):
    center = values - jnp.mean(values, axis=-1, keepdims=True)
    inverse = lax.rsqrt(jnp.mean(center * center, axis=-1, keepdims=True) + EPSILON)
    return (center * inverse, inverse)


def norm_backward(grad_hat, normed, inverse):
    mean_grad = jnp.mean(grad_hat, axis=-1, keepdims=True)
    mean_cross = jnp.mean(grad_hat * normed, axis=-1, keepdims=True)
    return inverse * (grad_hat - mean_grad - normed * mean_cross)


def ancestors(parent_row):
    seg_index = jnp.arange(SEGS, dtype=jnp.int32)

    def climb(step_index, running):
        current, seg_table = running
        reached = seg_index[None, :] == current[:, None]
        upward = jnp.sum(jnp.where(reached, parent_row[None, :], 0), axis=1)
        return (jnp.where(current >= 0, upward, -1), jnp.logical_or(seg_table, reached))

    start = (parent_row, jnp.zeros((SEGS, SEGS), dtype=jnp.bool_))
    return lax.fori_loop(0, SEGS, climb, start)[1]


def token_mask(seg_table, first_row, row_count, key_count):
    query_pos = first_row + jnp.arange(row_count, dtype=jnp.int32)
    key_pos = jnp.arange(key_count, dtype=jnp.int32)
    query_seg = query_pos // SEG_LEN
    key_seg = key_pos // SEG_LEN
    onehot = (query_seg[:, None] == jnp.arange(SEGS, dtype=jnp.int32)[None, :]).astype(jnp.float32)
    ancestor_hit = jnp.dot(onehot, seg_table.astype(jnp.float32)) > 0.5
    ancestor_hit = jnp.broadcast_to(ancestor_hit[:, :, None], (row_count, SEGS, SEG_LEN)).reshape(
        row_count, key_count
    )
    inside = jnp.logical_and(
        query_seg[:, None] == key_seg[None, :], key_pos[None, :] <= query_pos[:, None]
    )
    return jnp.logical_or(ancestor_hit, inside)


def masked_scores(query_block, tree_keys, seg_table, first_row):
    allowed = token_mask(seg_table, first_row, query_block.shape[0], tree_keys.shape[0])
    scores = jnp.einsum(
        "qhd,khd->hqk", query_block, tree_keys, preferred_element_type=jnp.float32
    ) * HEAD_DIM ** (-0.5)
    return jnp.where(allowed[None], scores, NEGATIVE)


def attend_forward(query_block, first_row, tree_keys, tree_values, seg_table):
    scores = masked_scores(query_block, tree_keys, seg_table, first_row)
    row_top = jnp.max(scores, axis=-1, keepdims=True)
    log_total = row_top + jnp.log(jnp.sum(jnp.exp(scores - row_top), axis=-1, keepdims=True))
    soft_probs = jnp.exp(scores - log_total)
    output = jnp.einsum(
        "hqk,khd->qhd",
        soft_probs.astype(jnp.bfloat16),
        tree_values,
        preferred_element_type=jnp.float32,
    )
    return (output, log_total)


def attend_backward(
    query_block, grad_output, log_total, first_row, tree_keys, tree_values, seg_table
):
    scores = masked_scores(query_block, tree_keys, seg_table, first_row)
    soft_probs = jnp.exp(scores - log_total)
    grad_probs = jnp.einsum(
        "qhd,khd->hqk", grad_output, tree_values, preferred_element_type=jnp.float32
    )
    row_total = jnp.sum(soft_probs * grad_probs, axis=-1, keepdims=True)
    grad_scores = (soft_probs * (grad_probs - row_total)).astype(jnp.bfloat16)
    scale_factor = HEAD_DIM ** (-0.5)
    grad_query = (
        jnp.einsum("hqk,khd->qhd", grad_scores, tree_keys, preferred_element_type=jnp.float32)
        * scale_factor
    ).astype(jnp.bfloat16)
    grad_keys = (
        jnp.einsum("hqk,qhd->khd", grad_scores, query_block, preferred_element_type=jnp.float32)
        * scale_factor
    )
    grad_values = jnp.einsum(
        "hqk,qhd->khd",
        soft_probs.astype(jnp.bfloat16),
        grad_output,
        preferred_element_type=jnp.float32,
    )
    return (grad_query, grad_keys, grad_values)


def group_gather(own_block, member, bit_order):
    gathered = own_block
    for bit_index in bit_order:
        partner = from_partner(gathered, "dp", bit_index)
        upper_bit = jnp.right_shift(member, bit_index) % 2 == 1
        gathered = jnp.where(
            upper_bit, jnp.stack([partner, gathered]), jnp.stack([gathered, partner])
        )
    placed_bits = list(bit_order)[::-1]
    ranked_axes = sorted(range(len(placed_bits)), key=lambda position: -placed_bits[position])
    gathered = jnp.transpose(
        gathered, tuple(ranked_axes) + tuple(range(len(placed_bits), gathered.ndim))
    )
    return gathered.reshape((-1,) + own_block.shape[1:])


def group_reduce(spread, member, bit_order, tokens):
    bits_left = sorted(bit_order, reverse=True)
    shaped = spread.reshape((2,) * len(bits_left) + (tokens,) + spread.shape[1:])
    for bit_index in list(bit_order)[::-1]:
        axis_place = len([other_bit for other_bit in bits_left if other_bit > bit_index])
        upper_bit = jnp.right_shift(member, bit_index) % 2 == 1
        lower_half = jnp.take(shaped, 0, axis=axis_place)
        upper_half = jnp.take(shaped, 1, axis=axis_place)
        kept_half = jnp.where(upper_bit, upper_half, lower_half)
        outgoing = jnp.where(upper_bit, lower_half, upper_half)
        shaped = kept_half + from_partner(outgoing.astype(jnp.bfloat16), "dp", bit_index).astype(
            outgoing.dtype
        )
        bits_left = [other_bit for other_bit in bits_left if other_bit != bit_index]
    return shaped


def sum_weights(weight_grads):
    return lax.psum(weight_grads, "dp")


def body(
    block_input,
    cotangent,
    parent,
    pre_attn_gain,
    qkv_weight,
    head_scale,
    out_weight,
    post_attn_gain,
    pre_ffn_gain,
    fc1_weight,
    ffn_norm_gain,
    fc2_weight,
):
    member = lax.axis_index("dp") % GROUP
    tree_index = lax.axis_index("dp") // GROUP
    shard_index = lax.axis_index("tensor")
    row_count = block_input.shape[1]
    tokens = cotangent.shape[1]
    head_count = head_scale.shape[0]
    local_width = qkv_weight.shape[2]
    tree_tokens = tokens * GROUP
    block_rows = min(512, tokens)
    block_count = tokens // block_rows
    bit_count = GROUP.bit_length() - 1
    bit_order = list(range(bit_count))
    block_starts = member * tokens + block_rows * jnp.arange(block_count, dtype=jnp.int32)
    outputs = []
    input_grads = []
    weight_totals = None
    gain_totals = (
        jnp.zeros(pre_attn_gain.shape, jnp.float32),
        jnp.zeros(post_attn_gain.shape, jnp.float32),
        jnp.zeros(pre_ffn_gain.shape, jnp.float32),
    )
    for micro_index in range(MICRO):
        seg_table = ancestors(
            lax.dynamic_index_in_dim(parent[micro_index], tree_index, 0, keepdims=False)
        )
        rows_in = block_input[micro_index].astype(jnp.float32)
        normed_one, inverse_one = normalize(rows_in)
        hidden_one = (normed_one * pre_attn_gain).astype(jnp.bfloat16)
        full_one = lax.all_gather(hidden_one, "tensor", axis=0, tiled=True)
        projected = jnp.einsum(
            "td,ide->ite", full_one, qkv_weight, preferred_element_type=jnp.float32
        ).astype(jnp.bfloat16)
        query_blocks = projected[0].reshape(block_count, block_rows, head_count, HEAD_DIM)
        key_value = jnp.stack([projected[1], projected[2]], axis=1)
        tree_pairs = group_gather(key_value, member, bit_order)
        tree_keys = tree_pairs[:, 0].reshape(tree_tokens, head_count, HEAD_DIM)
        tree_values = tree_pairs[:, 1].reshape(tree_tokens, head_count, HEAD_DIM)

        def forward_block(operands):
            return attend_forward(operands[0], operands[1], tree_keys, tree_values, seg_table)

        attended, log_totals = lax.map(forward_block, (query_blocks, block_starts))
        attended = attended.reshape(tokens, head_count, HEAD_DIM)
        scaled = (
            (attended * head_scale[None, :, None]).astype(jnp.bfloat16).reshape(tokens, local_width)
        )
        mixed = lax.psum_scatter(
            jnp.dot(scaled, out_weight, preferred_element_type=jnp.float32),
            "tensor",
            scatter_dimension=0,
            tiled=True,
        )
        normed_post, inverse_post = normalize(mixed)
        residual = rows_in + normed_post * post_attn_gain
        normed_two, inverse_two = normalize(residual)
        hidden_two = (normed_two * pre_ffn_gain).astype(jnp.bfloat16)
        full_two = lax.all_gather(hidden_two, "tensor", axis=0, tiled=True)
        pre_act = jnp.dot(full_two, fc1_weight, preferred_element_type=jnp.float32)
        activation, gelu_pull = jax.vjp(partial(jax.nn.gelu, approximate=True), pre_act)
        first_sum, square_sum = lax.psum(
            (
                jnp.sum(activation, axis=-1, keepdims=True),
                jnp.sum(activation * activation, axis=-1, keepdims=True),
            ),
            "tensor",
        )
        mean_wide = first_sum / FFN
        inverse_wide = lax.rsqrt(square_sum / FFN - mean_wide * mean_wide + EPSILON)
        normed_wide = (activation - mean_wide) * inverse_wide
        hidden_wide = (normed_wide * ffn_norm_gain).astype(jnp.bfloat16)
        ffn_rows = lax.psum_scatter(
            jnp.dot(
                lax.slice_in_dim(hidden_wide, 0, row_count * lax.axis_size("tensor"), axis=0),
                fc2_weight,
                preferred_element_type=jnp.float32,
            ).astype(jnp.bfloat16),
            "tensor",
            scatter_dimension=0,
            tiled=True,
        ).astype(jnp.float32)
        outputs.append((residual + ffn_rows).astype(jnp.bfloat16))
        grad_all = cotangent[micro_index]
        grad_rows = lax.dynamic_slice_in_dim(
            grad_all, shard_index * row_count, row_count, 0
        ).astype(jnp.float32)
        fc2_grad = jnp.einsum(
            "tf,td->fd", hidden_wide, grad_all, preferred_element_type=jnp.float32
        )
        grad_wide = jnp.einsum(
            "td,fd->tf", grad_all, fc2_weight, preferred_element_type=jnp.float32
        )
        grad_hat_wide = grad_wide * ffn_norm_gain
        wide_gain_grad = jnp.sum(grad_wide * normed_wide, axis=0)
        sum_grad, sum_cross = lax.psum(
            (
                jnp.sum(grad_hat_wide, axis=-1, keepdims=True),
                jnp.sum(grad_hat_wide * normed_wide, axis=-1, keepdims=True),
            ),
            "tensor",
        )
        grad_activation = inverse_wide * (
            grad_hat_wide - sum_grad / FFN - normed_wide * (sum_cross / FFN)
        )
        grad_pre = gelu_pull(grad_activation)[0].astype(jnp.bfloat16)
        fc1_grad = jnp.einsum("td,tf->df", full_two, grad_pre, preferred_element_type=jnp.float32)
        grad_two = lax.psum_scatter(
            jnp.einsum("tf,df->td", grad_pre, fc1_weight, preferred_element_type=jnp.float32),
            "tensor",
            scatter_dimension=0,
            tiled=True,
        )
        two_gain_grad = jnp.sum(grad_two * normed_two, axis=0)
        grad_residual = grad_rows + norm_backward(grad_two * pre_ffn_gain, normed_two, inverse_two)
        post_gain_grad = jnp.sum(grad_residual * normed_post, axis=0)
        grad_mixed = norm_backward(
            grad_residual * post_attn_gain, normed_post, inverse_post
        ).astype(jnp.bfloat16)
        grad_mixed_all = lax.all_gather(grad_mixed, "tensor", axis=0, tiled=True)
        out_grad = jnp.einsum(
            "te,td->ed", scaled, grad_mixed_all, preferred_element_type=jnp.float32
        )
        grad_scaled = jnp.einsum(
            "td,ed->te", grad_mixed_all, out_weight, preferred_element_type=jnp.float32
        ).reshape(tokens, head_count, HEAD_DIM)
        scale_grad = jnp.sum(grad_scaled * attended, axis=(0, 2))
        grad_attended = (grad_scaled * head_scale[None, :, None]).astype(jnp.bfloat16)
        grad_blocks = grad_attended.reshape(block_count, block_rows, head_count, HEAD_DIM)

        def backward_block(running, operands):
            grad_query, grad_keys, grad_values = attend_backward(
                operands[0],
                operands[1],
                operands[2],
                operands[3],
                tree_keys,
                tree_values,
                seg_table,
            )
            return ((running[0] + grad_keys, running[1] + grad_values), grad_query)

        zero_tree = jnp.zeros((tree_tokens, head_count, HEAD_DIM), jnp.float32)
        tree_grads, grad_queries = lax.scan(
            backward_block,
            (zero_tree, zero_tree),
            (query_blocks, grad_blocks, log_totals, block_starts),
        )
        spread = jnp.stack(
            [
                tree_grads[0].reshape(tree_tokens, local_width),
                tree_grads[1].reshape(tree_tokens, local_width),
            ],
            axis=1,
        )
        own_pairs = group_reduce(spread, member, bit_order, tokens).astype(jnp.bfloat16)
        grad_proj = jnp.stack(
            [grad_queries.reshape(tokens, local_width), own_pairs[:, 0], own_pairs[:, 1]]
        )
        qkv_grad = jnp.einsum(
            "td,ite->ide", full_one, grad_proj, preferred_element_type=jnp.float32
        )
        grad_one = lax.psum_scatter(
            jnp.einsum(
                "ite,ide->td", grad_proj, qkv_weight, preferred_element_type=jnp.float32
            ).astype(jnp.bfloat16),
            "tensor",
            scatter_dimension=0,
            tiled=True,
        ).astype(jnp.float32)
        one_gain_grad = jnp.sum(grad_one * normed_one, axis=0)
        input_grads.append(
            grad_residual + norm_backward(grad_one * pre_attn_gain, normed_one, inverse_one)
        )
        micro_weights = (qkv_grad, out_grad, fc1_grad, fc2_grad, scale_grad, wide_gain_grad)
        weight_totals = (
            micro_weights
            if weight_totals is None
            else tuple(
                (
                    running_total + addend
                    for running_total, addend in zip(weight_totals, micro_weights)
                )
            )
        )
        gain_totals = (
            gain_totals[0] + one_gain_grad,
            gain_totals[1] + post_gain_grad,
            gain_totals[2] + two_gain_grad,
        )
    weight_totals = sum_weights(weight_totals)
    gain_totals = lax.psum((gain_totals[0], gain_totals[1], gain_totals[2]), ("dp", "tensor"))
    return (
        jnp.stack(outputs),
        jnp.stack(input_grads),
        gain_totals[0],
        weight_totals[0],
        weight_totals[4],
        weight_totals[1],
        gain_totals[1],
        gain_totals[2],
        weight_totals[2],
        weight_totals[5],
        weight_totals[3],
    )


def solution(mesh):
    in_specs = (
        P(None, ("dp", "tensor"), None),
        P(None, "dp", None),
        P(),
        P(),
        P(None, None, "tensor"),
        P("tensor"),
        P("tensor", None),
        P(),
        P(),
        P(None, "tensor"),
        P("tensor"),
        P("tensor", None),
    )
    out_specs = (
        P(None, ("dp", "tensor"), None),
        P(None, ("dp", "tensor"), None),
        P(),
        P(None, None, "tensor"),
        P("tensor"),
        P("tensor", None),
        P(),
        P(),
        P(None, "tensor"),
        P("tensor"),
        P("tensor", None),
    )
    return jax.shard_map(body, mesh=mesh, in_specs=in_specs, out_specs=out_specs, check_vma=False)
```

profile of v0, /device:TPU:0, one launch (start us, length us, event | category | flops | bytes accessed | tf_op | source)
XLA Modules:
  0.0 1945.1 jit_solution(17884303020987562593)
XLA Ops:
  14.0 24.6 %all-gather.7.cloned.1.call-done = bf16[1024,1024]{1,0:T(8,128)(2,1)} async-done(((bf16[256,1024]{1,0:T(8,128)(2,1)}), bf16[1024,1024]{1,0:T(8,128)(2,1)}) %all-gather.7.cloned.1.call-update) | async-done | bytes 2097168 | tf_op jit(solution)/shard_map/all_gather | solution.py:196
  74.7 24.3 %while.99 = (s32[]{:T(128)}, s32[16]{0:T(128)S(1)}, pred[16,16]{1,0:T(8,128)(4,1)}, s32[16]{0:T(128)S(1)}, s32[]{:T(128)}, /*index=5*/s32[]{:T(128)}) while((s32[]{:T(128)}, s32[16]{0:T(128)S(1)}, pred[16,16]{1,0:T(8,128)(4,1)}, s32[16]{0:T(128)S(1)}, s32[]{:T(128)}, /*index=5*/s32[]{:T(128)}) %tuple.286), condition=%wide.region_23.24_spmd.clone, body=%wide.region_21.23_spmd.clone.sunk | while | flops 1555 | bytes 1039 | solution.py:48
  137.0 135.6 %while.96 = (s32[]{:T(128)}, f32[2,512,4,64]{1,0,3,2:T(2,128)}, f32[2,4,512,1]{2,1,3,0:T(4,128)S(1)}, s32[2]{0:T(128)}, pred[16,16]{1,0:T(8,128)(4,1)S(1)}, /*in...) while((s32[]{:T(128)}, f32[2,512,4,64]{1,0,3,2:T(2,128)}, ...), condition=%wide.region_8.9_spmd, body=%wide.region_5.8_spmd.sunk | while | flops 2248464384 | bytes 141437376 | solution.py:209
  147.4 14.0 fusion.343
  161.4 15.0 exponential_reduce_fusion.4
  176.4 16.5 fusion.344
  215.1 14.0 fusion.343
  229.1 15.0 exponential_reduce_fusion.4
  244.1 16.5 fusion.344
  295.6 137.6 %while.97 = (s32[]{:T(128)}, f32[2,512,4,64]{1,0,3,2:T(2,128)}, f32[2,4,512,1]{2,1,3,0:T(4,128)S(1)}, s32[2]{0:T(128)}, pred[16,16]{1,0:T(8,128)(4,1)}, /*index=...) while((s32[]{:T(128)}, f32[2,512,4,64]{1,0,3,2:T(2,128)}, ...), condition=%wide.region_27.28_spmd, body=%wide.region_24.27_spmd.sunk | while | flops 2248464384 | bytes 141437376 | solution.py:209
  306.9 14.1 fusion.349
  321.0 15.1 exponential_reduce_fusion.5
  336.1 16.6 fusion.350
  375.5 14.0 fusion.349
  389.5 15.0 exponential_reduce_fusion.5
  404.6 16.6 fusion.350
  442.6 40.9 %reduce-scatter.13.cloned.1.call-done = f32[256,1024]{1,0:T(8,128)} async-done(((f32[1024,1024]{1,0:T(8,128)}), f32[256,1024]{1,0:T(8,128)}) %reduce-scatter.13.cloned.1.call-update) | async-done | bytes 1048592 | tf_op jit(solution)/shard_map/reduce_scatter | solution.py:214
  497.5 16.2 all-gather.9.cloned.1.call-done
  521.6 16.7 all-gather.13.cloned.1.call-done
  622.5 19.9 %reduce-scatter.17.cloned.1.call-done = f32[256,1024]{1,0:T(8,128)} async-done(((f32[1024,1024]{1,0:T(8,128)}), f32[256,1024]{1,0:T(8,128)}) %reduce-scatter.17.cloned.1.call-update) | async-done | bytes 1048592 | tf_op jit(solution)/shard_map/reduce_scatter | solution.py:273
  644.7 31.8 %reduce-scatter.11.cloned.1.call-done = bf16[256,1024]{1,0:T(8,128)(2,1)} async-done(((bf16[1024,1024]{1,0:T(8,128)(2,1)}), bf16[256,1024]{1,0:T(8,128)(2,1)}) %reduce-scatter.11.cloned.1.call-update) | async-done | bytes 524304 | tf_op jit(solution)/shard_map/reduce_scatter | solution.py:238
  676.5 47.1 %reduce-scatter.21.cloned.1.call-done = f32[256,1024]{1,0:T(8,128)} async-done(((f32[1024,1024]{1,0:T(8,128)}), f32[256,1024]{1,0:T(8,128)}) %reduce-scatter.21.cloned.1.call-update) | async-done | bytes 1048592 | tf_op jit(solution)/shard_map/reduce_scatter | solution.py:273
  727.8 29.8 %reduce-scatter.15.cloned.1.call-done = bf16[256,1024]{1,0:T(8,128)(2,1)} async-done(((bf16[1024,1024]{1,0:T(8,128)(2,1)}), bf16[256,1024]{1,0:T(8,128)(2,1)}) %reduce-scatter.15.cloned.1.call-update) | async-done | bytes 524304 | tf_op jit(solution)/shard_map/reduce_scatter | solution.py:238
  766.9 19.2 all-gather.17.cloned.1.call-done
  793.8 16.4 all-gather.15.cloned.1.call-done
  821.4 229.5 %while.101 = (s32[]{:T(128)}, f32[4096,4,64]{0,2,1:T(8,128)}, f32[4096,4,64]{0,2,1:T(8,128)}, bf16[2,512,4,64]{1,3,2,0:T(8,128)(2,1)}, bf16[2,512,4,64]{1,3,2,0:...) while((s32[]{:T(128)}, f32[4096,4,64]{0,2,1:T(8,128)}, ...), condition=%wide.region_64.69_spmd.clone, body=%wide.region_62.68_spmd.clone.sunk | while | flops 5508749312 | bytes 381029920 | solution.py:309
  832.7 13.2 fusion.380
  845.9 25.5 %multiply_reduce_fusion.31 = (f32[4,512]{1,0:T(4,128)S(1)}, f32[4,512,4096]{2,1,0:T(8,128)}) fusion(f32[4,512,4096]{2,1,0:T(8,128)} %fusion.380, f32[4,512]{1,0:T(4,128)S(1)} %dynamic-slice_bitcast_fusion.5, pred[512,4096]{1,0:T(8,128)(4,1)S(1)} %fusion.381, bf16[4096,4,64]{0,2,1:T(8,128)(2,1)S(1)} %copy-done.11, ...), kind=kOutput, calls=%fused_computation.141.clone.1 | convolution fusion | flops 1115682816 | bytes 71581696 | tf_op jit(solution)/shard_map/while/body/eval_jaxpr/qhd,khd->hqk/dot_general | solution.py:94
  871.4 27.7 %multiply_convert_fusion.23 = bf16[4,512,4096]{2,1,0:T(8,128)(2,1)} fusion(f32[4,512,4096]{2,1,0:T(8,128)} %get-tuple-element.1571, f32[4,512,4096]{2,1,0:T(8,128)} %fusion.380, f32[4,512]{1,0:T(4,128)S(1)} %get-tuple-element.1572, f32[4,512]{1,0:T(4,128)S(1)} %dynamic-slice_bitcast_fusion.5, pred[512,4096]{1,0:T(8,128)(4,1)S(1)} %fusion.381), kind=kLoop, calls=%fused_computation.140.clone.1 | loop fusion | flops 50331648 | bytes 85999616 | tf_op jit(solution)/shard_map/while/body/eval_jaxpr/convert_element_type | solution.py:98
  918.4 16.6 fusion.383
  945.9 13.2 fusion.380
  959.1 25.5 %multiply_reduce_fusion.31 = (f32[4,512]{1,0:T(4,128)S(1)}, f32[4,512,4096]{2,1,0:T(8,128)}) fusion(f32[4,512,4096]{2,1,0:T(8,128)} %fusion.380, f32[4,512]{1,0:T(4,128)S(1)} %dynamic-slice_bitcast_fusion.5, pred[512,4096]{1,0:T(8,128)(4,1)S(1)} %fusion.381, bf16[4096,4,64]{0,2,1:T(8,128)(2,1)S(1)} %copy-done.11, ...), kind=kOutput, calls=%fused_computation.141.clone.1 | convolution fusion | flops 1115682816 | bytes 71581696 | tf_op jit(solution)/shard_map/while/body/eval_jaxpr/qhd,khd->hqk/dot_general | solution.py:94
  984.6 27.7 %multiply_convert_fusion.23 = bf16[4,512,4096]{2,1,0:T(8,128)(2,1)} fusion(f32[4,512,4096]{2,1,0:T(8,128)} %get-tuple-element.1571, f32[4,512,4096]{2,1,0:T(8,128)} %fusion.380, f32[4,512]{1,0:T(4,128)S(1)} %get-tuple-element.1572, f32[4,512]{1,0:T(4,128)S(1)} %dynamic-slice_bitcast_fusion.5, pred[512,4096]{1,0:T(8,128)(4,1)S(1)} %fusion.381), kind=kLoop, calls=%fused_computation.140.clone.1 | loop fusion | flops 50331648 | bytes 85999616 | tf_op jit(solution)/shard_map/while/body/eval_jaxpr/convert_element_type | solution.py:98
  1032.8 17.9 fusion.383
  1085.0 46.5 %collective-permute-done.6 = bf16[2,1024,2,256]{3,1,2,0:T(8,128)(2,1)} collective-permute-done((bf16[2,1024,2,256]{3,1,2,0:T(8,128)(2,1)}, bf16[2,1024,2,256]{3,1,2,0:T(8,128)(2,1)}, u32[]{:S(2)}, u32[]{:S(2)}) %collective-permute-start.6) | collective-permute-done | bytes 2097184 | tf_op jit(solution)/shard_map/ppermute | solution.py:23
  1141.4 228.4 %while.100 = (s32[]{:T(128)}, f32[4096,4,64]{0,2,1:T(8,128)}, f32[4096,4,64]{0,2,1:T(8,128)}, bf16[2,512,4,64]{1,3,2,0:T(8,128)(2,1)}, bf16[2,512,4,64]{1,3,2,0:...) while((s32[]{:T(128)}, f32[4096,4,64]{0,2,1:T(8,128)}, ...), condition=%wide.region_49.50_spmd.clone, body=%wide.region_47.49_spmd.clone.sunk | while | flops 5508749312 | bytes 381030976 | solution.py:309
  1165.0 25.5 %multiply_reduce_fusion.30 = (f32[4,512]{1,0:T(4,128)S(1)}, f32[4,512,4096]{2,1,0:T(8,128)}) fusion(f32[4,512,4096]{2,1,0:T(8,128)} %fusion.365, f32[4,512]{1,0:T(4,128)S(1)} %dynamic-slice_bitcast_fusion.4, pred[512,4096]{1,0:T(8,128)(4,1)S(1)} %fusion.366, bf16[4096,4,64]{0,2,1:T(8,128)(2,1)S(1)} %copy-done.10, ...), kind=kOutput, calls=%fused_computation.87.clone.1 | convolution fusion | flops 1115682816 | bytes 71581696 | tf_op jit(solution)/shard_map/while/body/eval_jaxpr/qhd,khd->hqk/dot_general | solution.py:94
  1190.5 27.7 %multiply_convert_fusion.22 = bf16[4,512,4096]{2,1,0:T(8,128)(2,1)} fusion(f32[4,512,4096]{2,1,0:T(8,128)} %get-tuple-element.1556, f32[4,512,4096]{2,1,0:T(8,128)} %fusion.365, f32[4,512]{1,0:T(4,128)S(1)} %get-tuple-element.1557, f32[4,512]{1,0:T(4,128)S(1)} %dynamic-slice_bitcast_fusion.4, pred[512,4096]{1,0:T(8,128)(4,1)S(1)} %fusion.366), kind=kLoop, calls=%fused_computation.86.clone.1 | loop fusion | flops 50331648 | bytes 85999616 | tf_op jit(solution)/shard_map/while/body/eval_jaxpr/convert_element_type | solution.py:98
  1237.6 16.7 fusion.368
  1264.5 13.2 fusion.365
  1277.7 25.5 %multiply_reduce_fusion.30 = (f32[4,512]{1,0:T(4,128)S(1)}, f32[4,512,4096]{2,1,0:T(8,128)}) fusion(f32[4,512,4096]{2,1,0:T(8,128)} %fusion.365, f32[4,512]{1,0:T(4,128)S(1)} %dynamic-slice_bitcast_fusion.4, pred[512,4096]{1,0:T(8,128)(4,1)S(1)} %fusion.366, bf16[4096,4,64]{0,2,1:T(8,128)(2,1)S(1)} %copy-done.10, ...), kind=kOutput, calls=%fused_computation.87.clone.1 | convolution fusion | flops 1115682816 | bytes 71581696 | tf_op jit(solution)/shard_map/while/body/eval_jaxpr/qhd,khd->hqk/dot_general | solution.py:94
  1303.1 27.7 %multiply_convert_fusion.22 = bf16[4,512,4096]{2,1,0:T(8,128)(2,1)} fusion(f32[4,512,4096]{2,1,0:T(8,128)} %get-tuple-element.1556, f32[4,512,4096]{2,1,0:T(8,128)} %fusion.365, f32[4,512]{1,0:T(4,128)S(1)} %get-tuple-element.1557, f32[4,512]{1,0:T(4,128)S(1)} %dynamic-slice_bitcast_fusion.4, pred[512,4096]{1,0:T(8,128)(4,1)S(1)} %fusion.366), kind=kLoop, calls=%fused_computation.86.clone.1 | loop fusion | flops 50331648 | bytes 85999616 | tf_op jit(solution)/shard_map/while/body/eval_jaxpr/convert_element_type | solution.py:98
  1351.4 17.8 fusion.368
  1412.0 39.7 %collective-permute-done.4 = bf16[2,1024,2,256]{3,1,2,0:T(8,128)(2,1)} collective-permute-done((bf16[2,1024,2,256]{3,1,2,0:T(8,128)(2,1)}, bf16[2,1024,2,256]{3,1,2,0:T(8,128)(2,1)}, u32[]{:S(2)}, u32[]{:S(2)}) %collective-permute-start.4) | collective-permute-done | bytes 2097184 | tf_op jit(solution)/shard_map/ppermute | solution.py:23
  1461.1 21.5 %collective-permute-done.5 = bf16[1024,2,256]{2,0,1:T(8,128)(2,1)S(1)} collective-permute-done((bf16[1024,2,256]{2,0,1:T(8,128)(2,1)}, bf16[1024,2,256]{2,0,1:T(8,128)(2,1)S(1)}, u32[]{:S(2)}, u32[]{:S(2)}) %collective-permute-start.5) | collective-permute-done | bytes 1048608 | tf_op jit(solution)/shard_map/ppermute | solution.py:23
  1520.5 22.0 %all-reduce.1 = (f32[4]{0:T(128)}, f32[1024]{0:T(1024)}) all-reduce(f32[4]{0:T(128)S(1)} %add.520, f32[1024]{0:T(1024)S(1)} %add.525), channel_id=1, replica_groups=mesh['dp'=8,'tensor'=4] {'dp'}, use_global_device_ids=true, to_apply=%region_76.81 | all-reduce | flops 1028 | bytes 8224 | tf_op jit(solution)/shard_map/psum | solution.py:151
  1544.8 41.8 %all-reduce = (f32[1024]{0:T(1024)}, f32[1024]{0:T(1024)}, f32[1024]{0:T(1024)}) all-reduce(f32[1024]{0:T(1024)S(1)} %add.517, f32[1024]{0:T(1024)S(1)} %add.522, f32[1024]{0:T(1024)S(1)} %add.523), channel_id=1, replica_groups=mesh['dp'=8,'tensor'=4] {'dp','tensor'}, use_global_device_ids=true, to_apply=%region_70.75 | all-reduce | flops 3072 | bytes 24576 | tf_op jit(solution)/shard_map/psum | solution.py:357
  1590.0 336.7 %all-reduce.7.cloned.1.call-done = (f32[3,1024,256]{1,2,0:T(8,128)}, f32[256,1024]{1,0:T(8,128)}, f32[1024,1024]{1,0:T(8,128)}, f32[1024,1024]{1,0:T(8,128)}) async-done(((f32[3,1024,256]{1,2,0:T(8,128)}, f32[256,1024]{1,0:T(8,128)}, f32[1024,1024]{1,0:T(8,128)}, f32[1024,1024]{1,0:T(8,128)}), (f32[3,1024,256]{1,2,0:T(8,128)}, f32[256,1024]{1,0:T(8,128)}, f32[1024,1024]{1,0:T(8,128)}, ...) | async-done | bytes 12582928 | tf_op jit(solution)/shard_map/psum | solution.py:151
  (654 shorter events, 656.7 us)
Async XLA Ops:
  7.2 484.4 %copy-start = (bf16[1024,1024]{1,0:T(8,128)(2,1)S(1)}, bf16[1024,1024]{1,0:T(8,128)(2,1)}, u32[]{:S(2)}) copy-start(bf16[1024,1024]{1,0:T(8,128)(2,1)} %param.43) | copy-start | bytes 6291460
  7.2 31.3 %all-gather.7.cloned.1.call-start = ((), (), s32[]{:S(2)}) async-start(), calls=%async_computation.8 | async-start | bytes 2621440 | tf_op jit(solution)/shard_map/all_gather | solution.py:196
  13.1 50.4 %all-gather.11.cloned.1.call-start = ((), (), s32[]{:S(2)}) async-start(), calls=%async_computation.12 | async-start | bytes 2621440 | tf_op jit(solution)/shard_map/all_gather | solution.py:196
  13.8 425.8 %reduce-scatter.9.cloned.1.call-start = ((), (), s32[]{:S(2)}) async-start(), calls=%async_computation.9 | async-start | bytes 5242880 | tf_op jit(solution)/shard_map/reduce_scatter | solution.py:214
  45.1 26.4 %collective-permute-start = (bf16[1024,2,256]{2,0,1:T(8,128)(2,1)}, bf16[1024,2,256]{2,0,1:T(8,128)(2,1)S(1)}, u32[]{:S(2)}, u32[]{:S(2)}) collective-permute-start(bf16[1024,2,256]{2,0,1:T(8,128)(2,1)} %get-tuple-element.1216), channel_id=1, source_target_pairs={{0,4},{4,0},{8,12},{12,8},{16,20},{20,16},{24,28},{28,24},{1,5},{5... | collective-permute-start | bytes 3145736 | tf_op jit(solution)/shard_map/ppermute | solution.py:23
  68.2 30.7 %copy-start.106 = (f32[4]{0:T(128)S(1)}, f32[4]{0:T(128)}, u32[]{:S(2)}) copy-start(f32[4]{0:T(128)} %param.37) | copy-start | bytes 52
  70.1 39.5 %collective-permute-start.2 = (bf16[1024,2,256]{2,0,1:T(8,128)(2,1)}, bf16[1024,2,256]{2,0,1:T(8,128)(2,1)}, u32[]{:S(2)}, u32[]{:S(2)}) collective-permute-start(bf16[1024,2,256]{2,0,1:T(8,128)(2,1)} %get-tuple-element.1219), channel_id=1, source_target_pairs={{0,4},{4,0},{8,12},{12,8},{16,20},{20,16},{24,28},{28,24},{1,5},{5... | collective-permute-start | bytes 3145736 | tf_op jit(solution)/shard_map/ppermute | solution.py:23
  71.6 28.7 %copy-start.43 = (bf16[1024,2,256]{2,0,1:T(8,128)(2,1)}, bf16[1024,2,256]{2,0,1:T(8,128)(2,1)S(1)}, u32[]{:S(2)}) copy-start(bf16[1024,2,256]{2,0,1:T(8,128)(2,1)S(1)} %collective-permute-done) | copy-start | bytes 3145732
  73.2 48.8 %collective-permute-start.1 = (bf16[2,1024,2,256]{3,1,2,0:T(8,128)(2,1)}, bf16[2,1024,2,256]{3,1,2,0:T(8,128)(2,1)}, u32[]{:S(2)}, u32[]{:S(2)}) collective-permute-start(bf16[2,1024,2,256]{3,1,2,0:T(8,128)(2,1)} %maximum_select_fusion.2), channel_id=1, source_target_pairs={{0,8},{4,12},{8,0},{12,4},{16,24},{20,28},{24,16},{28,20},{1,9},{5... | collective-permute-start | bytes 6291464 | tf_op jit(solution)/shard_map/ppermute | solution.py:23
  113.6 165.6 %collective-permute-start.3 = (bf16[2,1024,2,256]{3,1,2,0:T(8,128)(2,1)}, bf16[2,1024,2,256]{3,1,2,0:T(8,128)(2,1)}, u32[]{:S(2)}, u32[]{:S(2)}) collective-permute-start(bf16[2,1024,2,256]{3,1,2,0:T(8,128)(2,1)} %maximum_select_fusion.4), channel_id=1, source_target_pairs={{0,8},{4,12},{8,0},{12,4},{16,24},{20,28},{24,16},{28,20},{1,9},{5... | collective-permute-start | bytes 6291464 | tf_op jit(solution)/shard_map/ppermute | solution.py:23
  137.0 138.2 %copy-start.72 = (f32[256]{0:T(256)S(1)}, f32[256]{0:T(256)}, u32[]{:S(2)}) copy-start(f32[256]{0:T(256)} %mul.600) | copy-start | bytes 3076
  279.2 204.4 %reduce-scatter.13.cloned.1.call-start = ((), (), s32[]{:S(2)}) async-start(), calls=%async_computation.13 | async-start | bytes 5242880 | tf_op jit(solution)/shard_map/reduce_scatter | solution.py:214
  295.6 140.1 %copy-start.73 = (f32[256]{0:T(256)S(1)}, f32[256]{0:T(256)}, u32[]{:S(2)}) copy-start(f32[256]{0:T(256)} %mul.600) | copy-start | bytes 3076
  439.6 46.8 %copy-start.12 = (bf16[2,256,1024]{2,1,0:T(8,128)(2,1)S(1)}, bf16[2,256,1024]{2,1,0:T(8,128)(2,1)}, u32[]{:S(2)}) copy-start(bf16[2,256,1024]{2,1,0:T(8,128)(2,1)} %param.32) | copy-start | bytes 3145732
  439.6 46.9 %copy-start.71 = (f32[1024]{0:T(1024)S(1)}, f32[1024]{0:T(1024)}, u32[]{:S(2)}) copy-start(f32[1024]{0:T(1024)} %param.39) | copy-start | bytes 12292
  439.6 74.1 %all-gather.9.cloned.1.call-start = ((), (), s32[]{:S(2)}) async-start(), calls=%async_computation.10 | async-start | bytes 2621440 | tf_op jit(solution)/shard_map/all_gather | solution.py:224
  490.9 47.3 %all-gather.13.cloned.1.call-start = ((), (), s32[]{:S(2)}) async-start(), calls=%async_computation.14 | async-start | bytes 2621440 | tf_op jit(solution)/shard_map/all_gather | solution.py:224
  491.5 150.9 %reduce-scatter.17.cloned.1.call-start = ((), (), s32[]{:S(2)}) async-start(), calls=%async_computation.16 | async-start | bytes 5242880 | tf_op jit(solution)/shard_map/reduce_scatter | solution.py:273
  521.6 34.9 %copy-start.103 = (f32[1024]{0:T(1024)S(1)}, f32[1024]{0:T(1024)}, u32[]{:S(2)}) copy-start(f32[1024]{0:T(1024)} %param.42) | copy-start | bytes 12292
  556.4 54.1 %copy-start.91 = (f32[1024,1]{0,1:T(1,128)}, f32[1024,1]{0,1:T(1,128)S(1)}, u32[]{:S(2)}) copy-start(f32[1024,1]{0,1:T(1,128)S(1)} %get-tuple-element.1232) | copy-start | bytes 12292
  556.4 54.1 %copy-start.93 = (f32[1024,1]{0,1:T(1,128)}, f32[1024,1]{0,1:T(1,128)S(1)}, u32[]{:S(2)}) copy-start(f32[1024,1]{0,1:T(1,128)S(1)} %get-tuple-element.1233) | copy-start | bytes 12292
  556.4 40.1 %copy-start.95 = (f32[1024,1]{0,1:T(1,128)}, f32[1024,1]{0,1:T(1,128)S(1)}, u32[]{:S(2)}) copy-start(f32[1024,1]{0,1:T(1,128)S(1)} %get-tuple-element.1230) | copy-start | bytes 12292
  556.4 40.1 %copy-start.97 = (f32[1024,1]{0,1:T(1,128)}, f32[1024,1]{0,1:T(1,128)S(1)}, u32[]{:S(2)}) copy-start(f32[1024,1]{0,1:T(1,128)S(1)} %get-tuple-element.1231) | copy-start | bytes 12292
  596.5 80.0 %reduce-scatter.11.cloned.1.call-start = ((), (), s32[]{:S(2)}) async-start(), calls=%async_computation.11 | async-start | bytes 2621440 | tf_op jit(solution)/shard_map/reduce_scatter | solution.py:238
  603.5 120.2 %reduce-scatter.21.cloned.1.call-start = ((), (), s32[]{:S(2)}) async-start(), calls=%async_computation.19 | async-start | bytes 5242880 | tf_op jit(solution)/shard_map/reduce_scatter | solution.py:273
  610.3 147.3 %reduce-scatter.15.cloned.1.call-start = ((), (), s32[]{:S(2)}) async-start(), calls=%async_computation.15 | async-start | bytes 2621440 | tf_op jit(solution)/shard_map/reduce_scatter | solution.py:238
  617.6 168.6 %all-gather.17.cloned.1.call-start = ((), (), s32[]{:S(2)}) async-start(), calls=%async_computation.20 | async-start | bytes 2621440 | tf_op jit(solution)/shard_map/all_gather | solution.py:285
  617.6 106.0 %copy-start.19 = (f32[256,1024]{1,0:T(8,128)S(1)}, f32[256,1024]{1,0:T(8,128)}, u32[]{:S(2)}) copy-start(f32[256,1024]{1,0:T(8,128)} %reduce-scatter.9.cloned.1.call-done) | copy-start | bytes 3145732
  617.6 106.0 %copy-start.21 = (f32[256,1024]{1,0:T(8,128)S(1)}, f32[256,1024]{1,0:T(8,128)}, u32[]{:S(2)}) copy-start(f32[256,1024]{1,0:T(8,128)} %copy-done.20) | copy-start | bytes 3145732
  727.8 34.0 %copy-start.22 = (f32[256,1024]{1,0:T(8,128)S(1)}, f32[256,1024]{1,0:T(8,128)}, u32[]{:S(2)}) copy-start(f32[256,1024]{1,0:T(8,128)} %reduce-scatter.13.cloned.1.call-done) | copy-start | bytes 3145732
  763.4 46.8 %all-gather.15.cloned.1.call-start = ((), (), s32[]{:S(2)}) async-start(), calls=%async_computation.17 | async-start | bytes 2621440 | tf_op jit(solution)/shard_map/all_gather | solution.py:285
  764.0 778.4 %reduce-scatter.23.cloned.1.call-start = ((), (), s32[]{:S(2)}) async-start(), calls=%async_computation.21 | async-start | bytes 2621440 | tf_op jit(solution)/shard_map/reduce_scatter | solution.py:328
  1083.4 48.1 %collective-permute-start.6 = (bf16[2,1024,2,256]{3,1,2,0:T(8,128)(2,1)}, bf16[2,1024,2,256]{3,1,2,0:T(8,128)(2,1)}, u32[]{:S(2)}, u32[]{:S(2)}) collective-permute-start(bf16[2,1024,2,256]{3,1,2,0:T(8,128)(2,1)} %select_convert_fusion), channel_id=1, source_target_pairs={{0,8},{4,12},{8,0},{12,4},{16,24},{20,28},{24,16},{28,20},{1,9},{5... | collective-permute-start | bytes 6291464 | tf_op jit(solution)/shard_map/ppermute | solution.py:23
  1085.0 56.4 %copy-start.24 = (bf16[2,512,4,64]{1,3,2,0:T(8,128)(2,1)S(1)}, bf16[2,512,4,64]{1,3,2,0:T(8,128)(2,1)}, u32[]{:S(2)}) copy-start(bf16[2,512,4,64]{1,3,2,0:T(8,128)(2,1)} %copy-done.23) | copy-start | bytes 1572868
  1085.0 56.4 %copy-start.67 = (f32[2,4,512,1]{2,1,3,0:T(4,128)S(1)}, f32[2,4,512,1]{2,1,3,0:T(4,128)}, u32[]{:S(2)}) copy-start(f32[2,4,512,1]{2,1,3,0:T(4,128)} %copy-done.66) | copy-start | bytes 49156
  1085.0 56.4 %copy-start.76 = (pred[16,16]{1,0:T(8,128)(4,1)S(1)}, pred[16,16]{1,0:T(8,128)(4,1)}, u32[]{:S(2)}) copy-start(pred[16,16]{1,0:T(8,128)(4,1)} %copy-done.75) | copy-start | bytes 772
  1139.0 267.2 %collective-permute-start.7 = (bf16[1024,2,256]{2,0,1:T(8,128)(2,1)}, bf16[1024,2,256]{2,0,1:T(8,128)(2,1)}, u32[]{:S(2)}, u32[]{:S(2)}) collective-permute-start(bf16[1024,2,256]{2,0,1:T(8,128)(2,1)} %select_convert_fusion.2), channel_id=1, source_target_pairs={{0,4},{4,0},{8,12},{12,8},{16,20},{20,16},{24,28},{28,24},{1,5},{5... | collective-permute-start | bytes 3145736 | tf_op jit(solution)/shard_map/ppermute | solution.py:23
  1372.0 36.0 %copy-start.58 = (bf16[1,1024,256]{2,1,0:T(8,128)(2,1)}, bf16[1,1024,256]{2,1,0:T(8,128)(2,1)S(1)}, u32[]{:S(2)}) copy-start(bf16[1,1024,256]{2,1,0:T(8,128)(2,1)S(1)} %reshape.924) | copy-start | bytes 1572868
  1404.7 47.0 %collective-permute-start.4 = (bf16[2,1024,2,256]{3,1,2,0:T(8,128)(2,1)}, bf16[2,1024,2,256]{3,1,2,0:T(8,128)(2,1)}, u32[]{:S(2)}, u32[]{:S(2)}) collective-permute-start(bf16[2,1024,2,256]{3,1,2,0:T(8,128)(2,1)} %select_convert_fusion.1), channel_id=1, source_target_pairs={{0,8},{4,12},{8,0},{12,4},{16,24},{20,28},{24,16},{28,20},{1,9},{5... | collective-permute-start | bytes 6291464 | tf_op jit(solution)/shard_map/ppermute | solution.py:23
  1412.0 47.8 %copy-start.55 = (bf16[2,512,4,64]{1,3,2,0:T(8,128)(2,1)S(1)}, bf16[2,512,4,64]{1,3,2,0:T(8,128)(2,1)}, u32[]{:S(2)}) copy-start(bf16[2,512,4,64]{1,3,2,0:T(8,128)(2,1)} %get-tuple-element.1840) | copy-start | bytes 1572868
  1412.0 130.5 %reduce-scatter.19.cloned.1.call-start = ((), (), s32[]{:S(2)}) async-start(), calls=%async_computation.18 | async-start | bytes 2621440 | tf_op jit(solution)/shard_map/reduce_scatter | solution.py:328
  1459.2 23.5 %collective-permute-start.5 = (bf16[1024,2,256]{2,0,1:T(8,128)(2,1)}, bf16[1024,2,256]{2,0,1:T(8,128)(2,1)S(1)}, u32[]{:S(2)}, u32[]{:S(2)}) collective-permute-start(bf16[1024,2,256]{2,0,1:T(8,128)(2,1)} %select_convert_fusion.3), channel_id=1, source_target_pairs={{0,4},{4,0},{8,12},{12,8},{16,20},{20,16},{24,28},{28,24},{1,5},{5... | collective-permute-start | bytes 3145736 | tf_op jit(solution)/shard_map/ppermute | solution.py:23
  1488.6 438.2 %all-reduce.7.cloned.1.call-start = ((), (), s32[]{:S(2)}) async-start(), calls=%async_computation.22 | async-start | bytes 25165824 | tf_op jit(solution)/shard_map/psum | solution.py:151
  1516.7 25.7 %copy-start.13 = (bf16[2,256,1024]{2,1,0:T(8,128)(2,1)S(1)}, bf16[2,256,1024]{2,1,0:T(8,128)(2,1)}, u32[]{:S(2)}) copy-start(bf16[2,256,1024]{2,1,0:T(8,128)(2,1)} %param.32) | copy-start | bytes 3145732
  1516.8 25.7 %copy-start.78 = (f32[1024]{0:T(1024)S(1)}, f32[1024]{0:T(1024)}, u32[]{:S(2)}) copy-start(f32[1024]{0:T(1024)} %param.35) | copy-start | bytes 12292
  1516.8 25.7 %copy-start.80 = (f32[256]{0:T(256)S(1)}, f32[256]{0:T(256)}, u32[]{:S(2)}) copy-start(f32[256]{0:T(256)} %copy-done.79) | copy-start | bytes 3076
  1516.8 69.7 %copy-start.35 = (f32[256,1024]{1,0:T(8,128)S(1)}, f32[256,1024]{1,0:T(8,128)}, u32[]{:S(2)}) copy-start(f32[256,1024]{1,0:T(8,128)} %get-tuple-element.1168) | copy-start | bytes 3145732
  1516.8 69.7 %copy-start.37 = (f32[256,1024]{1,0:T(8,128)S(1)}, f32[256,1024]{1,0:T(8,128)}, u32[]{:S(2)}) copy-start(f32[256,1024]{1,0:T(8,128)} %copy-done.36) | copy-start | bytes 3145732
  (104 other events, 856.8 us)
Sparse Core Ops, SparseCore 0:
  13.2 25.2 all-gather.6
  40.7 22.7 all-gather.10
  279.3 43.5 reduce-scatter.8
  439.7 43.7 reduce-scatter.12
  491.1 22.5 all-gather.8
  515.7 22.5 all-gather.12
  596.6 45.7 reduce-scatter.16
  645.1 31.3 reduce-scatter.10
  679.1 44.5 reduce-scatter.20
  726.2 31.3 reduce-scatter.14
  763.5 22.5 all-gather.16
  787.6 22.5 all-gather.14
  1412.1 29.6 reduce-scatter.22
  1488.7 30.5 reduce-scatter.18
  1525.0 401.6 all-reduce.6
where the time goes:
time: 1960 us; the launch traced here: 1950 us
  waiting for transfers between devices  726 us (37%)
  matrix products  540 us (28%)
  other arithmetic  321 us (16%)
  local copies, waits for them, and re-layouts  244 us (12%)
  blocking collectives  84.5 us (4%)
    psum x1, waiting for transfers between devices, sum_weights(): return lax.psum(weight_grads, 'dp')  337 us
    ppermute x8, waiting for transfers between devices, from_partner(): return lax.ppermute(value, axis, pairs)  112 us
    convert_element_type x4, other arithmetic, attend_backward(): grad_scores = (soft_probs * (grad_probs - row_total)).astype(jnp.bfloat16)  111 us
    dot_general x8, matrix products, masked_scores(): jnp.einsum('qhd,khd->hqk', query_block, tree_keys, preferred_element_type...  109 us
    dot_general x4, matrix products, attend_backward(): jnp.einsum('qhd,khd->hqk', grad_output, tree_values, preferred_element_ty...  102 us
    dot_general x4, matrix products, attend_backward(): jnp.einsum('hqk,qhd->khd', soft_probs.astype(jnp.bfloat16), grad_output,...  69 us
    reduce_scatter x2, waiting for transfers between devices, body(): lax.psum_scatter(jnp.einsum('tf,df->td', grad_pre, fc1_weight, preferred_...  67 us
    dot_general x4, matrix products, attend_forward(): jnp.einsum('hqk,khd->qhd', soft_probs.astype(jnp.bfloat16), tree_values,...  66.1 us
  transfers between devices with their start and end apart: 23, of which 16 were waited for; matrix products, arithmetic and copies ran while one was open for 38% of the time, Pallas kernels for 0%

commit v1 on v0

v1 whole, which is shorter than its diff:
```python
from functools import partial

import jax
import jax.numpy as jnp
from jax import lax
from jax.experimental import pallas as pl
from jax.experimental.pallas import tpu as pltpu
from jax.sharding import PartitionSpec as P

HEAD_DIM = 64
FFN = 4096
SEG = 256
SEGS = 16
DEPTH = 5
MICRO = 2

EPSILON = 1e-05
NEGATIVE = -1e30
F32 = jnp.float32
BF = jnp.bfloat16
NN = (((1,), (0,)), ((), ()))
NT = (((1,), (1,)), ((), ()))
TN = (((0,), (0,)), ((), ()))


def mm(a, b, dims=NN):
    return lax.dot_general(a, b, dims, preferred_element_type=F32)


def swap(value, axis, mask):
    return lax.ppermute(value, axis, [(i, i ^ mask) for i in range(lax.axis_size(axis))])


def normalize(values):
    center = values - jnp.mean(values, axis=-1, keepdims=True)
    inverse = lax.rsqrt(jnp.mean(center * center, axis=-1, keepdims=True) + EPSILON)
    return (center * inverse, inverse)


def norm_backward(grad_hat, normed, inverse):
    mean_grad = jnp.mean(grad_hat, axis=-1, keepdims=True)
    mean_cross = jnp.mean(grad_hat * normed, axis=-1, keepdims=True)
    return inverse * (grad_hat - mean_grad - normed * mean_cross)


def gather_rows(own):
    far = swap(own, "tensor", 2)
    near = swap(own, "tensor", 1)
    cross = swap(far, "tensor", 1)
    return jnp.concatenate([own, near, far, cross], axis=0)


def scatter_rows(partial_rows):
    rows = partial_rows.shape[0] // 4
    blocks = [partial_rows[r * rows:(r + 1) * rows] for r in range(4)]
    got_far = swap(blocks[3].astype(BF), "tensor", 1)
    got_own = swap(blocks[1].astype(BF), "tensor", 1)
    far = blocks[2].astype(F32) + got_far.astype(F32)
    got = swap(far.astype(BF), "tensor", 2)
    return blocks[0].astype(F32) + got_own.astype(F32) + got.astype(F32)


def sum_small(values, axis):
    mask = 1
    while mask < lax.axis_size(axis):
        values = values + swap(values, axis, mask)
        mask *= 2
    return values


def sum_rows(values):
    blocks = values.reshape(values.shape[0], 4, -1)
    got = swap(blocks, "tensor", 1)
    blocks = blocks + jnp.stack([got[:, r ^ 1] for r in range(4)], axis=1)
    got = swap(blocks, "tensor", 2)
    blocks = blocks + jnp.stack([got[:, r ^ 2] for r in range(4)], axis=1)
    return blocks.reshape(values.shape)


def sum_spread(values):
    bits = [2**b for b in range(lax.axis_size("dp").bit_length() - 1)]
    index = lax.axis_index("dp")
    part = values
    for mask in bits:
        half = part.shape[0] // 2
        upper = (index // mask) % 2
        send = lax.dynamic_slice_in_dim(part, (1 - upper) * half, half, 0)
        keep = lax.dynamic_slice_in_dim(part, upper * half, half, 0)
        part = keep + swap(send.astype(BF), "dp", mask).astype(F32)
    part = part.astype(BF)
    for mask in bits[::-1]:
        got = swap(part, "dp", mask)
        upper = (index // mask) % 2 == 1
        part = jnp.where(upper, jnp.stack([got, part]), jnp.stack([part, got]))
        part = part.reshape((-1,) + part.shape[2:])
    return part.astype(F32)


def climb(parents, base, seg):
    found = []
    current = seg
    count = jnp.int32(0)
    for _ in range(DEPTH):
        up = parents[base + current]
        valid = up >= 0
        count = count + valid.astype(jnp.int32)
        current = jnp.where(valid, up, current)
        found.append(current)
    return count, found


def place_of(seg, per, member, shard):
    return ((seg // per) ^ member) * per + ((seg % per) ^ shard)


def attend_forward(place, parents, q_ref, *rest):
    keys, values = rest[0:4], rest[4:8]
    scale_ref, o_ref, os_ref, lse_ref, tree, picked, sems = rest[8:]
    step = pl.program_id(0)
    width = q_ref.shape[1]
    heads = width // HEAD_DIM
    tokens = keys[0].shape[0]
    per = tokens // SEG
    base, member, shard = place[0], place[1], place[2]

    @pl.when(step == 0)
    def _():
        copies = []
        for r in range(4):
            rows = pl.ds(r * tokens, tokens)
            copies.append(pltpu.make_async_copy(keys[r], tree.at[rows, pl.ds(0, width)], sems.at[r]))
            copies.append(pltpu.make_async_copy(values[r], tree.at[rows, pl.ds(width, width)], sems.at[4 + r]))
        for copy in copies:
            copy.start()
        for copy in copies:
            copy.wait()

    count, found = climb(parents, base, member * per + (step ^ shard))
    for slot in range(DEPTH):
        start = pl.multiple_of(place_of(found[slot], per, member, shard) * SEG, SEG)
        picked[pl.ds(slot * SEG, SEG), :] = tree[pl.ds(start, SEG), :]
    past = DEPTH * SEG
    picked[pl.ds(past, SEG), :] = tree[pl.ds(pl.multiple_of(step * SEG, SEG), SEG), :]
    lane = lax.broadcasted_iota(jnp.int32, (SEG, width), 1) // HEAD_DIM
    row = lax.broadcasted_iota(jnp.int32, (SEG, SEG), 0)
    col = lax.broadcasted_iota(jnp.int32, (SEG, SEG), 1)
    slot_of = lax.broadcasted_iota(jnp.int32, (1, past), 1) // SEG
    bias = jnp.where(slot_of < count, 0.0, NEGATIVE).astype(F32)
    q = q_ref[...] * BF(HEAD_DIM ** -0.5)
    lse_lane = lax.broadcasted_iota(jnp.int32, (SEG, 128), 1)
    lse_all = jnp.zeros((SEG, 128), F32)
    out = jnp.zeros((SEG, width), F32)
    for head in range(heads):
        qh = jnp.where(lane == head, q, jnp.zeros_like(q))
        s_past = mm(qh, picked[0:past, 0:width], NT) + bias
        s_own = jnp.where(col <= row, mm(qh, picked[past:past + SEG, 0:width], NT), NEGATIVE)
        top = jnp.maximum(
            jnp.max(s_past, axis=1, keepdims=True), jnp.max(s_own, axis=1, keepdims=True)
        )
        p_past = jnp.exp(s_past - top)
        p_own = jnp.exp(s_own - top)
        total = jnp.sum(p_past, axis=1, keepdims=True) + jnp.sum(p_own, axis=1, keepdims=True)
        got = mm(p_past.astype(BF), picked[0:past, width:2 * width])
        got = got + mm(p_own.astype(BF), picked[past:past + SEG, width:2 * width])
        out = jnp.where(lane == head, got / total, out)
        lse_all = jnp.where(lse_lane == head, top + jnp.log(total), lse_all)
    o_ref[...] = out
    os_ref[...] = (out * scale_ref[...]).astype(BF)
    lse_ref[...] = jnp.transpose(lse_all)[0:8].reshape(1, 8, SEG)


def attend_backward(place, parents, q_ref, dos_ref, o_ref, lse_ref, scale_ref, *rest):
    keys, values = rest[0:4], rest[4:8]
    dq_ref, dks, dvs, sg_ref = rest[8], rest[9:13], rest[13:17], rest[17]
    tree, acc, dqt, sems = rest[18:]
    step = pl.program_id(0)
    width = q_ref.shape[1]
    heads = width // HEAD_DIM
    tokens = keys[0].shape[0]
    per = tokens // SEG
    base, member, shard = place[0], place[1], place[2]

    @pl.when(step == 0)
    def _():
        copies = []
        for r in range(4):
            rows = pl.ds(r * tokens, tokens)
            copies.append(pltpu.make_async_copy(keys[r], tree.at[rows, pl.ds(0, width)], sems.at[r]))
            copies.append(pltpu.make_async_copy(values[r], tree.at[rows, pl.ds(width, width)], sems.at[4 + r]))
        for copy in copies:
            copy.start()
        acc[...] = jnp.zeros_like(acc)
        sg_ref[...] = jnp.zeros_like(sg_ref)
        for copy in copies:
            copy.wait()

    dos = dos_ref[...].astype(F32)
    cross = dos * o_ref[...]
    sg_ref[...] += jnp.sum(cross.reshape(SEG // 8, 8, width), axis=0)
    scale = scale_ref[...]
    go = (dos * scale).astype(BF)
    cross_t = jnp.transpose(cross * scale)
    lane = lax.broadcasted_iota(jnp.int32, (SEG, width), 1) // HEAD_DIM
    q = q_ref[...] * BF(HEAD_DIM ** -0.5)
    zero = jnp.zeros_like(q)
    q_heads = [jnp.where(lane == h, q, zero) for h in range(heads)]
    g_heads = [jnp.where(lane == h, go, zero) for h in range(heads)]
    deltas = [
        jnp.sum(cross_t[h * HEAD_DIM:(h + 1) * HEAD_DIM], axis=0, keepdims=True) for h in range(heads)
    ]
    lses = [lse_ref[0, h:h + 1, :] for h in range(heads)]
    dqt[...] = jnp.zeros_like(dqt)

    def block(start, own):
        rows = pl.ds(pl.multiple_of(start, SEG), SEG)
        k = tree[rows, 0:width]
        v = tree[rows, width:2 * width]
        kt = jnp.transpose(k)
        dk = jnp.zeros((SEG, width), F32)
        dv = jnp.zeros((SEG, width), F32)
        for h in range(heads):
            p = jnp.exp(mm(k, q_heads[h], NT) - lses[h])
            if own:
                key_row = lax.broadcasted_iota(jnp.int32, (SEG, SEG), 0)
                query_col = lax.broadcasted_iota(jnp.int32, (SEG, SEG), 1)
                p = jnp.where(key_row <= query_col, p, 0.0)
            dv += mm(p.astype(BF), g_heads[h])
            dp = mm(v, g_heads[h], NT)
            ds = (p * (dp - deltas[h])).astype(BF)
            dk += mm(ds, q_heads[h])
            dqt[pl.ds(h * HEAD_DIM, HEAD_DIM), :] += mm(kt[h * HEAD_DIM:(h + 1) * HEAD_DIM], ds)
        acc[rows, 0:width] += dk
        acc[rows, width:2 * width] += dv

    def upward(j, current):
        up = parents[base + current]
        block(place_of(up, per, member, shard) * SEG, False)
        return up

    seg = member * per + (step ^ shard)
    count, _ = climb(parents, base, seg)
    lax.fori_loop(0, count, upward, seg)
    block(step * SEG, True)
    dq_ref[...] = (jnp.transpose(dqt[...]) * HEAD_DIM ** -0.5).astype(BF)

    @pl.when(step == pl.num_programs(0) - 1)
    def _():
        for r in range(4):
            dks[r][...] = acc[r * tokens:(r + 1) * tokens, 0:width].astype(BF)
            dvs[r][...] = acc[r * tokens:(r + 1) * tokens, width:2 * width].astype(BF)


ROW = lambda i, *s: (i, 0)
FIX = lambda i, *s: (0, 0)
HBM = pl.BlockSpec(memory_space=pl.ANY)


def attention(place, parents, q, keys, values, scale_row):
    tokens, width = q.shape
    segs = tokens // SEG
    return pl.pallas_call(
        attend_forward,
        out_shape=(
            jax.ShapeDtypeStruct((tokens, width), F32),
            jax.ShapeDtypeStruct((tokens, width), BF),
            jax.ShapeDtypeStruct((segs, 8, SEG), F32),
        ),
        grid_spec=pltpu.PrefetchScalarGridSpec(
            num_scalar_prefetch=2,
            grid=(segs,),
            in_specs=[pl.BlockSpec((SEG, width), ROW)] + [HBM] * 8 + [pl.BlockSpec((1, width), FIX)],
            out_specs=[
                pl.BlockSpec((SEG, width), ROW),
                pl.BlockSpec((SEG, width), ROW),
                pl.BlockSpec((1, 8, SEG), lambda i, *s: (i, 0, 0)),
            ],
            scratch_shapes=[
                pltpu.VMEM((4 * tokens, 2 * width), BF),
                pltpu.VMEM(((DEPTH + 1) * SEG, 2 * width), BF),
                pltpu.SemaphoreType.DMA((8,)),
            ],
        ),
        compiler_params=pltpu.CompilerParams(
            dimension_semantics=("arbitrary",), vmem_limit_bytes=32 << 20
        ),
        cost_estimate=pl.CostEstimate(flops=16 * 10**9, transcendentals=0, bytes_accessed=8 << 20),
        name="attend_forward",
    )(place, parents, q, *keys, *values, scale_row)


def attention_grad(place, parents, q, dos, o, lse, scale_row, keys, values):
    tokens, width = q.shape
    segs = tokens // SEG
    piece = jax.ShapeDtypeStruct((tokens, width), BF)
    whole = pl.BlockSpec((tokens, width), FIX)
    return pl.pallas_call(
        attend_backward,
        out_shape=(piece,) + (piece,) * 8 + (jax.ShapeDtypeStruct((8, width), F32),),
        grid_spec=pltpu.PrefetchScalarGridSpec(
            num_scalar_prefetch=2,
            grid=(segs,),
            in_specs=[
                pl.BlockSpec((SEG, width), ROW),
                pl.BlockSpec((SEG, width), ROW),
                pl.BlockSpec((SEG, width), ROW),
                pl.BlockSpec((1, 8, SEG), lambda i, *s: (i, 0, 0)),
                pl.BlockSpec((1, width), FIX),
            ]
            + [HBM] * 8,
            out_specs=[pl.BlockSpec((SEG, width), ROW)] + [whole] * 8 + [pl.BlockSpec((8, width), FIX)],
            scratch_shapes=[
                pltpu.VMEM((4 * tokens, 2 * width), BF),
                pltpu.VMEM((4 * tokens, 2 * width), F32),
                pltpu.VMEM((width, SEG), F32),
                pltpu.SemaphoreType.DMA((8,)),
            ],
        ),
        compiler_params=pltpu.CompilerParams(
            dimension_semantics=("arbitrary",), vmem_limit_bytes=40 << 20
        ),
        cost_estimate=pl.CostEstimate(flops=36 * 10**9, transcendentals=0, bytes_accessed=12 << 20),
        name="attend_backward",
    )(place, parents, q, dos, o, lse, scale_row, *keys, *values)


def gelu_parts(c):
    root = 0.7978845608028654
    square = c * c
    tanh = jnp.tanh(root * (c + 0.044715 * (square * c)))
    act = 0.5 * c * (1.0 + tanh)
    slope = 0.5 * (1.0 + tanh) + 0.5 * c * (1.0 - tanh * tanh) * (root * (1.0 + 3 * 0.044715 * square))
    return act, slope


def body(
    block_input,
    cotangent,
    parent,
    pre_attn_gain,
    qkv_weight,
    head_scale,
    out_weight,
    post_attn_gain,
    pre_ffn_gain,
    fc1_weight,
    ffn_norm_gain,
    fc2_weight,
):
    trees = parent.shape[1]
    group = lax.axis_size("dp") // trees
    member = lax.axis_index("dp") % group
    tree_index = lax.axis_index("dp") // group
    shard = lax.axis_index("tensor")
    row_count = block_input.shape[1]
    tokens = cotangent.shape[1]
    width = qkv_weight.shape[2]
    parents = parent.reshape(-1)
    scale_row = jnp.repeat(head_scale, HEAD_DIM)[None, :]

    def place(micro):
        return jnp.stack([(micro * trees + tree_index) * SEGS, member, shard]).astype(jnp.int32)

    state = [dict() for _ in range(MICRO)]
    for micro, s in enumerate(state):
        s["rows"] = block_input[micro].astype(F32)
        s["n1"], s["i1"] = normalize(s["rows"])
        s["full1"] = gather_rows((s["n1"] * pre_attn_gain).astype(BF))
    for micro, s in enumerate(state):
        own_k = mm(s["full1"], qkv_weight[1]).astype(BF)
        own_v = mm(s["full1"], qkv_weight[2]).astype(BF)
        k1, k2 = swap(own_k, "dp", 1), swap(own_k, "dp", 2)
        v1, v2 = swap(own_v, "dp", 1), swap(own_v, "dp", 2)
        k3, v3 = swap(k1, "dp", 2), swap(v2, "dp", 1)
        s["keys"] = (own_k, k1, k2, k3)
        s["values"] = (own_v, v1, v2, v3)
        s["q"] = mm(s["full1"], qkv_weight[0]).astype(BF)
    fc1_grad = fc2_grad = out_grad = wide_gain = 0.0
    for micro, s in enumerate(state):
        s["o"], s["os"], s["lse"] = attention(
            place(micro), parents, s["q"], s["keys"], s["values"], scale_row
        )
        mixed = scatter_rows(mm(s["os"], out_weight))
        s["nu"], s["iu"] = normalize(mixed)
        s["r1"] = s["rows"] + s["nu"] * post_attn_gain
        s["n2"], s["i2"] = normalize(s["r1"])
        s["full2"] = gather_rows((s["n2"] * pre_ffn_gain).astype(BF))
    for micro, s in enumerate(state):
        grad_all = jnp.concatenate(
            [
                lax.dynamic_slice_in_dim(cotangent[micro], (shard ^ r) * row_count, row_count, 0)
                for r in range(4)
            ],
            axis=0,
        )
        s["grad_all"] = grad_all
        s["grad_rows"] = grad_all[0:row_count].astype(F32)
        act, slope = gelu_parts(mm(s["full2"], fc1_weight))
        dz = mm(grad_all, fc2_weight, NT)
        dna = dz * ffn_norm_gain
        sums = jnp.stack(
            [jnp.sum(act, -1), jnp.sum(act * act, -1), jnp.sum(dna, -1), jnp.sum(dna * act, -1)]
        )
        sums = sum_rows(sums) / FFN
        mu, square, m_dna, m_cross = [sums[i][:, None] for i in range(4)]
        rw = lax.rsqrt(square - mu * mu + EPSILON)
        m_dna_na = (m_cross - mu * m_dna) * rw
        na = (act - mu) * rw
        z = (na * ffn_norm_gain).astype(BF)
        wide_gain = wide_gain + jnp.sum(dz * na, axis=0)
        dc = (rw * (dna - m_dna - na * m_dna_na) * slope).astype(BF)
        dh2 = scatter_rows(mm(dc, fc1_weight, NT))
        s["ffn_rows"] = scatter_rows(mm(z, fc2_weight))
        fc2_grad = fc2_grad + mm(z, grad_all, TN)
        fc1_grad = fc1_grad + mm(s["full2"], dc, TN)
        s["two_gain"] = jnp.sum(dh2 * s["n2"], axis=0)
        s["dr1"] = s["grad_rows"] + norm_backward(dh2 * pre_ffn_gain, s["n2"], s["i2"])
        s["post_gain"] = jnp.sum(s["dr1"] * s["nu"], axis=0)
        du = norm_backward(s["dr1"] * post_attn_gain, s["nu"], s["iu"]).astype(BF)
        s["du"] = gather_rows(du)
    ffn_grads = sum_spread(jnp.concatenate([fc1_grad, fc2_grad], axis=0))
    qkv_grad = 0.0
    head_grad = 0.0
    for micro, s in enumerate(state):
        dos = mm(s["du"], out_weight, NT)
        out_grad = out_grad + mm(s["os"], s["du"], TN)
        got = attention_grad(
            place(micro), parents, s["q"], dos, s["o"], s["lse"], scale_row, s["keys"], s["values"]
        )
        dq, dk, dv, sg = got[0], got[1:5], got[5:9], got[9]
        head_grad = head_grad + sg
        add = lambda a, b: (a.astype(F32) + b.astype(F32)).astype(BF)
        k0, k1 = add(dk[0], swap(dk[2], "dp", 2)), add(dk[1], swap(dk[3], "dp", 2))
        v0, v2 = add(dv[0], swap(dv[1], "dp", 1)), add(dv[2], swap(dv[3], "dp", 1))
        own_k = add(k0, swap(k1, "dp", 1))
        own_v = add(v0, swap(v2, "dp", 2))
        grads = [dq, own_k, own_v]
        qkv_grad = qkv_grad + jnp.stack([mm(s["full1"], g, TN) for g in grads])
        dh1 = mm(dq, qkv_weight[0], NT) + mm(own_k, qkv_weight[1], NT) + mm(own_v, qkv_weight[2], NT)
        dh1 = scatter_rows(dh1)
        s["one_gain"] = jnp.sum(dh1 * s["n1"], axis=0)
        s["din"] = s["dr1"] + norm_backward(dh1 * pre_attn_gain, s["n1"], s["i1"])
    attn_grads = sum_spread(
        jnp.concatenate([qkv_grad.reshape(-1, 1024), out_grad], axis=0)
    )
    gains = jnp.stack([sum(s[k] for s in state) for k in ("one_gain", "post_gain", "two_gain")])
    gains = sum_small(gains, "tensor")
    head_row = jnp.sum(head_grad, axis=0).reshape(-1, HEAD_DIM).sum(-1)
    head_row = jnp.pad(head_row, (0, wide_gain.shape[0] - head_row.shape[0]))
    small = sum_small(jnp.concatenate([gains, wide_gain[None], head_row[None]], axis=0), "dp")
    return (
        jnp.stack([(s["r1"] + s["ffn_rows"]).astype(BF) for s in state]),
        jnp.stack([s["din"] for s in state]),
        small[0],
        attn_grads[0:3 * width].reshape(qkv_weight.shape),
        small[4, 0:head_scale.shape[0]],
        attn_grads[3 * width:],
        small[1],
        small[2],
        ffn_grads[0:fc1_weight.shape[0]],
        small[3],
        ffn_grads[fc1_weight.shape[0]:],
    )


def solution(mesh):
    in_specs = (
        P(None, ("dp", "tensor"), None),
        P(None, "dp", None),
        P(),
        P(),
        P(None, None, "tensor"),
        P("tensor"),
        P("tensor", None),
        P(),
        P(),
        P(None, "tensor"),
        P("tensor"),
        P("tensor", None),
    )
    out_specs = (
        P(None, ("dp", "tensor"), None),
        P(None, ("dp", "tensor"), None),
        P(),
        P(None, None, "tensor"),
        P("tensor"),
        P("tensor", None),
        P(),
        P(),
        P(None, "tensor"),
        P("tensor"),
        P("tensor", None),
    )
    return jax.shard_map(body, mesh=mesh, in_specs=in_specs, out_specs=out_specs, check_vma=False)
```

time: 1960 us -> 700 us (0.36)
  matrix products: 540 us -> 104 us
  waiting for transfers between devices: 726 us -> 312 us
  other arithmetic: 321 us -> 62.5 us
  local copies, waits for them, and re-layouts: 244 us -> 50 us
  Pallas kernels: 0 us -> 87.8 us
  blocking collectives: 84.5 us -> 0 us
  starting transfers between devices: 10.9 us -> 69.9 us
    dot_general x60 -> x36, matrix products: 540 us -> 104 us  [mm(): return lax.dot_general(a, b, dims, preferred_element_type=F32)]
    psum x1 -> x0, waiting for transfers between devices: 337 us -> none  [sum_weights(): return lax.psum(weight_grads, 'dp')]
    ppermute x8 -> x87, waiting for transfers between devices: 112 us -> 312 us  [swap(): lax.ppermute(value, axis, [(i, i ^ mask) for i in range(lax.axis_size(axi...]
    reduce_scatter x8 -> x0, waiting for transfers between devices: 170 us -> none  [the longest x2 67 us: body(): lax.psum_scatter(jnp.einsum('tf,df->td', grad_pre, fc1_weight, preferred_...]
    convert_element_type x15 -> x21, other arithmetic: 145 us -> 22.7 us  [the longest x2 5.71 us: sum_spread(): part = keep + swap(send.astype(BF), 'dp', mask).astype(F32)]
    all_gather x6 -> x0, waiting for transfers between devices: 105 us -> none  [the longest x2 36.8 us: body(): full_one = lax.all_gather(hidden_one, 'tensor', axis=0, tiled=True)]
    pallas_call x0 -> x4, Pallas kernels: none -> 87.8 us  [the longest x2 60.2 us: attention_grad(): pl.pallas_call(attend_backward, out_shape=(piece,) + (piece,) * 8 + (jax....]
    psum x4 -> x0, blocking collectives: 84.5 us -> none  [the longest x1 41.8 us: body(): lax.psum((gain_totals[0], gain_totals[1], gain_totals[2]), ('dp', 'tensor'))]
  transfers between devices with their start and end apart: 23 -> 87, of which waited for: 16 -> 34; matrix products, arithmetic and copies ran while one was open for 38% -> 24% of each run, Pallas kernels for 0% -> 13%
where the time goes in v1:
time: 700 us; the launch traced here: 690 us
  waiting for transfers between devices  312 us (45%)
  matrix products  104 us (15%)
  Pallas kernels  87.8 us (13%)
  starting transfers between devices  69.9 us (10%)
  other arithmetic  62.5 us (9%)
  local copies, waits for them, and re-layouts  50 us (7%)
    ppermute x87, waiting for transfers between devices, swap(): lax.ppermute(value, axis, [(i, i ^ mask) for i in range(lax.axis_size(axi...  312 us
    dot_general x36, matrix products, mm(): return lax.dot_general(a, b, dims, preferred_element_type=F32)  104 us
    ppermute x87, starting transfers between devices, swap(): lax.ppermute(value, axis, [(i, i ^ mask) for i in range(lax.axis_size(axi...  69.9 us
    pallas_call x2, Pallas kernels, attention_grad(): pl.pallas_call(attend_backward, out_shape=(piece,) + (piece,) * 8 + (jax....  60.2 us
    pallas_call x2, Pallas kernels, attention(): pl.pallas_call(attend_forward, out_shape=(jax.ShapeDtypeStruct((tokens, w...  27.5 us
    dynamic_slice x9, local copies, waits for them, and re-layouts, body(): lax.dynamic_slice_in_dim(cotangent[micro], (shard ^ r) * row_count, row_c...  17.6 us
  transfers between devices with their start and end apart: 87, of which 34 were waited for; matrix products, arithmetic and copies ran while one was open for 24% of the time, Pallas kernels for 13%

profile of v1, /device:TPU:0, one launch (start us, length us, event | category | flops | bytes accessed | tf_op | source)
XLA Modules:
  0.0 690.3 jit_solution(5455238495597574213)
XLA Ops:
  9.5 13.0 %collective-permute-done.1 = bf16[256,1024]{0,1:T(8,128)(2,1)} collective-permute-done((bf16[256,1024]{0,1:T(8,128)(2,1)}, bf16[256,1024]{0,1:T(8,128)(2,1)}, u32[]{:S(2)}, u32[]{:S(2)}) %collective-permute-start.1) | collective-permute-done | bytes 524320 | tf_op jit(solution)/shard_map/ppermute | solution.py:31
  23.4 9.5 %collective-permute-done.21 = bf16[256,1024]{0,1:T(8,128)(2,1)} collective-permute-done((bf16[256,1024]{0,1:T(8,128)(2,1)}, bf16[256,1024]{0,1:T(8,128)(2,1)}, u32[]{:S(2)}, u32[]{:S(2)}) %collective-permute-start.21) | collective-permute-done | bytes 524320 | tf_op jit(solution)/shard_map/ppermute | solution.py:31
  51.9 11.3 %collective-permute-done.7.rest_6_ = bf16[1024,256]{1,0:T(8,128)(2,1)S(1)} collective-permute-done((bf16[1024,256]{1,0:T(8,128)(2,1)S(1)}, bf16[1024,256]{1,0:T(8,128)(2,1)S(1)}, u32[]{:S(2)}, u32[]{:S(2)}) %collective-permute-start.7) | collective-permute-done | bytes 524320 | tf_op jit(solution)/shard_map/ppermute | solution.py:31
  76.5 9.1 %collective-permute-done.5.rest_3_ = bf16[1024,256]{1,0:T(8,128)(2,1)S(1)} collective-permute-done((bf16[1024,256]{1,0:T(8,128)(2,1)S(1)}, bf16[1024,256]{1,0:T(8,128)(2,1)S(1)}, u32[]{:S(2)}, u32[]{:S(2)}) %collective-permute-start.5) | collective-permute-done | bytes 524320 | tf_op jit(solution)/shard_map/ppermute | solution.py:31
  87.3 13.7 %attend_forward.2 = (f32[1024,256]{1,0:T(8,128)S(1)}, bf16[1024,256]{1,0:T(8,128)(2,1)S(1)}, f32[4,8,256]{2,1,0:T(8,128)S(1)}) custom-call(s32[3]{0:T(128)S(1)} %add_add_fusion.2.place, s32[64]{0:T(128)S(1)} %reshape.462.parents, bf16[1024,256]{1,0:T(8,128)(2,1)S(1)} %convolution_convert_fusion.5.q_ref, ...), custom_call_target="tpu_custom_call" | custom-call | flops 16000000000 | bytes 8388608 | tf_op jit(solution)/shard_map/attend_forward/pallas_call | solution.py:261
  107.5 13.9 %attend_forward.3 = (f32[1024,256]{1,0:T(8,128)S(1)}, bf16[1024,256]{1,0:T(8,128)(2,1)S(1)}, f32[4,8,256]{2,1,0:T(8,128)S(1)}) custom-call(s32[3]{0:T(128)S(1)} %add_add_fusion.3.place, s32[64]{0:T(128)S(1)} %reshape.462.parents, bf16[1024,256]{1,0:T(8,128)(2,1)S(1)} %convolution_convert_fusion.2.q_ref, ...), custom_call_target="tpu_custom_call" | custom-call | flops 16000000000 | bytes 8388608 | tf_op jit(solution)/shard_map/attend_forward/pallas_call | solution.py:261
  130.5 11.3 %collective-permute-done.11 = bf16[256,1024]{0,1:T(8,128)(2,1)} collective-permute-done((bf16[256,1024]{0,1:T(8,128)(2,1)}, bf16[256,1024]{0,1:T(8,128)(2,1)}, u32[]{:S(2)}, u32[]{:S(2)}) %collective-permute-start.11) | collective-permute-done | bytes 524320 | tf_op jit(solution)/shard_map/ppermute | solution.py:31
  143.8 8.3 %collective-permute-done.31 = bf16[256,1024]{0,1:T(8,128)(2,1)S(1)} collective-permute-done((bf16[256,1024]{0,1:T(8,128)(2,1)S(1)}, bf16[256,1024]{0,1:T(8,128)(2,1)S(1)}, u32[]{:S(2)}, u32[]{:S(2)}) %collective-permute-start.31) | collective-permute-done | bytes 524320 | tf_op jit(solution)/shard_map/ppermute | solution.py:31
  177.1 3.8 fusion.99
  181.3 9.4 %collective-permute-done.13 = bf16[256,1024]{0,1:T(8,128)(2,1)S(1)} collective-permute-done((bf16[256,1024]{0,1:T(8,128)(2,1)}, bf16[256,1024]{0,1:T(8,128)(2,1)S(1)}, u32[]{:S(2)}, u32[]{:S(2)}) %collective-permute-start.13) | collective-permute-done | bytes 524320 | tf_op jit(solution)/shard_map/ppermute | solution.py:31
  190.8 4.2 fusion.101
  198.0 7.9 %multiply_reduce_fusion.4 = (f32[1024]{0:T(1024)S(1)}, f32[1024]{0:T(1024)S(1)}, f32[1024]{0:T(1024)S(1)}, f32[1024]{0:T(1024)S(1)}, f32[1024]{0:T(1024)S(1)}, /...) fusion(f32[1024]{0:T(1024)S(1)} %copy-done.137, f32[1024,1024]{0,1:T(8,128)S(1)} %fusion.104, ...), kind=kOutput, calls=%fused_computation.50 | convolution fusion | flops 2187321344 | bytes 21008384 | tf_op jit(solution)/shard_map/dot_general | solution.py:27
  211.3 8.0 %fusion.102 = f32[1024,1024]{1,0:T(8,128)} fusion(bf16[256,1024]{0,1:T(8,128)(2,1)} %bitcast.246, bf16[256,1024]{0,1:T(8,128)(2,1)} %bitcast.244, bf16[256,1024]{0,1:T(8,128)(2,1)} %bitcast.242, bf16[256,1024]{0,1:T(8,128)(2,1)} %bitcast.228, f32[1024]{0:T(1024)S(1)} %get-tuple-element.194, f32[1024]{0:T(1024)S(1)} %bitcast.265, f32[1024]{0:T(1024)S(1)} %copy-done.137, ...), kind=kOutput, calls=%fused_computation.233 | convolution fusion | flops 2168455168 | bytes 10498048 | tf_op jit(solution)/shard_map/dot_general | solution.py:27
  219.3 5.3 fusion.180
  224.8 4.9 fusion.179
  229.7 5.5 convolution_add_fusion
  235.2 5.7 multiply_reduce_fusion
  244.1 5.8 multiply_reduce_fusion.1
  258.4 10.7 %collective-permute-done.57 = bf16[256,1024]{0,1:T(8,128)(2,1)S(1)} collective-permute-done((bf16[256,1024]{0,1:T(8,128)(2,1)S(1)}, bf16[256,1024]{0,1:T(8,128)(2,1)S(1)}, u32[]{:S(2)}, u32[]{:S(2)}) %collective-permute-start.57) | collective-permute-done | bytes 524320 | tf_op jit(solution)/shard_map/ppermute | solution.py:31
  269.9 10.5 %collective-permute-done.42 = bf16[256,1024]{0,1:T(8,128)(2,1)} collective-permute-done((bf16[256,1024]{0,1:T(8,128)(2,1)S(1)}, bf16[256,1024]{0,1:T(8,128)(2,1)}, u32[]{:S(2)}, u32[]{:S(2)}) %collective-permute-start.42) | collective-permute-done | bytes 524320 | tf_op jit(solution)/shard_map/ppermute | solution.py:31
  283.2 8.4 %collective-permute-done.19 = bf16[256,1024]{0,1:T(8,128)(2,1)S(1)} collective-permute-done((bf16[256,1024]{0,1:T(8,128)(2,1)S(1)}, bf16[256,1024]{0,1:T(8,128)(2,1)S(1)}, u32[]{:S(2)}, u32[]{:S(2)}) %collective-permute-start.19) | collective-permute-done | bytes 524320 | tf_op jit(solution)/shard_map/ppermute | solution.py:31
  292.7 9.6 %collective-permute-done.39 = bf16[256,1024]{0,1:T(8,128)(2,1)S(1)} collective-permute-done((bf16[256,1024]{0,1:T(8,128)(2,1)S(1)}, bf16[256,1024]{0,1:T(8,128)(2,1)S(1)}, u32[]{:S(2)}, u32[]{:S(2)}) %collective-permute-start.39) | collective-permute-done | bytes 524320 | tf_op jit(solution)/shard_map/ppermute | solution.py:31
  305.6 3.6 fusion.100
  310.8 9.4 %collective-permute-done.59 = bf16[256,1024]{0,1:T(8,128)(2,1)} collective-permute-done((bf16[256,1024]{0,1:T(8,128)(2,1)}, bf16[256,1024]{0,1:T(8,128)(2,1)}, u32[]{:S(2)}, u32[]{:S(2)}) %collective-permute-start.59) | collective-permute-done | bytes 524320 | tf_op jit(solution)/shard_map/ppermute | solution.py:31
  322.6 3.4 fusion.21
  333.1 26.2 %attend_backward.3 = (bf16[1024,256]{1,0:T(8,128)(2,1)S(1)}, bf16[1024,256]{1,0:T(8,128)(2,1)S(1)}, bf16[1024,256]{1,0:T(8,128)(2,1)S(1)}, bf16[1024,256]{1,0:T(...) custom-call(s32[3]{0:T(128)S(1)} %add_add_fusion.3.place, ...), custom_call_target="tpu_custom_call" | custom-call | flops 35999997952 | bytes 12582912 | tf_op jit(solution)/shard_map/attend_backward/pallas_call | solution.py:296
  362.3 6.6 collective-permute-start.65
  372.0 34.1 %attend_backward.2 = (bf16[1024,256]{1,0:T(8,128)(2,1)S(1)}, bf16[1024,256]{1,0:T(8,128)(2,1)S(1)}, bf16[1024,256]{1,0:T(8,128)(2,1)S(1)}, bf16[1024,256]{1,0:T(...) custom-call(s32[3]{0:T(128)S(1)} %copy-done.15, ...), custom_call_target="tpu_custom_call" | custom-call | flops 35999997952 | bytes 12582912 | tf_op jit(solution)/shard_map/attend_backward/pallas_call | solution.py:296
  406.2 3.4 fusion.105
  419.5 4.7 fusion.23
  428.9 5.6 collective-permute-done.47
  434.7 6.1 collective-permute-done.50
  441.2 15.8 %collective-permute-done.82 = bf16[512,1024]{1,0:T(8,128)(2,1)S(1)} collective-permute-done((bf16[512,1024]{1,0:T(8,128)(2,1)S(1)}, bf16[512,1024]{1,0:T(8,128)(2,1)S(1)}, u32[]{:S(2)}, u32[]{:S(2)}) %collective-permute-start.82) | collective-permute-done | bytes 1048608 | tf_op jit(solution)/shard_map/ppermute | solution.py:31
  464.8 14.7 %collective-permute-done.66 = bf16[1024,256]{1,0:T(8,128)(2,1)S(1)} collective-permute-done((bf16[1024,256]{1,0:T(8,128)(2,1)S(1)}, bf16[1024,256]{1,0:T(8,128)(2,1)S(1)}, u32[]{:S(2)}, u32[]{:S(2)}) %collective-permute-start.66) | collective-permute-done | bytes 524320 | tf_op jit(solution)/shard_map/ppermute | solution.py:31
  484.7 11.4 %collective-permute-done.51 = bf16[1024,256]{1,0:T(8,128)(2,1)S(1)} collective-permute-done((bf16[1024,256]{1,0:T(8,128)(2,1)S(1)}, bf16[1024,256]{1,0:T(8,128)(2,1)S(1)}, u32[]{:S(2)}, u32[]{:S(2)}) %collective-permute-start.51) | collective-permute-done | bytes 524320 | tf_op jit(solution)/shard_map/ppermute | solution.py:31
  500.7 4.9 add.541
  519.6 12.5 %collective-permute-done.75 = bf16[512,1024]{1,0:T(8,128)(2,1)S(1)} collective-permute-done((bf16[512,1024]{1,0:T(8,128)(2,1)S(1)}, bf16[512,1024]{1,0:T(8,128)(2,1)S(1)}, u32[]{:S(2)}, u32[]{:S(2)}) %collective-permute-start.75) | collective-permute-done | bytes 1048608 | tf_op jit(solution)/shard_map/ppermute | solution.py:31
  533.6 10.3 %collective-permute-done.84 = bf16[256,1024]{1,0:T(8,128)(2,1)S(1)} collective-permute-done((bf16[256,1024]{1,0:T(8,128)(2,1)S(1)}, bf16[256,1024]{1,0:T(8,128)(2,1)S(1)}, u32[]{:S(2)}, u32[]{:S(2)}) %collective-permute-start.84) | collective-permute-done | bytes 524320 | tf_op jit(solution)/shard_map/ppermute | solution.py:31
  547.9 10.7 %collective-permute-done.76 = bf16[256,1024]{1,0:T(8,128)(2,1)S(1)} collective-permute-done((bf16[256,1024]{1,0:T(8,128)(2,1)S(1)}, bf16[256,1024]{1,0:T(8,128)(2,1)S(1)}, u32[]{:S(2)}, u32[]{:S(2)}) %collective-permute-start.76) | collective-permute-done | bytes 524320 | tf_op jit(solution)/shard_map/ppermute | solution.py:31
  559.3 24.3 %collective-permute-done.77 = bf16[128,1024]{1,0:T(8,128)(2,1)S(1)} collective-permute-done((bf16[128,1024]{1,0:T(8,128)(2,1)S(1)}, bf16[128,1024]{1,0:T(8,128)(2,1)S(1)}, u32[]{:S(2)}, u32[]{:S(2)}) %collective-permute-start.77) | collective-permute-done | bytes 262176 | tf_op jit(solution)/shard_map/ppermute | solution.py:31
  583.7 3.4 collective-permute-start.78
  587.9 10.9 %collective-permute-done.78 = bf16[128,1024]{1,0:T(8,128)(2,1)S(1)} collective-permute-done((bf16[128,1024]{1,0:T(8,128)(2,1)S(1)}, bf16[128,1024]{1,0:T(8,128)(2,1)S(1)}, u32[]{:S(2)}, u32[]{:S(2)}) %collective-permute-start.78) | collective-permute-done | bytes 262176 | tf_op jit(solution)/shard_map/ppermute | solution.py:31
  602.7 8.9 %collective-permute-done.79 = bf16[256,1024]{1,0:T(8,128)(2,1)S(1)} collective-permute-done((bf16[256,1024]{1,0:T(8,128)(2,1)S(1)}, bf16[256,1024]{1,0:T(8,128)(2,1)S(1)}, u32[]{:S(2)}, u32[]{:S(2)}) %collective-permute-start.79) | collective-permute-done | bytes 524320 | tf_op jit(solution)/shard_map/ppermute | solution.py:31
  614.5 35.5 %collective-permute-done.72 = f32[5,1024]{1,0:T(8,128)S(1)} collective-permute-done((f32[5,1024]{1,0:T(8,128)S(1)}, f32[5,1024]{1,0:T(8,128)S(1)}, u32[]{:S(2)}, u32[]{:S(2)}) %collective-permute-start.72) | collective-permute-done | bytes 20512 | tf_op jit(solution)/shard_map/ppermute | solution.py:31
  660.0 10.5 %collective-permute-done.80 = bf16[512,1024]{1,0:T(8,128)(2,1)} collective-permute-done((bf16[512,1024]{1,0:T(8,128)(2,1)}, bf16[512,1024]{1,0:T(8,128)(2,1)}, u32[]{:S(2)}, u32[]{:S(2)}) %collective-permute-start.80) | collective-permute-done | bytes 1048608 | tf_op jit(solution)/shard_map/ppermute | solution.py:31
  676.7 4.8 reshape.464
  681.5 4.3 fusion.24
  685.8 4.3 slice_bitcast_fusion
  (647 shorter events, 206.9 us)
Async XLA Ops:
  9.4 23.5 %collective-permute-start.21 = (bf16[256,1024]{0,1:T(8,128)(2,1)}, bf16[256,1024]{0,1:T(8,128)(2,1)}, u32[]{:S(2)}, u32[]{:S(2)}) collective-permute-start(bf16[256,1024]{0,1:T(8,128)(2,1)} %get-tuple-element.209), channel_id=1, source_target_pairs={{0,2},{1,3},{2,0},{3,1},{4,6},{5,7},{6,4},{7,5},{8,10},{9,11},{10,... | collective-permute-start | bytes 1572872 | tf_op jit(solution)/shard_map/ppermute | solution.py:31
  9.5 23.4 %collective-permute-start = (bf16[256,1024]{0,1:T(8,128)(2,1)}, bf16[256,1024]{0,1:T(8,128)(2,1)}, u32[]{:S(2)}, u32[]{:S(2)}) collective-permute-start(bf16[256,1024]{0,1:T(8,128)(2,1)} %get-tuple-element.208), channel_id=1, source_target_pairs={{0,1},{1,0},{2,3},{3,2},{4,5},{5,4},{6,7},{7,6},{8,9},{9,8},{10,11... | collective-permute-start | bytes 1572872 | tf_op jit(solution)/shard_map/ppermute | solution.py:31
  37.2 27.6 %collective-permute-start.4 = (bf16[1024,256]{1,0:T(8,128)(2,1)S(1)}, bf16[1024,256]{1,0:T(8,128)(2,1)S(1)}, u32[]{:S(2)}, u32[]{:S(2)}) collective-permute-start(bf16[1024,256]{1,0:T(8,128)(2,1)S(1)} %convolution_convert_fusion.4.rest_0_), channel_id=1, source_target_pairs={{0,8},{4,12},{8,0},{12,4},{16,24},{20,28},{24,16},{28,20},{1,9},{5... | collective-permute-start | bytes 1572872 | tf_op jit(solution)/shard_map/ppermute | solution.py:31
  41.1 22.1 %collective-permute-start.7 = (bf16[1024,256]{1,0:T(8,128)(2,1)S(1)}, bf16[1024,256]{1,0:T(8,128)(2,1)S(1)}, u32[]{:S(2)}, u32[]{:S(2)}) collective-permute-start(bf16[1024,256]{1,0:T(8,128)(2,1)S(1)} %convolution_convert_fusion.3.rest_4_), channel_id=1, source_target_pairs={{0,8},{4,12},{8,0},{12,4},{16,24},{20,28},{24,16},{28,20},{1,9},{5... | collective-permute-start | bytes 1572872 | tf_op jit(solution)/shard_map/ppermute | solution.py:31
  41.6 28.4 %collective-permute-start.6 = (bf16[1024,256]{1,0:T(8,128)(2,1)S(1)}, bf16[1024,256]{1,0:T(8,128)(2,1)S(1)}, u32[]{:S(2)}, u32[]{:S(2)}) collective-permute-start(bf16[1024,256]{1,0:T(8,128)(2,1)S(1)} %convolution_convert_fusion.3.rest_4_), channel_id=1, source_target_pairs={{0,4},{4,0},{8,12},{12,8},{16,20},{20,16},{24,28},{28,24},{1,5},{5... | collective-permute-start | bytes 1572872 | tf_op jit(solution)/shard_map/ppermute | solution.py:31
  44.2 30.2 %collective-permute-start.27 = (bf16[1024,256]{1,0:T(8,128)(2,1)S(1)}, bf16[1024,256]{1,0:T(8,128)(2,1)S(1)}, u32[]{:S(2)}, u32[]{:S(2)}) collective-permute-start(bf16[1024,256]{1,0:T(8,128)(2,1)S(1)} %convolution_convert_fusion.rest_4_), channel_id=1, source_target_pairs={{0,8},{4,12},{8,0},{12,4},{16,24},{20,28},{24,16},{28,20},{1,9},{5... | collective-permute-start | bytes 1572872 | tf_op jit(solution)/shard_map/ppermute | solution.py:31
  50.2 25.8 %collective-permute-start.23 = (bf16[1024,256]{1,0:T(8,128)(2,1)S(1)}, bf16[1024,256]{1,0:T(8,128)(2,1)S(1)}, u32[]{:S(2)}, u32[]{:S(2)}) collective-permute-start(bf16[1024,256]{1,0:T(8,128)(2,1)S(1)} %convolution_convert_fusion.1.rest_0_), channel_id=1, source_target_pairs={{0,4},{4,0},{8,12},{12,8},{16,20},{20,16},{24,28},{28,24},{1,5},{5... | collective-permute-start | bytes 1572872 | tf_op jit(solution)/shard_map/ppermute | solution.py:31
  63.2 22.5 %collective-permute-start.5 = (bf16[1024,256]{1,0:T(8,128)(2,1)S(1)}, bf16[1024,256]{1,0:T(8,128)(2,1)S(1)}, u32[]{:S(2)}, u32[]{:S(2)}) collective-permute-start(bf16[1024,256]{1,0:T(8,128)(2,1)S(1)} %collective-permute-done.3.rest_1_), channel_id=1, source_target_pairs={{0,8},{4,12},{8,0},{12,4},{16,24},{20,28},{24,16},{28,20},{1,9},{5... | collective-permute-start | bytes 1572872 | tf_op jit(solution)/shard_map/ppermute | solution.py:31
  64.8 22.5 %collective-permute-start.8 = (bf16[1024,256]{1,0:T(8,128)(2,1)S(1)}, bf16[1024,256]{1,0:T(8,128)(2,1)S(1)}, u32[]{:S(2)}, u32[]{:S(2)}) collective-permute-start(bf16[1024,256]{1,0:T(8,128)(2,1)S(1)} %collective-permute-done.7.rest_6_), channel_id=1, source_target_pairs={{0,4},{4,0},{8,12},{12,8},{16,20},{20,16},{24,28},{28,24},{1,5},{5... | collective-permute-start | bytes 1572872 | tf_op jit(solution)/shard_map/ppermute | solution.py:31
  70.0 32.8 %collective-permute-start.26 = (bf16[1024,256]{1,0:T(8,128)(2,1)S(1)}, bf16[1024,256]{1,0:T(8,128)(2,1)S(1)}, u32[]{:S(2)}, u32[]{:S(2)}) collective-permute-start(bf16[1024,256]{1,0:T(8,128)(2,1)S(1)} %convolution_convert_fusion.rest_4_), channel_id=1, source_target_pairs={{0,4},{4,0},{8,12},{12,8},{16,20},{20,16},{24,28},{28,24},{1,5},{5... | collective-permute-start | bytes 1572872 | tf_op jit(solution)/shard_map/ppermute | solution.py:31
  74.4 28.4 %collective-permute-start.24 = (bf16[1024,256]{1,0:T(8,128)(2,1)S(1)}, bf16[1024,256]{1,0:T(8,128)(2,1)S(1)}, u32[]{:S(2)}, u32[]{:S(2)}) collective-permute-start(bf16[1024,256]{1,0:T(8,128)(2,1)S(1)} %convolution_convert_fusion.1.rest_0_), channel_id=1, source_target_pairs={{0,8},{4,12},{8,0},{12,4},{16,24},{20,28},{24,16},{28,20},{1,9},{5... | collective-permute-start | bytes 1572872 | tf_op jit(solution)/shard_map/ppermute | solution.py:31
  76.0 30.0 %collective-permute-start.28 = (bf16[1024,256]{1,0:T(8,128)(2,1)S(1)}, bf16[1024,256]{1,0:T(8,128)(2,1)S(1)}, u32[]{:S(2)}, u32[]{:S(2)}) collective-permute-start(bf16[1024,256]{1,0:T(8,128)(2,1)S(1)} %collective-permute-done.27.rest_6_), channel_id=1, source_target_pairs={{0,4},{4,0},{8,12},{12,8},{16,20},{20,16},{24,28},{28,24},{1,5},{5... | collective-permute-start | bytes 1572872 | tf_op jit(solution)/shard_map/ppermute | solution.py:31
  85.7 21.8 %collective-permute-start.25 = (bf16[1024,256]{1,0:T(8,128)(2,1)S(1)}, bf16[1024,256]{1,0:T(8,128)(2,1)S(1)}, u32[]{:S(2)}, u32[]{:S(2)}) collective-permute-start(bf16[1024,256]{1,0:T(8,128)(2,1)S(1)} %collective-permute-done.23.rest_1_), channel_id=1, source_target_pairs={{0,8},{4,12},{8,0},{12,4},{16,24},{20,28},{24,16},{28,20},{1,9},{5... | collective-permute-start | bytes 1572872 | tf_op jit(solution)/shard_map/ppermute | solution.py:31
  102.8 23.0 %collective-permute-start.10 = (bf16[256,1024]{0,1:T(8,128)(2,1)S(1)}, bf16[256,1024]{0,1:T(8,128)(2,1)S(1)}, u32[]{:S(2)}, u32[]{:S(2)}) collective-permute-start(bf16[256,1024]{0,1:T(8,128)(2,1)S(1)} %get-tuple-element.154), channel_id=1, source_target_pairs={{0,1},{1,0},{2,3},{3,2},{4,5},{5,4},{6,7},{7,6},{8,9},{9,8},{10,11... | collective-permute-start | bytes 1572872 | tf_op jit(solution)/shard_map/ppermute | solution.py:31
  129.7 22.3 %collective-permute-start.31 = (bf16[256,1024]{0,1:T(8,128)(2,1)S(1)}, bf16[256,1024]{0,1:T(8,128)(2,1)S(1)}, u32[]{:S(2)}, u32[]{:S(2)}) collective-permute-start(bf16[256,1024]{0,1:T(8,128)(2,1)S(1)} %fusion.73), channel_id=1, source_target_pairs={{0,2},{1,3},{2,0},{3,1},{4,6},{5,7},{6,4},{7,5},{8,10},{9,11},{10,... | collective-permute-start | bytes 1572872 | tf_op jit(solution)/shard_map/ppermute | solution.py:31
  156.6 20.3 %collective-permute-start.33 = (bf16[256,1024]{0,1:T(8,128)(2,1)}, bf16[256,1024]{0,1:T(8,128)(2,1)}, u32[]{:S(2)}, u32[]{:S(2)}) collective-permute-start(bf16[256,1024]{0,1:T(8,128)(2,1)} %get-tuple-element.204), channel_id=1, source_target_pairs={{0,2},{1,3},{2,0},{3,1},{4,6},{5,7},{6,4},{7,5},{8,10},{9,11},{10,... | collective-permute-start | bytes 1572872 | tf_op jit(solution)/shard_map/ppermute | solution.py:31
  255.2 25.2 %collective-permute-start.42 = (bf16[256,1024]{0,1:T(8,128)(2,1)S(1)}, bf16[256,1024]{0,1:T(8,128)(2,1)}, u32[]{:S(2)}, u32[]{:S(2)}) collective-permute-start(bf16[256,1024]{0,1:T(8,128)(2,1)S(1)} %fusion.67), channel_id=1, source_target_pairs={{0,2},{1,3},{2,0},{3,1},{4,6},{5,7},{6,4},{7,5},{8,10},{9,11},{10,... | collective-permute-start | bytes 1572872 | tf_op jit(solution)/shard_map/ppermute | solution.py:31
  256.9 26.3 %collective-permute-start.17 = (bf16[256,1024]{0,1:T(8,128)(2,1)S(1)}, bf16[256,1024]{0,1:T(8,128)(2,1)S(1)}, u32[]{:S(2)}, u32[]{:S(2)}) collective-permute-start(bf16[256,1024]{0,1:T(8,128)(2,1)S(1)} %get-tuple-element.145), channel_id=1, source_target_pairs={{0,1},{1,0},{2,3},{3,2},{4,5},{5,4},{6,7},{7,6},{8,9},{9,8},{10,11... | collective-permute-start | bytes 1572872 | tf_op jit(solution)/shard_map/ppermute | solution.py:31
  257.2 35.5 %collective-permute-start.37 = (bf16[256,1024]{0,1:T(8,128)(2,1)S(1)}, bf16[256,1024]{0,1:T(8,128)(2,1)S(1)}, u32[]{:S(2)}, u32[]{:S(2)}) collective-permute-start(bf16[256,1024]{0,1:T(8,128)(2,1)S(1)} %get-tuple-element.147), channel_id=1, source_target_pairs={{0,1},{1,0},{2,3},{3,2},{4,5},{5,4},{6,7},{7,6},{8,9},{9,8},{10,11... | collective-permute-start | bytes 1572872 | tf_op jit(solution)/shard_map/ppermute | solution.py:31
  257.8 33.8 %collective-permute-start.19 = (bf16[256,1024]{0,1:T(8,128)(2,1)S(1)}, bf16[256,1024]{0,1:T(8,128)(2,1)S(1)}, u32[]{:S(2)}, u32[]{:S(2)}) collective-permute-start(bf16[256,1024]{0,1:T(8,128)(2,1)S(1)} %fusion.75), channel_id=1, source_target_pairs={{0,2},{1,3},{2,0},{3,1},{4,6},{5,7},{6,4},{7,5},{8,10},{9,11},{10,... | collective-permute-start | bytes 1572872 | tf_op jit(solution)/shard_map/ppermute | solution.py:31
  269.1 33.1 %collective-permute-start.39 = (bf16[256,1024]{0,1:T(8,128)(2,1)S(1)}, bf16[256,1024]{0,1:T(8,128)(2,1)S(1)}, u32[]{:S(2)}, u32[]{:S(2)}) collective-permute-start(bf16[256,1024]{0,1:T(8,128)(2,1)S(1)} %fusion.69), channel_id=1, source_target_pairs={{0,2},{1,3},{2,0},{3,1},{4,6},{5,7},{6,4},{7,5},{8,10},{9,11},{10,... | collective-permute-start | bytes 1572872 | tf_op jit(solution)/shard_map/ppermute | solution.py:31
  309.2 21.2 %collective-permute-start.58 = (bf16[256,1024]{0,1:T(8,128)(2,1)}, bf16[256,1024]{0,1:T(8,128)(2,1)}, u32[]{:S(2)}, u32[]{:S(2)}) collective-permute-start(bf16[256,1024]{0,1:T(8,128)(2,1)} %get-tuple-element.199), channel_id=1, source_target_pairs={{0,1},{1,0},{2,3},{3,2},{4,5},{5,4},{6,7},{7,6},{8,9},{9,8},{10,11... | collective-permute-start | bytes 1572872 | tf_op jit(solution)/shard_map/ppermute | solution.py:31
  309.3 20.7 %collective-permute-start.44 = (bf16[256,1024]{0,1:T(8,128)(2,1)}, bf16[256,1024]{0,1:T(8,128)(2,1)}, u32[]{:S(2)}, u32[]{:S(2)}) collective-permute-start(bf16[256,1024]{0,1:T(8,128)(2,1)} %get-tuple-element.198), channel_id=1, source_target_pairs={{0,2},{1,3},{2,0},{3,1},{4,6},{5,7},{6,4},{7,5},{8,10},{9,11},{10,... | collective-permute-start | bytes 1572872 | tf_op jit(solution)/shard_map/ppermute | solution.py:31
  326.0 93.3 %collective-permute-start.81 = (bf16[1024,1024]{1,0:T(8,128)(2,1)}, bf16[1024,1024]{1,0:T(8,128)(2,1)}, u32[]{:S(2)}, u32[]{:S(2)}) collective-permute-start(bf16[1024,1024]{1,0:T(8,128)(2,1)} %fusion.21), channel_id=1, source_target_pairs={{0,4},{4,0},{8,12},{12,8},{16,20},{20,16},{24,28},{28,24},{1,5},{5... | collective-permute-start | bytes 6291464 | tf_op jit(solution)/shard_map/ppermute | solution.py:31
  327.1 35.2 %collective-permute-start.43 = (bf16[256,1024]{0,1:T(8,128)(2,1)}, bf16[256,1024]{0,1:T(8,128)(2,1)}, u32[]{:S(2)}, u32[]{:S(2)}) collective-permute-start(bf16[256,1024]{0,1:T(8,128)(2,1)} %get-tuple-element.198), channel_id=1, source_target_pairs={{0,1},{1,0},{2,3},{3,2},{4,5},{5,4},{6,7},{7,6},{8,9},{9,8},{10,11... | collective-permute-start | bytes 1572872 | tf_op jit(solution)/shard_map/ppermute | solution.py:31
  330.0 38.9 %collective-permute-start.45 = (bf16[256,1024]{0,1:T(8,128)(2,1)}, bf16[256,1024]{0,1:T(8,128)(2,1)S(1)}, u32[]{:S(2)}, u32[]{:S(2)}) collective-permute-start(bf16[256,1024]{0,1:T(8,128)(2,1)} %collective-permute-done.44), channel_id=1, source_target_pairs={{0,1},{1,0},{2,3},{3,2},{4,5},{5,4},{6,7},{7,6},{8,9},{9,8},{10,11... | collective-permute-start | bytes 1572872 | tf_op jit(solution)/shard_map/ppermute | solution.py:31
  359.3 65.1 %collective-permute-start.62 = (bf16[1024,256]{1,0:T(8,128)(2,1)}, bf16[1024,256]{1,0:T(8,128)(2,1)}, u32[]{:S(2)}, u32[]{:S(2)}) collective-permute-start(bf16[1024,256]{1,0:T(8,128)(2,1)} %get-tuple-element.56), channel_id=1, source_target_pairs={{0,8},{4,12},{8,0},{12,4},{16,24},{20,28},{24,16},{28,20},{1,9},{5... | collective-permute-start | bytes 1572872 | tf_op jit(solution)/shard_map/ppermute | solution.py:31
  362.2 95.2 %collective-permute-start.61 = (bf16[1024,256]{1,0:T(8,128)(2,1)}, bf16[1024,256]{1,0:T(8,128)(2,1)}, u32[]{:S(2)}, u32[]{:S(2)}) collective-permute-start(bf16[1024,256]{1,0:T(8,128)(2,1)} %get-tuple-element.54), channel_id=1, source_target_pairs={{0,8},{4,12},{8,0},{12,4},{16,24},{20,28},{24,16},{28,20},{1,9},{5... | collective-permute-start | bytes 1572872 | tf_op jit(solution)/shard_map/ppermute | solution.py:31
  362.3 65.3 %collective-permute-start.65 = (bf16[1024,256]{1,0:T(8,128)(2,1)}, bf16[1024,256]{1,0:T(8,128)(2,1)}, u32[]{:S(2)}, u32[]{:S(2)}) collective-permute-start(bf16[1024,256]{1,0:T(8,128)(2,1)} %get-tuple-element.60), channel_id=1, source_target_pairs={{0,4},{4,0},{8,12},{12,8},{16,20},{20,16},{24,28},{28,24},{1,5},{5... | collective-permute-start | bytes 1572872 | tf_op jit(solution)/shard_map/ppermute | solution.py:31
  369.0 93.9 %collective-permute-start.64 = (bf16[1024,256]{1,0:T(8,128)(2,1)}, bf16[1024,256]{1,0:T(8,128)(2,1)}, u32[]{:S(2)}, u32[]{:S(2)}) collective-permute-start(bf16[1024,256]{1,0:T(8,128)(2,1)} %get-tuple-element.58), channel_id=1, source_target_pairs={{0,4},{4,0},{8,12},{12,8},{16,20},{20,16},{24,28},{28,24},{1,5},{5... | collective-permute-start | bytes 1572872 | tf_op jit(solution)/shard_map/ppermute | solution.py:31
  424.4 32.5 %collective-permute-start.82 = (bf16[512,1024]{1,0:T(8,128)(2,1)S(1)}, bf16[512,1024]{1,0:T(8,128)(2,1)S(1)}, u32[]{:S(2)}, u32[]{:S(2)}) collective-permute-start(bf16[512,1024]{1,0:T(8,128)(2,1)S(1)} %dynamic-slice_convert_fusion), channel_id=1, source_target_pairs={{0,8},{4,12},{8,0},{12,4},{16,24},{20,28},{24,16},{28,20},{1,9},{5... | collective-permute-start | bytes 3145736 | tf_op jit(solution)/shard_map/ppermute | solution.py:31
  434.5 47.5 %collective-permute-start.46 = (bf16[1024,256]{1,0:T(8,128)(2,1)S(1)}, bf16[1024,256]{1,0:T(8,128)(2,1)S(1)}, u32[]{:S(2)}, u32[]{:S(2)}) collective-permute-start(bf16[1024,256]{1,0:T(8,128)(2,1)S(1)} %copy-done.51), channel_id=1, source_target_pairs={{0,8},{4,12},{8,0},{12,4},{16,24},{20,28},{24,16},{28,20},{1,9},{5... | collective-permute-start | bytes 1572872 | tf_op jit(solution)/shard_map/ppermute | solution.py:31
  456.9 27.7 %collective-permute-start.49 = (bf16[1024,256]{1,0:T(8,128)(2,1)S(1)}, bf16[1024,256]{1,0:T(8,128)(2,1)S(1)}, u32[]{:S(2)}, u32[]{:S(2)}) collective-permute-start(bf16[1024,256]{1,0:T(8,128)(2,1)S(1)} %copy-done.49), channel_id=1, source_target_pairs={{0,4},{4,0},{8,12},{12,8},{16,20},{20,16},{24,28},{28,24},{1,5},{5... | collective-permute-start | bytes 1572872 | tf_op jit(solution)/shard_map/ppermute | solution.py:31
  457.4 22.0 %collective-permute-start.66 = (bf16[1024,256]{1,0:T(8,128)(2,1)S(1)}, bf16[1024,256]{1,0:T(8,128)(2,1)S(1)}, u32[]{:S(2)}, u32[]{:S(2)}) collective-permute-start(bf16[1024,256]{1,0:T(8,128)(2,1)S(1)} %add_convert_fusion.2), channel_id=1, source_target_pairs={{0,8},{4,12},{8,0},{12,4},{16,24},{20,28},{24,16},{28,20},{1,9},{5... | collective-permute-start | bytes 1572872 | tf_op jit(solution)/shard_map/ppermute | solution.py:31
  457.5 24.4 %collective-permute-start.48 = (bf16[1024,256]{1,0:T(8,128)(2,1)S(1)}, bf16[1024,256]{1,0:T(8,128)(2,1)S(1)}, u32[]{:S(2)}, u32[]{:S(2)}) collective-permute-start(bf16[1024,256]{1,0:T(8,128)(2,1)S(1)} %add_convert_fusion.11), channel_id=1, source_target_pairs={{0,4},{4,0},{8,12},{12,8},{16,20},{20,16},{24,28},{28,24},{1,5},{5... | collective-permute-start | bytes 1572872 | tf_op jit(solution)/shard_map/ppermute | solution.py:31
  462.8 33.2 %collective-permute-start.51 = (bf16[1024,256]{1,0:T(8,128)(2,1)S(1)}, bf16[1024,256]{1,0:T(8,128)(2,1)S(1)}, u32[]{:S(2)}, u32[]{:S(2)}) collective-permute-start(bf16[1024,256]{1,0:T(8,128)(2,1)S(1)} %add_convert_fusion.8), channel_id=1, source_target_pairs={{0,8},{4,12},{8,0},{12,4},{16,24},{20,28},{24,16},{28,20},{1,9},{5... | collective-permute-start | bytes 1572872 | tf_op jit(solution)/shard_map/ppermute | solution.py:31
  479.4 36.8 %collective-permute-start.83 = (bf16[256,1024]{1,0:T(8,128)(2,1)}, bf16[256,1024]{1,0:T(8,128)(2,1)}, u32[]{:S(2)}, u32[]{:S(2)}) collective-permute-start(bf16[256,1024]{1,0:T(8,128)(2,1)} %dynamic-slice_convert_fusion.1), channel_id=1, source_target_pairs={{0,16},{4,20},{8,24},{12,28},{16,0},{20,4},{24,8},{28,12},{1,17},{... | collective-permute-start | bytes 1572872 | tf_op jit(solution)/shard_map/ppermute | solution.py:31
  508.1 24.1 %collective-permute-start.75 = (bf16[512,1024]{1,0:T(8,128)(2,1)S(1)}, bf16[512,1024]{1,0:T(8,128)(2,1)S(1)}, u32[]{:S(2)}, u32[]{:S(2)}) collective-permute-start(bf16[512,1024]{1,0:T(8,128)(2,1)S(1)} %fusion.26), channel_id=1, source_target_pairs={{0,4},{4,0},{8,12},{12,8},{16,20},{20,16},{24,28},{28,24},{1,5},{5... | collective-permute-start | bytes 3145736 | tf_op jit(solution)/shard_map/ppermute | solution.py:31
  511.0 33.1 %collective-permute-start.52 = (bf16[256,1024]{0,1:T(8,128)(2,1)S(1)}, bf16[256,1024]{0,1:T(8,128)(2,1)S(1)}, u32[]{:S(2)}, u32[]{:S(2)}) collective-permute-start(bf16[256,1024]{0,1:T(8,128)(2,1)S(1)} %get-tuple-element.137), channel_id=1, source_target_pairs={{0,1},{1,0},{2,3},{3,2},{4,5},{5,4},{6,7},{7,6},{8,9},{9,8},{10,11... | collective-permute-start | bytes 1572872 | tf_op jit(solution)/shard_map/ppermute | solution.py:31
  516.2 30.6 %collective-permute-start.67 = (bf16[256,1024]{0,1:T(8,128)(2,1)S(1)}, bf16[256,1024]{0,1:T(8,128)(2,1)S(1)}, u32[]{:S(2)}, u32[]{:S(2)}) collective-permute-start(bf16[256,1024]{0,1:T(8,128)(2,1)S(1)} %get-tuple-element.141), channel_id=1, source_target_pairs={{0,1},{1,0},{2,3},{3,2},{4,5},{5,4},{6,7},{7,6},{8,9},{9,8},{10,11... | collective-permute-start | bytes 1572872 | tf_op jit(solution)/shard_map/ppermute | solution.py:31
  518.3 25.6 %collective-permute-start.84 = (bf16[256,1024]{1,0:T(8,128)(2,1)S(1)}, bf16[256,1024]{1,0:T(8,128)(2,1)S(1)}, u32[]{:S(2)}, u32[]{:S(2)}) collective-permute-start(bf16[256,1024]{1,0:T(8,128)(2,1)S(1)} %add_convert_fusion), channel_id=1, source_target_pairs={{0,16},{4,20},{8,24},{12,28},{16,0},{20,4},{24,8},{28,12},{1,17},{... | collective-permute-start | bytes 1572872 | tf_op jit(solution)/shard_map/ppermute | solution.py:31
  518.7 27.5 %collective-permute-start.54 = (bf16[256,1024]{0,1:T(8,128)(2,1)S(1)}, bf16[256,1024]{0,1:T(8,128)(2,1)S(1)}, u32[]{:S(2)}, u32[]{:S(2)}) collective-permute-start(bf16[256,1024]{0,1:T(8,128)(2,1)S(1)} %fusion.65), channel_id=1, source_target_pairs={{0,2},{1,3},{2,0},{3,1},{4,6},{5,7},{6,4},{7,5},{8,10},{9,11},{10,... | collective-permute-start | bytes 1572872 | tf_op jit(solution)/shard_map/ppermute | solution.py:31
  544.1 54.8 %collective-permute-start.85 = (bf16[512,1024]{1,0:T(8,128)(2,1)S(1)}, bf16[512,1024]{1,0:T(8,128)(2,1)S(1)}, u32[]{:S(2)}, u32[]{:S(2)}) collective-permute-start(bf16[512,1024]{1,0:T(8,128)(2,1)S(1)} %bitcast.223), channel_id=1, source_target_pairs={{0,8},{4,12},{8,0},{12,4},{16,24},{20,28},{24,16},{28,20},{1,9},{5... | collective-permute-start | bytes 3145736 | tf_op jit(solution)/shard_map/ppermute | solution.py:31
  558.9 24.8 %collective-permute-start.77 = (bf16[128,1024]{1,0:T(8,128)(2,1)S(1)}, bf16[128,1024]{1,0:T(8,128)(2,1)S(1)}, u32[]{:S(2)}, u32[]{:S(2)}) collective-permute-start(bf16[128,1024]{1,0:T(8,128)(2,1)S(1)} %dynamic-slice_convert_fusion.3), channel_id=1, source_target_pairs={{0,16},{4,20},{8,24},{12,28},{16,0},{20,4},{24,8},{28,12},{1,17},{... | collective-permute-start | bytes 786440 | tf_op jit(solution)/shard_map/ppermute | solution.py:31
  559.2 27.9 %collective-permute-start.70 = (f32[3,1024]{1,0:T(4,128)S(1)}, f32[3,1024]{1,0:T(4,128)S(1)}, u32[]{:S(2)}, u32[]{:S(2)}) collective-permute-start(f32[3,1024]{1,0:T(4,128)S(1)} %pad_maximum_fusion.25), channel_id=1, source_target_pairs={{0,1},{1,0},{2,3},{3,2},{4,5},{5,4},{6,7},{7,6},{8,9},{9,8},{10,11... | collective-permute-start | bytes 36872 | tf_op jit(solution)/shard_map/ppermute | solution.py:31
  600.6 80.9 %collective-permute-start.86 = (bf16[1024,1024]{1,0:T(8,128)(2,1)}, bf16[1024,1024]{1,0:T(8,128)(2,1)}, u32[]{:S(2)}, u32[]{:S(2)}) collective-permute-start(bf16[1024,1024]{1,0:T(8,128)(2,1)} %bitcast.67), channel_id=1, source_target_pairs={{0,4},{4,0},{8,12},{12,8},{16,20},{20,16},{24,28},{28,24},{1,5},{5... | collective-permute-start | bytes 6291464 | tf_op jit(solution)/shard_map/ppermute | solution.py:31
  602.4 47.7 %collective-permute-start.72 = (f32[5,1024]{1,0:T(8,128)S(1)}, f32[5,1024]{1,0:T(8,128)S(1)}, u32[]{:S(2)}, u32[]{:S(2)}) collective-permute-start(f32[5,1024]{1,0:T(8,128)S(1)} %pad_maximum_fusion.22), channel_id=1, source_target_pairs={{0,4},{4,0},{8,12},{12,8},{16,20},{20,16},{24,28},{28,24},{1,5},{5... | collective-permute-start | bytes 61448 | tf_op jit(solution)/shard_map/ppermute | solution.py:31
  612.8 57.7 %collective-permute-start.80 = (bf16[512,1024]{1,0:T(8,128)(2,1)}, bf16[512,1024]{1,0:T(8,128)(2,1)}, u32[]{:S(2)}, u32[]{:S(2)}) collective-permute-start(bf16[512,1024]{1,0:T(8,128)(2,1)} %bitcast.54), channel_id=1, source_target_pairs={{0,4},{4,0},{8,12},{12,8},{16,20},{20,16},{24,28},{28,24},{1,5},{5... | collective-permute-start | bytes 3145736 | tf_op jit(solution)/shard_map/ppermute | solution.py:31
  (198 other events, 2843.3 us)

commit v2 on v1

--- a/solution.py
+++ b/solution.py
@@ -171,8 +171,7 @@
 
 def attend_backward(place, parents, q_ref, dos_ref, o_ref, lse_ref, scale_ref, *rest):
     keys, values = rest[0:4], rest[4:8]
-    dq_ref, dks, dvs, sg_ref = rest[8], rest[9:13], rest[13:17], rest[17]
-    tree, acc, dqt, sems = rest[18:]
+    dq_ref, dk_ref, dv_ref, sg_ref, tree, acc, dqt, sems = rest[8:]
     step = pl.program_id(0)
     width = q_ref.shape[1]
     heads = width // HEAD_DIM
@@ -246,8 +245,8 @@
     @pl.when(step == pl.num_programs(0) - 1)
     def _():
         for r in range(4):
-            dks[r][...] = acc[r * tokens:(r + 1) * tokens, 0:width].astype(BF)
-            dvs[r][...] = acc[r * tokens:(r + 1) * tokens, width:2 * width].astype(BF)
+            dk_ref[r] = acc[r * tokens:(r + 1) * tokens, 0:width].astype(BF)
+            dv_ref[r] = acc[r * tokens:(r + 1) * tokens, width:2 * width].astype(BF)
 
 
 ROW = lambda i, *s: (i, 0)
@@ -291,11 +290,16 @@
 def attention_grad(place, parents, q, dos, o, lse, scale_row, keys, values):
     tokens, width = q.shape
     segs = tokens // SEG
-    piece = jax.ShapeDtypeStruct((tokens, width), BF)
-    whole = pl.BlockSpec((tokens, width), FIX)
+    pieces = jax.ShapeDtypeStruct((4, tokens, width), BF)
+    whole = pl.BlockSpec((4, tokens, width), lambda i, *s: (0, 0, 0))
     return pl.pallas_call(
         attend_backward,
-        out_shape=(piece,) + (piece,) * 8 + (jax.ShapeDtypeStruct((8, width), F32),),
+        out_shape=(
+            jax.ShapeDtypeStruct((tokens, width), BF),
+            pieces,
+            pieces,
+            jax.ShapeDtypeStruct((8, width), F32),
+        ),
         grid_spec=pltpu.PrefetchScalarGridSpec(
             num_scalar_prefetch=2,
             grid=(segs,),
@@ -307,7 +311,7 @@
                 pl.BlockSpec((1, width), FIX),
             ]
             + [HBM] * 8,
-            out_specs=[pl.BlockSpec((SEG, width), ROW)] + [whole] * 8 + [pl.BlockSpec((8, width), FIX)],
+            out_specs=[pl.BlockSpec((SEG, width), ROW)] + [whole] * 2 + [pl.BlockSpec((8, width), FIX)],
             scratch_shapes=[
                 pltpu.VMEM((4 * tokens, 2 * width), BF),
                 pltpu.VMEM((4 * tokens, 2 * width), F32),
@@ -330,6 +334,694 @@
     act = 0.5 * c * (1.0 + tanh)
     slope = 0.5 * (1.0 + tanh) + 0.5 * c * (1.0 - tanh * tanh) * (root * (1.0 + 3 * 0.044715 * square))
     return act, slope
+
+
+def other(shard, mask):
+    near = shard + 1 - 2 * (shard % 2)
+    return {0: shard, 1: near, 2: (shard + 2) % 4, 3: (near + 2) % 4}[mask]
+
+
+def middle(
+    os0, os1, x, g_hbm, fc1_hbm, fc2_hbm, out_w, post, pre, wide,
+    z_hbm, dc_hbm, h2_hbm, du_hbm, dos, dr1, f_own, f_far, gains,
+    fc1, fc2, gd, act, slz, dzc, full, core_out, core_in, y_out, y_in, nu, inv, st_out, st_in, sums, cols,
+    send, recv, local,
+):
+    shard = lax.axis_index("tensor")
+    peers = [other(shard, k) for k in range(4)]
+    rows = x.shape[1]
+    model = x.shape[2]
+    hidden = fc1.shape[1]
+    parts = hidden // SEG
+    used = [0]
+    pending = []
+
+    def remote(src, dst, mask):
+        i = used[0]
+        used[0] += 1
+        copy = pltpu.make_async_remote_copy(
+            src_ref=src, dst_ref=dst, send_sem=send.at[i], recv_sem=recv.at[i],
+            device_id={"tensor": peers[mask]}, device_id_type=pl.DeviceIdType.MESH,
+        )
+        copy.start()
+        pending.append(copy)
+        return copy
+
+    stored = [0]
+    stores = []
+
+    def store(src, dst):
+        i = stored[0]
+        stored[0] += 1
+        copy = pltpu.make_async_copy(src, dst, local.at[i])
+        copy.start()
+        stores.append(copy)
+
+    def fetch(src, dst):
+        i = stored[0]
+        stored[0] += 1
+        copy = pltpu.make_async_copy(src, dst, local.at[i])
+        copy.start()
+        return copy
+
+    got_fc2 = fetch(fc2_hbm, fc2)
+    got_g = [
+        [fetch(g_hbm.at[m, pl.ds(peers[r] * rows, rows), :], gd.at[m, r]) for r in range(4)] for m in range(MICRO)
+    ]
+    got_fc1 = fetch(fc1_hbm, fc1)
+    barrier = pltpu.get_barrier_semaphore()
+    for mask in (1, 2, 3):
+        pl.semaphore_signal(
+            barrier, inc=1, device_id={"tensor": peers[mask]}, device_id_type=pl.DeviceIdType.MESH
+        )
+    pl.semaphore_wait(barrier, 3)
+    gains[...] = jnp.zeros_like(gains)
+
+    def each(count, fn):
+        lax.fori_loop(0, count, lambda i, c: (fn(i), c)[1], 0)
+
+    def tile(n):
+        return pl.ds(pl.multiple_of(n * SEG, SEG), SEG)
+
+    def first_hop(kind, m, block, out):
+        block(3, core_out.at[kind, m, 0])
+        hop3 = remote(core_out.at[kind, m, 0], core_in.at[kind, m, 0], 1)
+        block(1, core_out.at[kind, m, 1])
+        hop1 = remote(core_out.at[kind, m, 1], core_in.at[kind, m, 1], 1)
+        block(2, None)
+        block(0, out)
+        return hop3, hop1
+
+    chunk = 32
+
+    def chunks(fn):
+        each(rows // chunk, lambda i: fn(pl.ds(pl.multiple_of(i * chunk, chunk), chunk)))
+
+    def add_far(kind, m):
+        def one(at):
+            y_out[kind, m, at] = (sums_far[m][at] + core_in[kind, m, 0, at].astype(F32)).astype(BF)
+
+        chunks(one)
+
+    sums_far = [f_own.at[m] for m in range(MICRO)]
+    oss = (os0, os1)
+
+    def mixed_block(m):
+        def block(r, out):
+            part = mm(oss[m][r * rows:(r + 1) * rows, :], out_w[...])
+            if r == 2:
+                sums_far[m][...] = part
+            else:
+                out[...] = part.astype(out.dtype)
+
+        return block
+
+    hops = [first_hop(0, m, mixed_block(m), nu.at[m]) for m in range(MICRO)]
+    far_hops = []
+    for m in range(MICRO):
+        hops[m][0].wait_recv()
+        add_far(0, m)
+        far_hops.append(remote(y_out.at[0, m], y_in.at[0, m], 2))
+
+    got_fc2.wait()
+
+    def project_grad(m):
+        for r in range(4):
+            got_g[m][r].wait()
+
+        def one(i):
+            r, n = i // parts, i % parts
+            dzc[m, r, :, tile(n)] = mm(gd[m, r], fc2[tile(n), :], NT).astype(BF)
+
+        each(4 * parts, one)
+
+    def own_sum(kind, m, base, at):
+        return base + core_in[kind, m, 1, at].astype(F32) + y_in[kind, m, at].astype(F32)
+
+    def norm_two(m, at, residual):
+        center = residual - jnp.mean(residual, axis=-1, keepdims=True)
+        inverse = lax.rsqrt(jnp.mean(center * center, axis=-1, keepdims=True) + EPSILON)
+        return center * inverse, inverse
+
+    def forward_norms(m):
+        hops[m][1].wait_recv()
+        far_hops[m].wait_recv()
+
+        def one(at):
+            mixed, inverse = norm_two(m, at, own_sum(0, m, nu[m, at], at))
+            nu[m, at] = mixed
+            inv[m, at] = jnp.broadcast_to(inverse, (chunk, 128))
+            residual = x[m, at].astype(F32) + mixed * post[...]
+            normed, _ = norm_two(m, at, residual)
+            full[m, 0, at] = (normed * pre[...]).astype(BF)
+
+        chunks(one)
+
+    def spread(m, buf):
+        return remote(buf.at[m, 0], buf.at[m, 2], 2), remote(buf.at[m, 0], buf.at[m, 1], 1)
+
+    def ffn_forward(m, r):
+        sums[...] = jnp.zeros_like(sums)
+
+        def one(n):
+            value, slope = gelu_parts(mm(full[m, r], fc1[:, tile(n)]))
+            act[m, r, :, tile(n)] = value
+            slz[m, r, :, tile(n)] = slope.astype(BF)
+            dna = dzc[m, r, :, tile(n)].astype(F32) * wide[:, tile(n)]
+            for i, term in enumerate((value, value * value, dna, dna * value)):
+                sums[i] += term[:, 0:128] + term[:, 128:256]
+
+        each(parts, one)
+        lane = lax.broadcasted_iota(jnp.int32, (rows, 128), 1)
+        merged = jnp.zeros((rows, 128), F32)
+        for i in range(4):
+            merged = jnp.where(lane == i, jnp.sum(sums[i], axis=-1, keepdims=True), merged)
+        st_out[m, :, r * rows:(r + 1) * rows] = jnp.transpose(merged)[0:8]
+
+    def send_stats(m):
+        return [remote(st_out.at[m], st_in.at[m, mask - 1], mask) for mask in (1, 2, 3)]
+
+    def ffn_backward_rows(m, r):
+        total = st_out[m, :, r * rows:(r + 1) * rows]
+        for mask in (1, 2, 3):
+            b = r ^ mask
+            total = total + st_in[m, mask - 1, :, b * rows:(b + 1) * rows]
+        cols[0:8, :] = total * (1.0 / FFN)
+        flipped = jnp.transpose(cols[...])
+        mu, square, m_dna, m_cross = [flipped[:, i:i + 1] for i in range(4)]
+        rw = lax.rsqrt(square - mu * mu + EPSILON)
+        m_both = (m_cross - mu * m_dna) * rw
+
+        def one(n):
+            gain = wide[:, tile(n)]
+            dz = dzc[m, r, :, tile(n)].astype(F32)
+            na = (act[m, r, :, tile(n)] - mu) * rw
+            slope = slz[m, r, :, tile(n)].astype(F32)
+            slz[m, r, :, tile(n)] = (na * gain).astype(BF)
+            gains[16:24, tile(n)] += jnp.sum((dz * na).reshape(rows // 8, 8, SEG), axis=0)
+            dzc[m, r, :, tile(n)] = (rw * (dz * gain - m_dna - na * m_both) * slope).astype(BF)
+
+        each(parts, one)
+
+    def grad_block(m):
+        def block(r, out):
+            ffn_backward_rows(m, r)
+            if r == 2:
+                out = sums_far[m]
+
+            def one(n):
+                out[:, tile(n)] = mm(dzc[m, r], fc1[tile(n), :], NT).astype(out.dtype)
+
+            each(model // SEG, one)
+            store(slz.at[m, r], z_hbm.at[m, pl.ds(peers[r] * rows, rows), :])
+            store(dzc.at[m, r], dc_hbm.at[m, pl.ds(r * rows, rows), :])
+
+        return block
+
+    def ffn_out_block(m):
+        def block(r, out):
+            if r == 2:
+                out = sums_far[m]
+
+            def one(n):
+                out[:, tile(n)] = mm(slz[m, r], fc2[:, tile(n)]).astype(out.dtype)
+
+            each(model // SEG, one)
+
+        return block
+
+    def backward_norms(m, hop1, far_hop):
+        hop1.wait_recv()
+        far_hop.wait_recv()
+
+        def one(at):
+            dh2 = own_sum(1, m, dr1[m, at], at)
+            mixed = nu[m, at]
+            residual = x[m, at].astype(F32) + mixed * post[...]
+            normed, inverse = norm_two(m, at, residual)
+            gains[8:16, :] += jnp.sum((dh2 * normed).reshape(chunk // 8, 8, model), axis=0)
+            grad = gd[m, 0, at].astype(F32) + norm_backward(dh2 * pre[...], normed, inverse)
+            gains[0:8, :] += jnp.sum((grad * mixed).reshape(chunk // 8, 8, model), axis=0)
+            dr1[m, at] = grad
+            back = norm_backward(grad * post[...], mixed, inv[m, at][:, 0:1])
+            gd[m, 0, at] = back.astype(BF)
+
+        chunks(one)
+
+    def unmix(m, r):
+        dos[m, r * rows:(r + 1) * rows, :] = mm(gd[m, r], out_w[...], NT)
+
+    project_grad(0)
+    project_grad(1)
+    forward_norms(0)
+    far0, near0 = spread(0, full)
+    got_fc1.wait()
+    ffn_forward(0, 0)
+    near0.wait_recv()
+    ffn_forward(0, 1)
+    forward_norms(1)
+    far1, near1 = spread(1, full)
+    ffn_forward(1, 0)
+    far0.wait_recv()
+    cross0 = remote(full.at[0, 2], full.at[0, 3], 1)
+    ffn_forward(0, 2)
+    cross0.wait_recv()
+    ffn_forward(0, 3)
+    stats0 = send_stats(0)
+    near1.wait_recv()
+    ffn_forward(1, 1)
+    far1.wait_recv()
+    cross1 = remote(full.at[1, 2], full.at[1, 3], 1)
+    ffn_forward(1, 2)
+    for copy in stats0:
+        copy.wait_recv()
+    hop_a = first_hop(1, 0, grad_block(0), dr1.at[0])
+    hop_a[0].wait_recv()
+    add_far(1, 0)
+    far_a = remote(y_out.at[1, 0], y_in.at[1, 0], 2)
+    cross1.wait_recv()
+    ffn_forward(1, 3)
+    stats1 = send_stats(1)
+    for m in range(MICRO):
+        for r in range(4):
+            store(full.at[m, r], h2_hbm.at[m, pl.ds(r * rows, rows), :])
+    for copy in stats1:
+        copy.wait_recv()
+    hop_b = first_hop(1, 1, grad_block(1), dr1.at[1])
+    hop_b[0].wait_recv()
+    add_far(1, 1)
+    far_b = remote(y_out.at[1, 1], y_in.at[1, 1], 2)
+    backward_norms(0, hop_a[1], far_a)
+    du_far0, du_near0 = spread(0, gd)
+
+    for hop in hops:
+        hop[0].wait_send()
+        hop[1].wait_send()
+        pending.remove(hop[0])
+        pending.remove(hop[1])
+
+    def ffn_out(m):
+        hop3, hop1 = first_hop(0, m, ffn_out_block(m), f_far_f32)
+        hop3.wait_recv()
+
+        def one(at):
+            f_far[m, at] = (sums_far[m][at] + core_in[0, m, 0, at].astype(F32)).astype(BF)
+
+        chunks(one)
+        hop1.wait_recv()
+
+        def two(at):
+            residual = x[m, at].astype(F32) + nu[m, at] * post[...]
+            f_own[m, at] = residual + f_far_f32[at] + core_in[0, m, 1, at].astype(F32)
+
+        chunks(two)
+
+    f_far_f32 = act.at[0, 0]
+    ffn_out(0)
+    backward_norms(1, hop_b[1], far_b)
+    du_far1, du_near1 = spread(1, gd)
+    unmix(0, 0)
+    du_near0.wait_recv()
+    unmix(0, 1)
+    du_far0.wait_recv()
+    du_cross0 = remote(gd.at[0, 2], gd.at[0, 3], 1)
+    unmix(0, 2)
+    ffn_out(1)
+    du_cross0.wait_recv()
+    unmix(0, 3)
+    unmix(1, 0)
+    du_near1.wait_recv()
+    unmix(1, 1)
+    for r in range(4):
+        store(gd.at[0, r], du_hbm.at[0, pl.ds(r * rows, rows), :])
+    du_far1.wait_recv()
+    du_cross1 = remote(gd.at[1, 2], gd.at[1, 3], 1)
+    unmix(1, 2)
+    du_cross1.wait_recv()
+    unmix(1, 3)
+    for r in range(4):
+        store(gd.at[1, r], du_hbm.at[1, pl.ds(r * rows, rows), :])
+    for copy in pending:
+        copy.wait_send()
+    for copy in stores:
+        copy.wait()
+
+
+def middle_call(os_pair, x, g, fc1, fc2, out_w, post, pre, wide):
+    micro, rows, model = x.shape
+    hidden = fc1.shape[1]
+    width = out_w.shape[0]
+    tokens = 4 * rows
+    vmem = pl.BlockSpec(memory_space=pltpu.VMEM)
+    big = jax.ShapeDtypeStruct((micro, tokens, hidden), BF)
+    wide_rows = jax.ShapeDtypeStruct((micro, tokens, model), BF)
+    own = jax.ShapeDtypeStruct((micro, rows, model), F32)
+    return pl.pallas_call(
+        middle,
+        out_shape=(
+            big, big, wide_rows, wide_rows,
+            jax.ShapeDtypeStruct((micro, tokens, width), F32),
+            own, own,
+            jax.ShapeDtypeStruct((micro, rows, model), BF),
+            jax.ShapeDtypeStruct((24, model), F32),
+        ),
+        in_specs=[vmem, vmem, vmem, HBM, HBM, HBM, vmem, vmem, vmem, vmem],
+        out_specs=(HBM, HBM, HBM, HBM, vmem, vmem, vmem, vmem, vmem),
+        scratch_shapes=[
+            pltpu.VMEM((model, hidden), BF),
+            pltpu.VMEM((hidden, model), BF),
+            pltpu.VMEM((micro, 4, rows, model), BF),
+            pltpu.VMEM((micro, 4, rows, hidden), F32),
+            pltpu.VMEM((micro, 4, rows, hidden), BF),
+            pltpu.VMEM((micro, 4, rows, hidden), BF),
+            pltpu.VMEM((micro, 4, rows, model), BF),
+            pltpu.VMEM((2, micro, 2, rows, model), BF),
+            pltpu.VMEM((2, micro, 2, rows, model), BF),
+            pltpu.VMEM((2, micro, rows, model), BF),
+            pltpu.VMEM((2, micro, rows, model), BF),
+            pltpu.VMEM((micro, rows, model), F32),
+            pltpu.VMEM((micro, rows, 128), F32),
+            pltpu.VMEM((micro, 8, tokens), F32),
+            pltpu.VMEM((micro, 3, 8, tokens), F32),
+            pltpu.VMEM((4, rows, 128), F32),
+            pltpu.VMEM((128, rows), F32),
+            pltpu.SemaphoreType.DMA((40,)),
+            pltpu.SemaphoreType.DMA((40,)),
+            pltpu.SemaphoreType.DMA((48,)),
+        ],
+        compiler_params=pltpu.CompilerParams(
+            collective_id=0, has_side_effects=True, vmem_limit_bytes=58 << 20
+        ),
+        cost_estimate=pl.CostEstimate(flops=100 * 10**9, transcendentals=0, bytes_accessed=40 << 20),
+        name="middle",
+    )(*os_pair, x, g, fc1, fc2, out_w, post, pre, wide)
+
+
+def finish(
+    bits, dq0, dq1, dk0, dk1, dv0, dv1, full0, full1, x, dr1, weight, pre, mid_gains, head0, head1,
+    din, grad, small_out,
+    piece, inbox, inner, grads, acc, stage, arrived, res, core_out, core_in, y_out, y_in, small, small_in,
+    send, recv, local,
+):
+    shard = lax.axis_index("tensor")
+    index = lax.axis_index("dp")
+    near, far = other(shard, 1), other(shard, 2)
+    rows, model = x.shape[1], x.shape[2]
+    tokens, width = dq0.shape
+    dqs, dks, dvs, fulls = (dq0, dq1), (dk0, dk1), (dv0, dv1), (full0, full1)
+
+    def bit_of(mask):
+        return (index // mask) % 2
+
+    def dp_peer(mask):
+        return {"dp": index + mask - 2 * mask * bit_of(mask)}
+
+    used = [0]
+    pending = []
+
+    def remote(src, dst, target):
+        i = used[0]
+        used[0] += 1
+        copy = pltpu.make_async_remote_copy(
+            src_ref=src, dst_ref=dst, send_sem=send.at[i], recv_sem=recv.at[i],
+            device_id=target, device_id_type=pl.DeviceIdType.MESH,
+        )
+        copy.start()
+        pending.append(copy)
+        return copy
+
+    fetched = [0]
+
+    def fetch(src, dst):
+        i = fetched[0]
+        fetched[0] += 1
+        copy = pltpu.make_async_copy(src, dst, local.at[i])
+        copy.start()
+        return copy
+
+    def each(count, fn):
+        lax.fori_loop(0, count, lambda i, c: (fn(i), c)[1], 0)
+
+    def tile(n):
+        return pl.ds(pl.multiple_of(n * SEG, SEG), SEG)
+
+    barrier = pltpu.get_barrier_semaphore()
+    targets = [{"tensor": near}, {"tensor": far}] + [dp_peer(mask) for mask in bits]
+    for target in targets:
+        pl.semaphore_signal(barrier, inc=1, device_id=target, device_id_type=pl.DeviceIdType.MESH)
+    got = [
+        [fetch(dks[m].at[0], piece.at[m, 0]), fetch(dks[m].at[1], piece.at[m, 1]),
+         fetch(dvs[m].at[0], piece.at[m, 2]), fetch(dvs[m].at[2], piece.at[m, 3])]
+        for m in range(MICRO)
+    ]
+    pl.semaphore_wait(barrier, len(targets))
+
+    def first_sends(m):
+        return [
+            remote(dks[m].at[3], inbox.at[m, 0], dp_peer(2)),
+            remote(dvs[m].at[3], inbox.at[m, 1], dp_peer(1)),
+            remote(dks[m].at[2], inbox.at[m, 2], dp_peer(2)),
+            remote(dvs[m].at[1], inbox.at[m, 3], dp_peer(1)),
+        ]
+
+    def add_rows(out, terms):
+        def one(n):
+            total = terms[0][tile(n), :].astype(F32)
+            for term in terms[1:]:
+                total = total + term[tile(n), :].astype(F32)
+            out[tile(n), :] = total.astype(out.dtype)
+
+        each(tokens // SEG, one)
+
+    def second_sends(m, first):
+        for copy in got[m]:
+            copy.wait()
+        first[0].wait_recv()
+        add_rows(inner.at[m, 0], [piece.at[m, 1], inbox.at[m, 0]])
+        one = remote(inner.at[m, 0], inbox.at[m, 4], dp_peer(1))
+        first[1].wait_recv()
+        add_rows(inner.at[m, 1], [piece.at[m, 3], inbox.at[m, 1]])
+        two = remote(inner.at[m, 1], inbox.at[m, 5], dp_peer(2))
+        return one, two
+
+    def own_sums(m, first, second):
+        first[2].wait_recv()
+        second[0].wait_recv()
+        add_rows(grads.at[m, :, width:2 * width], [piece.at[m, 0], inbox.at[m, 2], inbox.at[m, 4]])
+        first[3].wait_recv()
+        second[1].wait_recv()
+        add_rows(grads.at[m, :, 2 * width:3 * width], [piece.at[m, 2], inbox.at[m, 3], inbox.at[m, 5]])
+
+    def weight_rows(m, kind):
+        cols = slice(kind * width, (kind + 1) * width)
+
+        def one(n):
+            part = mm(fulls[m][:, tile(n)], grads[m, :, cols], TN)
+            acc[kind, tile(n), :] = part if m == 0 else acc[kind, tile(n), :] + part
+
+        each(model // SEG, one)
+
+    def input_rows(m):
+        def block(r, out):
+            def one(n):
+                part = jnp.zeros((rows, SEG), F32)
+                for kind in range(3):
+                    part += mm(
+                        grads[m, r * rows:(r + 1) * rows, kind * width:(kind + 1) * width],
+                        weight[kind, tile(n), :],
+                        NT,
+                    )
+                out[:, tile(n)] = part.astype(out.dtype)
+
+            each(model // SEG, one)
+
+        block(3, core_out.at[m, 0])
+        hop3 = remote(core_out.at[m, 0], core_in.at[m, 0], {"tensor": near})
+        block(1, core_out.at[m, 1])
+        hop1 = remote(core_out.at[m, 1], core_in.at[m, 1], {"tensor": near})
+        block(2, din.at[m])
+        hop3.wait_recv()
+        y_out[m] = (din[m] + core_in[m, 0].astype(F32)).astype(BF)
+        hop = remote(y_out.at[m], y_in.at[m], {"tensor": far})
+        block(0, din.at[m])
+        return hop1, hop
+
+    chunk = 32
+
+    def input_norms(m, hops):
+        hops[0].wait_recv()
+        hops[1].wait_recv()
+
+        def one(i):
+            at = pl.ds(pl.multiple_of(i * chunk, chunk), chunk)
+            dh1 = din[m, at] + core_in[m, 1, at].astype(F32) + y_in[m, at].astype(F32)
+            values = x[m, at].astype(F32)
+            center = values - jnp.mean(values, axis=-1, keepdims=True)
+            inverse = lax.rsqrt(jnp.mean(center * center, axis=-1, keepdims=True) + EPSILON)
+            normed = center * inverse
+            small[0] += jnp.sum((dh1 * normed).reshape(chunk // 8, 8, model), axis=0)
+            din[m, at] = dr1[m, at] + norm_backward(dh1 * pre[...], normed, inverse)
+
+        each(rows // chunk, one)
+
+    class Chain:
+        def __init__(self, kind):
+            self.kind, self.base, self.size, self.at, self.step = kind, 0, model, 0, 0
+            self.copy = None
+
+        def reduce_send(self):
+            mask = bits[self.step]
+            half = self.size // 2
+            out = pl.ds(pl.multiple_of(self.base + (1 - bit_of(mask)) * half, 16), half)
+            slot = pl.ds(self.at, half)
+            stage[self.kind, slot, :] = acc[self.kind, out, :].astype(BF)
+            self.copy = remote(stage.at[self.kind, slot, :], arrived.at[self.kind, slot, :], dp_peer(mask))
+            self.base, self.size = self.base + bit_of(mask) * half, half
+
+        def reduce_wait(self):
+            self.copy.wait_recv()
+            mine = pl.ds(pl.multiple_of(self.base, 16), self.size)
+            total = acc[self.kind, mine, :] + arrived[self.kind, pl.ds(self.at, self.size), :].astype(F32)
+            self.at += self.size
+            self.step += 1
+            if self.step < len(bits):
+                acc[self.kind, mine, :] = total
+            else:
+                res[self.kind, mine, :] = total.astype(BF)
+
+        def gather_send(self):
+            self.step -= 1
+            mask = bits[self.step]
+            mine = pl.ds(pl.multiple_of(self.base, 16), self.size)
+            self.copy = remote(res.at[self.kind, mine, :], res.at[self.kind, mine, :], dp_peer(mask))
+            self.base, self.size = self.base - bit_of(mask) * self.size, 2 * self.size
+
+        def gather_wait(self):
+            self.copy.wait_recv()
+
+    for m in range(MICRO):
+        grads[m, :, 0:width] = dqs[m][...]
+    small[...] = jnp.zeros_like(small)
+    small[1:4] = mid_gains[...].reshape(3, 8, model)
+    small[4, :, 0:width] = head0[...] + head1[...]
+
+    first0 = first_sends(0)
+    weight_rows(0, 0)
+    weight_rows(1, 0)
+    second0 = second_sends(0, first0)
+    first1 = first_sends(1)
+    query = Chain(0)
+    query.reduce_send()
+    own_sums(0, first0, second0)
+    hops0 = input_rows(0)
+    second1 = second_sends(1, first1)
+    weight_rows(0, 1)
+    weight_rows(0, 2)
+    query.reduce_wait()
+    query.reduce_send()
+    input_norms(0, hops0)
+    own_sums(1, first1, second1)
+    weight_rows(1, 1)
+    key = Chain(1)
+    key.reduce_send()
+    weight_rows(1, 2)
+    value = Chain(2)
+    value.reduce_send()
+    hops1 = input_rows(1)
+    query.reduce_wait()
+    chains = [query, key, value]
+    for _ in range(len(bits) - 2):
+        query.reduce_send()
+        query.reduce_wait()
+    query.gather_send()
+    for step in range(len(bits)):
+        for chain in (key, value):
+            chain.reduce_wait()
+            if step + 1 < len(bits):
+                chain.reduce_send()
+        if step == 0:
+            input_norms(1, hops1)
+            totals = jnp.zeros((8, model), F32)
+            place_row = lax.broadcasted_iota(jnp.int32, (8, model), 0)
+            for i in range(5):
+                totals = jnp.where(place_row == i, jnp.sum(small[i], axis=0, keepdims=True), totals)
+            small[0] = totals
+            small_copy = remote(small.at[0], small_in.at[0], {"tensor": near})
+    key.gather_send()
+    value.gather_send()
+    place_row = lax.broadcasted_iota(jnp.int32, (8, model), 0)
+    small_copy.wait_recv()
+    small[1] = small[0] + jnp.where(place_row < 3, small_in[0], 0.0)
+    small_copy = remote(small.at[1], small_in.at[1], {"tensor": far})
+    small_copy.wait_recv()
+    small[2] = small[1] + jnp.where(place_row < 3, small_in[1], 0.0)
+    small_step = [0]
+
+    def small_send():
+        i = small_step[0]
+        return remote(small.at[2 + i], small_in.at[2 + i], dp_peer(bits[i]))
+
+    small_copy = small_send()
+    for step in range(len(bits)):
+        small_copy.wait_recv()
+        small[3 + step] = small[2 + step] + small_in[2 + step]
+        small_step[0] += 1
+        if step + 1 < len(bits):
+            small_copy = small_send()
+        for chain in chains:
+            chain.gather_wait()
+            if step + 1 < len(bits):
+                chain.gather_send()
+    small_out[...] = small[2 + len(bits)]
+
+    def widen(n):
+        for kind in range(3):
+            grad[kind, tile(n), :] = res[kind, tile(n), :].astype(F32)
+
+    each(model // SEG, widen)
+    for copy in pending:
+        copy.wait_send()
+
+
+def finish_call(dqs, dks, dvs, fulls, x, dr1, weight, pre, mid_gains, heads):
+    micro, rows, model = x.shape
+    tokens, width = dqs[0].shape
+    bits = tuple(2**b for b in range(lax.axis_size("dp").bit_length() - 1))
+    vmem = pl.BlockSpec(memory_space=pltpu.VMEM)
+    return pl.pallas_call(
+        partial(finish, bits),
+        out_shape=(
+            jax.ShapeDtypeStruct((micro, rows, model), F32),
+            jax.ShapeDtypeStruct((3, model, width), F32),
+            jax.ShapeDtypeStruct((8, model), F32),
+        ),
+        in_specs=[vmem] * 2 + [HBM] * 4 + [vmem] * 9,
+        out_specs=(vmem,) * 3,
+        scratch_shapes=[
+            pltpu.VMEM((micro, 4, tokens, width), BF),
+            pltpu.VMEM((micro, 6, tokens, width), BF),
+            pltpu.VMEM((micro, 2, tokens, width), BF),
+            pltpu.VMEM((micro, tokens, 3 * width), BF),
+            pltpu.VMEM((3, model, width), F32),
+            pltpu.VMEM((3, model, width), BF),
+            pltpu.VMEM((3, model, width), BF),
+            pltpu.VMEM((3, model, width), BF),
+            pltpu.VMEM((micro, 2, rows, model), BF),
+            pltpu.VMEM((micro, 2, rows, model), BF),
+            pltpu.VMEM((micro, rows, model), BF),
+            pltpu.VMEM((micro, rows, model), BF),
+            pltpu.VMEM((3 + len(bits) + 2, 8, model), F32),
+            pltpu.VMEM((2 + len(bits), 8, model), F32),
+            pltpu.SemaphoreType.DMA((24 + 7 * len(bits),)),
+            pltpu.SemaphoreType.DMA((24 + 7 * len(bits),)),
+            pltpu.SemaphoreType.DMA((8,)),
+        ],
+        compiler_params=pltpu.CompilerParams(
+            collective_id=1, has_side_effects=True, vmem_limit_bytes=56 << 20
+        ),
+        cost_estimate=pl.CostEstimate(flops=60 * 10**9, transcendentals=0, bytes_accessed=30 << 20),
+        name="finish",
+    )(*dqs, *dks, *dvs, *fulls, x, dr1, weight, pre, mid_gains, *heads)
 
 
 def body(
@@ -374,91 +1066,63 @@
         s["keys"] = (own_k, k1, k2, k3)
         s["values"] = (own_v, v1, v2, v3)
         s["q"] = mm(s["full1"], qkv_weight[0]).astype(BF)
-    fc1_grad = fc2_grad = out_grad = wide_gain = 0.0
     for micro, s in enumerate(state):
         s["o"], s["os"], s["lse"] = attention(
             place(micro), parents, s["q"], s["keys"], s["values"], scale_row
         )
-        mixed = scatter_rows(mm(s["os"], out_weight))
-        s["nu"], s["iu"] = normalize(mixed)
-        s["r1"] = s["rows"] + s["nu"] * post_attn_gain
-        s["n2"], s["i2"] = normalize(s["r1"])
-        s["full2"] = gather_rows((s["n2"] * pre_ffn_gain).astype(BF))
-    for micro, s in enumerate(state):
-        grad_all = jnp.concatenate(
-            [
-                lax.dynamic_slice_in_dim(cotangent[micro], (shard ^ r) * row_count, row_count, 0)
-                for r in range(4)
-            ],
-            axis=0,
+    z, dc, h2, du, dos, dr1, f_own, f_far, mid_gains = middle_call(
+        [s["os"] for s in state],
+        block_input,
+        cotangent,
+        fc1_weight,
+        fc2_weight,
+        out_weight,
+        post_attn_gain[None],
+        pre_ffn_gain[None],
+        ffn_norm_gain[None],
+    )
+    over = (((0, 1), (0, 1)), ((), ()))
+    fc1_grad = lax.dot_general(h2, dc, over, preferred_element_type=F32).astype(BF)
+    fc2_grad = lax.dot_general(z, cotangent, over, preferred_element_type=F32).astype(BF)
+    out_grad = lax.dot_general(
+        jnp.stack([s["os"] for s in state]), du, over, preferred_element_type=F32
+    ).astype(BF)
+    early = (fc1_grad, jnp.concatenate([fc2_grad, out_grad], axis=0))
+    early, dos = lax.optimization_barrier((early, dos))
+    early = lax.psum(early, "dp")
+    f_got = swap(f_far, "tensor", 2)
+    outputs = (f_own + f_got.astype(F32)).astype(BF)
+    backs = [
+        attention_grad(
+            place(m), parents, s["q"], dos[m], s["o"], s["lse"], scale_row, s["keys"], s["values"]
         )
-        s["grad_all"] = grad_all
-        s["grad_rows"] = grad_all[0:row_count].astype(F32)
-        act, slope = gelu_parts(mm(s["full2"], fc1_weight))
-        dz = mm(grad_all, fc2_weight, NT)
-        dna = dz * ffn_norm_gain
-        sums = jnp.stack(
-            [jnp.sum(act, -1), jnp.sum(act * act, -1), jnp.sum(dna, -1), jnp.sum(dna * act, -1)]
-        )
-        sums = sum_rows(sums) / FFN
-        mu, square, m_dna, m_cross = [sums[i][:, None] for i in range(4)]
-        rw = lax.rsqrt(square - mu * mu + EPSILON)
-        m_dna_na = (m_cross - mu * m_dna) * rw
-        na = (act - mu) * rw
-        z = (na * ffn_norm_gain).astype(BF)
-        wide_gain = wide_gain + jnp.sum(dz * na, axis=0)
-        dc = (rw * (dna - m_dna - na * m_dna_na) * slope).astype(BF)
-        dh2 = scatter_rows(mm(dc, fc1_weight, NT))
-        s["ffn_rows"] = scatter_rows(mm(z, fc2_weight))
-        fc2_grad = fc2_grad + mm(z, grad_all, TN)
-        fc1_grad = fc1_grad + mm(s["full2"], dc, TN)
-        s["two_gain"] = jnp.sum(dh2 * s["n2"], axis=0)
-        s["dr1"] = s["grad_rows"] + norm_backward(dh2 * pre_ffn_gain, s["n2"], s["i2"])
-        s["post_gain"] = jnp.sum(s["dr1"] * s["nu"], axis=0)
-        du = norm_backward(s["dr1"] * post_attn_gain, s["nu"], s["iu"]).astype(BF)
-        s["du"] = gather_rows(du)
-    ffn_grads = sum_spread(jnp.concatenate([fc1_grad, fc2_grad], axis=0))
-    qkv_grad = 0.0
-    head_grad = 0.0
-    for micro, s in enumerate(state):
-        dos = mm(s["du"], out_weight, NT)
-        out_grad = out_grad + mm(s["os"], s["du"], TN)
-        got = attention_grad(
-            place(micro), parents, s["q"], dos, s["o"], s["lse"], scale_row, s["keys"], s["values"]
-        )
-        dq, dk, dv, sg = got[0], got[1:5], got[5:9], got[9]
-        head_grad = head_grad + sg
-        add = lambda a, b: (a.astype(F32) + b.astype(F32)).astype(BF)
-        k0, k1 = add(dk[0], swap(dk[2], "dp", 2)), add(dk[1], swap(dk[3], "dp", 2))
-        v0, v2 = add(dv[0], swap(dv[1], "dp", 1)), add(dv[2], swap(dv[3], "dp", 1))
-        own_k = add(k0, swap(k1, "dp", 1))
-        own_v = add(v0, swap(v2, "dp", 2))
-        grads = [dq, own_k, own_v]
-        qkv_grad = qkv_grad + jnp.stack([mm(s["full1"], g, TN) for g in grads])
-        dh1 = mm(dq, qkv_weight[0], NT) + mm(own_k, qkv_weight[1], NT) + mm(own_v, qkv_weight[2], NT)
-        dh1 = scatter_rows(dh1)
-        s["one_gain"] = jnp.sum(dh1 * s["n1"], axis=0)
-        s["din"] = s["dr1"] + norm_backward(dh1 * pre_attn_gain, s["n1"], s["i1"])
-    attn_grads = sum_spread(
-        jnp.concatenate([qkv_grad.reshape(-1, 1024), out_grad], axis=0)
+        for m, s in enumerate(state)
+    ]
+    din, qkv_grad, small = finish_call(
+        [b[0] for b in backs],
+        [b[1] for b in backs],
+        [b[2] for b in backs],
+        [s["full1"] for s in state],
+        block_input,
+        dr1,
+        qkv_weight,
+        pre_attn_gain[None],
+        mid_gains,
+        [b[3] for b in backs],
     )
-    gains = jnp.stack([sum(s[k] for s in state) for k in ("one_gain", "post_gain", "two_gain")])
-    gains = sum_small(gains, "tensor")
-    head_row = jnp.sum(head_grad, axis=0).reshape(-1, HEAD_DIM).sum(-1)
-    head_row = jnp.pad(head_row, (0, wide_gain.shape[0] - head_row.shape[0]))
-    small = sum_small(jnp.concatenate([gains, wide_gain[None], head_row[None]], axis=0), "dp")
+    head_grad = small[4, 0:width].reshape(-1, HEAD_DIM).sum(-1)
     return (
-        jnp.stack([(s["r1"] + s["ffn_rows"]).astype(BF) for s in state]),
-        jnp.stack([s["din"] for s in state]),
+        outputs,
+        din,
         small[0],
-        attn_grads[0:3 * width].reshape(qkv_weight.shape),
-        small[4, 0:head_scale.shape[0]],
-        attn_grads[3 * width:],
+        qkv_grad,
+        head_grad,
+        early[1][fc2_weight.shape[0]:].astype(F32),
         small[1],
         small[2],
-        ffn_grads[0:fc1_weight.shape[0]],
+        early[0].astype(F32),
         small[3],
-        ffn_grads[fc1_weight.shape[0]:],
+        early[1][:fc2_weight.shape[0]].astype(F32),
     )
 
 

time: 700 us -> 588 us (0.84)
  Pallas kernels: 87.8 us -> 417 us
  waiting for transfers between devices: 312 us -> 62.1 us
  matrix products: 104 us -> 19.6 us
  starting transfers between devices: 69.9 us -> 21.8 us
  other arithmetic: 62.5 us -> 18.8 us
  local copies, waits for them, and re-layouts: 50 us -> 28 us
  between operations: 3.8 us -> 15.2 us
    pallas_call x2 -> x4, Pallas kernels: 60.2 us -> 393 us  [the longest x1 211 us: finish_call(): pl.pallas_call(partial(finish, bits), out_shape=(jax.ShapeDtypeStruct((mi...]
    ppermute x87 -> x19, waiting for transfers between devices: 312 us -> 62.1 us  [swap(): lax.ppermute(value, axis, [(i, i ^ mask) for i in range(lax.axis_size(axi...]
    dot_general x36 -> x6, matrix products: 104 us -> 4.28 us  [mm(): return lax.dot_general(a, b, dims, preferred_element_type=F32)]
    ppermute x87 -> x19, starting transfers between devices: 69.9 us -> 21.7 us  [swap(): lax.ppermute(value, axis, [(i, i ^ mask) for i in range(lax.axis_size(axi...]
    dynamic_slice x9 -> x0, local copies, waits for them, and re-layouts: 17.6 us -> none  [body(): lax.dynamic_slice_in_dim(cotangent[micro], (shard ^ r) * row_count, row_c...]
    reduce_sum x9 -> x1, other arithmetic: 18 us -> 0.63 us  [body(): head_grad = small[4, 0:width].reshape(-1, HEAD_DIM).sum(-1)]
    unnamed x332 -> x130, local copies, waits for them, and re-layouts: 7.62 us -> 23.8 us
    dot_general x0 -> x3, matrix products: none -> 15.3 us  [the longest x1 8.17 us: body(): lax.dot_general(z, cotangent, over, preferred_element_type=F32).astype(BF)]
  transfers between devices with their start and end apart: 87 -> 20, of which waited for: 34 -> 7; matrix products, arithmetic and copies ran while one was open for 24% -> 5% of each run, Pallas kernels for 13% -> 47%
where the time goes in v2:
time: 588 us; the launch traced here: 583 us
  Pallas kernels  417 us (71%)
  waiting for transfers between devices  62.1 us (11%)
  local copies, waits for them, and re-layouts  28 us (5%)
  starting transfers between devices  21.8 us (4%)
  matrix products  19.6 us (3%)
  other arithmetic  18.8 us (3%)
  between operations  15.2 us (3%)
    pallas_call x1, Pallas kernels, finish_call(): pl.pallas_call(partial(finish, bits), out_shape=(jax.ShapeDtypeStruct((mi...  211 us
    pallas_call x1, Pallas kernels, middle_call(): pl.pallas_call(middle, out_shape=(big, big, wide_rows, wide_rows, jax.Sha...  132 us
    ppermute x19, waiting for transfers between devices, swap(): lax.ppermute(value, axis, [(i, i ^ mask) for i in range(lax.axis_size(axi...  62.1 us
    pallas_call x2, Pallas kernels, attention_grad(): pl.pallas_call(attend_backward, out_shape=(jax.ShapeDtypeStruct((tokens,...  49.6 us
    pallas_call x2, Pallas kernels, attention(): pl.pallas_call(attend_forward, out_shape=(jax.ShapeDtypeStruct((tokens, w...  24.9 us
    unnamed x130, local copies, waits for them, and re-layouts  23.8 us
    ppermute x19, starting transfers between devices, swap(): lax.ppermute(value, axis, [(i, i ^ mask) for i in range(lax.axis_size(axi...  21.7 us
  transfers between devices with their start and end apart: 20, of which 7 were waited for; matrix products, arithmetic and copies ran while one was open for 5% of the time, Pallas kernels for 47%

profile of v2, /device:TPU:0, one launch (start us, length us, event | category | flops | bytes accessed | tf_op | source)
XLA Modules:
  0.0 582.9 jit_solution(2586756945895768896)
XLA Ops:
  7.3 1.5 convert_reduce_fusion
  8.8 1.6 fusion.10
  10.8 3.0 collective-permute-start.1
  13.9 12.7 %collective-permute-done.1 = bf16[256,1024]{1,0:T(8,128)(2,1)S(1)} collective-permute-done((bf16[256,1024]{1,0:T(8,128)(2,1)S(1)}, bf16[256,1024]{1,0:T(8,128)(2,1)S(1)}, u32[]{:S(2)}, u32[]{:S(2)}) %collective-permute-start.1) | collective-permute-done | bytes 524320 | tf_op jit(solution)/shard_map/ppermute | solution.py:31
  27.3 9.7 %collective-permute-done.10 = bf16[256,1024]{1,0:T(8,128)(2,1)S(1)} collective-permute-done((bf16[256,1024]{1,0:T(8,128)(2,1)S(1)}, bf16[256,1024]{1,0:T(8,128)(2,1)S(1)}, u32[]{:S(2)}, u32[]{:S(2)}) %collective-permute-start.10) | collective-permute-done | bytes 524320 | tf_op jit(solution)/shard_map/ppermute | solution.py:31
  37.0 1.2 pad_maximum_fusion.1.full0
  40.6 1.8 collective-permute-start.12
  42.7 1.8 collective-permute-start.7
  44.9 1.7 collective-permute-start.6
  47.3 8.1 %collective-permute-done.12.rest_1_ = bf16[1024,256]{1,0:T(8,128)(2,1)S(1)} collective-permute-done((bf16[1024,256]{1,0:T(8,128)(2,1)S(1)}, bf16[1024,256]{1,0:T(8,128)(2,1)S(1)}, u32[]{:S(2)}, u32[]{:S(2)}) %collective-permute-start.12) | collective-permute-done | bytes 524320 | tf_op jit(solution)/shard_map/ppermute | solution.py:31
  55.4 1.8 collective-permute-start.16
  57.2 9.4 %collective-permute-done.3.rest_1_ = bf16[1024,256]{1,0:T(8,128)(2,1)S(1)} collective-permute-done((bf16[1024,256]{1,0:T(8,128)(2,1)S(1)}, bf16[1024,256]{1,0:T(8,128)(2,1)S(1)}, u32[]{:S(2)}, u32[]{:S(2)}) %collective-permute-start.3) | collective-permute-done | bytes 524320 | tf_op jit(solution)/shard_map/ppermute | solution.py:31
  66.7 1.8 collective-permute-start.5
  68.4 1.5 collective-permute-start.8
  71.4 8.6 %collective-permute-done.16.rest_6_ = bf16[1024,256]{1,0:T(8,128)(2,1)S(1)} collective-permute-done((bf16[1024,256]{1,0:T(8,128)(2,1)S(1)}, bf16[1024,256]{1,0:T(8,128)(2,1)S(1)}, u32[]{:S(2)}, u32[]{:S(2)}) %collective-permute-start.16) | collective-permute-done | bytes 524320 | tf_op jit(solution)/shard_map/ppermute | solution.py:31
  80.0 1.8 collective-permute-start.13
  81.8 1.5 collective-permute-start.15
  83.7 7.5 %collective-permute-done.5.rest_3_ = bf16[1024,256]{1,0:T(8,128)(2,1)S(1)} collective-permute-done((bf16[1024,256]{1,0:T(8,128)(2,1)S(1)}, bf16[1024,256]{1,0:T(8,128)(2,1)S(1)}, u32[]{:S(2)}, u32[]{:S(2)}) %collective-permute-start.5) | collective-permute-done | bytes 524320 | tf_op jit(solution)/shard_map/ppermute | solution.py:31
  91.2 1.7 collective-permute-start.17
  93.0 12.7 %attend_forward.2 = (f32[1024,256]{1,0:T(8,128)S(1)}, bf16[1024,256]{1,0:T(8,128)(2,1)S(1)}, f32[4,8,256]{2,1,0:T(8,128)S(1)}) custom-call(s32[3]{0:T(128)S(1)} %add_add_fusion.place, s32[64]{0:T(128)S(1)} %reshape.52.parents, bf16[1024,256]{1,0:T(8,128)(2,1)S(1)} %convolution_convert_fusion.5.q_ref, ...), custom_call_target="tpu_custom_call" | custom-call | flops 16000000000 | bytes 8388608 | tf_op jit(solution)/shard_map/attend_forward/pallas_call | solution.py:260
  106.5 6.2 %collective-permute-done.14.rest_3_ = bf16[1024,256]{1,0:T(8,128)(2,1)S(1)} collective-permute-done((bf16[1024,256]{1,0:T(8,128)(2,1)S(1)}, bf16[1024,256]{1,0:T(8,128)(2,1)S(1)}, u32[]{:S(2)}, u32[]{:S(2)}) %collective-permute-start.14) | collective-permute-done | bytes 524320 | tf_op jit(solution)/shard_map/ppermute | solution.py:31
  112.8 12.2 %attend_forward.3 = (f32[1024,256]{1,0:T(8,128)S(1)}, bf16[1024,256]{1,0:T(8,128)(2,1)S(1)}, f32[4,8,256]{2,1,0:T(8,128)S(1)}) custom-call(s32[3]{0:T(128)S(1)} %add_add_fusion.1.place, s32[64]{0:T(128)S(1)} %reshape.52.parents, bf16[1024,256]{1,0:T(8,128)(2,1)S(1)} %convolution_convert_fusion.2.q_ref, ...), custom_call_target="tpu_custom_call" | custom-call | flops 16000000000 | bytes 8388608 | tf_op jit(solution)/shard_map/attend_forward/pallas_call | solution.py:260
  126.9 131.9 %middle.1 = (bf16[2,1024,1024]{2,1,0:T(8,128)(2,1)}, bf16[2,1024,1024]{2,1,0:T(8,128)(2,1)}, bf16[2,1024,1024]{2,1,0:T(8,128)(2,1)}, bf16[2,1024,1024]{2,1,0:T(8...) custom-call(bf16[1024,256]{1,0:T(8,128)(2,1)} %copy-done.30, ...), custom_call_target="tpu_custom_call" | custom-call | flops 99999997952 | bytes 41943040 | tf_op jit(solution)/shard_map/middle/pallas_call | solution.py:679
  258.8 1.7 collective-permute-start.18
  260.5 8.2 %bitcast_convert_fusion = bf16[1024,1024]{1,0:T(8,128)(2,1)S(1)} fusion(bf16[2,1024,1024]{2,1,0:T(8,128)(2,1)} %get-tuple-element.46, bf16[2,1024,1024]{2,1,0:T(8,128)(2,1)} %g_hbm.1), kind=kOutput, calls=%fused_computation | convolution fusion | flops 4296015872 | bytes 10485760 | tf_op jit(solution)/shard_map/dot_general | solution.py:1086
  268.7 5.8 %bitcast_convert_fusion.1 = bf16[1024,1024]{1,0:T(8,128)(2,1)} fusion(bf16[2,1024,1024]{2,1,0:T(8,128)(2,1)S(1)} %copy-done.63, bf16[2,1024,1024]{2,1,0:T(8,128)(2,1)S(1)} %copy-done.62), kind=kOutput, calls=%fused_computation.1 | convolution fusion | flops 4296015872 | bytes 10485760 | tf_op jit(solution)/shard_map/dot_general | solution.py:1085
  274.6 1.3 fusion
  275.9 1.7 pad_maximum_fusion
  277.6 1.7 slice_bitcast_fusion
  280.4 1.0 copy-done.13
  284.6 1.2 copy-done.25
  285.7 1.1 copy-done.37
  286.8 1.2 copy-done.41
  288.2 24.9 %attend_backward.2 = (bf16[1024,256]{1,0:T(8,128)(2,1)S(1)}, bf16[4,1024,256]{2,1,0:T(8,128)(2,1)S(1)}, bf16[4,1024,256]{2,1,0:T(8,128)(2,1)S(1)}, f32[8,256]{1,0:T(8,128)S(1)}) custom-call(s32[3]{0:T(128)S(1)} %add_add_fusion.place, s32[64]{0:T(128)S(1)} %reshape.52.parents, bf16[1024,256]{1,0:T(8,128)(2,1)S(1)} %copy-done.37, ...), custom_call_target="tpu_custom_call" | custom-call | flops 35999997952 | bytes 12582912 | tf_op jit(solution)/shard_map/attend_backward/pallas_call | solution.py:295
  313.1 1.3 copy-done.42
  314.4 1.3 copy-done.43
  317.2 24.7 %attend_backward.3 = (bf16[1024,256]{1,0:T(8,128)(2,1)S(1)}, bf16[4,1024,256]{2,1,0:T(8,128)(2,1)S(1)}, bf16[4,1024,256]{2,1,0:T(8,128)(2,1)S(1)}, f32[8,256]{1,0:T(8,128)S(1)}) custom-call(s32[3]{0:T(128)S(1)} %copy-done.1, s32[64]{0:T(128)S(1)} %reshape.52.parents, bf16[1024,256]{1,0:T(8,128)(2,1)S(1)} %copy-done.35, ...), custom_call_target="tpu_custom_call" | custom-call | flops 35999997952 | bytes 12582912 | tf_op jit(solution)/shard_map/attend_backward/pallas_call | solution.py:295
  341.9 1.3 copy-done.44
  343.2 1.3 copy-done.45
  345.9 211.1 %finish.1 = (f32[2,256,1024]{2,1,0:T(8,128)}, f32[3,1024,256]{2,1,0:T(8,128)}, f32[8,1024]{1,0:T(8,128)}) custom-call(bf16[1024,256]{1,0:T(8,128)(2,1)} %copy-done.46, bf16[1024,256]{1,0:T(8,128)(2,1)} %copy-done.47, bf16[4,1024,256]{2,1,0:T(8,128)(2,1)} %copy-done.42, bf16[4,1024,256]{2,1,0:T(8,128)(2,1)} %copy-done.44, bf16[4,1024,256]{2,1,0:T(8,128)(2,1)} %copy-done.43, ...), custom_call_target="tpu_custom_call" | custom-call | flops 60000002048 | bytes 31457280 | tf_op jit(solution)/shard_map/finish/pallas_call | solution.py:991
  558.4 1.5 fusion.29
  559.9 2.5 add_convert_fusion
  562.5 2.1 slice_convert_fusion.1
  564.6 4.2 slice_convert_fusion
  568.8 2.5 convert_element_type.78
  571.3 1.3 copy.33
  572.6 1.3 copy-done.51
  574.0 1.7 copy.34
  (161 shorter events, 18.0 us)
Async XLA Ops:
  7.2 19.9 %copy-start.58 = (s32[2,2,16]{2,1,0:T(2,128)S(1)}, s32[2,2,16]{2,1,0:T(2,128)}, u32[]{:S(2)}) copy-start(s32[2,2,16]{2,1,0:T(2,128)} %param.14) | copy-start | bytes 772
  7.2 20.0 %copy-start.59 = (f32[4]{0:T(128)S(1)}, f32[4]{0:T(128)}, u32[]{:S(2)}) copy-start(f32[4]{0:T(128)} %param.17) | copy-start | bytes 52
  7.2 555.3 %all-reduce.3.cloned.1.call-start = ((), (), s32[]{:S(2)}) async-start(), calls=%async_computation | async-start | bytes 9437184 | tf_op jit(solution)/shard_map/psum | solution.py:1092
  10.8 15.8 %collective-permute-start.1 = (bf16[256,1024]{1,0:T(8,128)(2,1)S(1)}, bf16[256,1024]{1,0:T(8,128)(2,1)S(1)}, u32[]{:S(2)}, u32[]{:S(2)}) collective-permute-start(bf16[256,1024]{1,0:T(8,128)(2,1)S(1)} %get-tuple-element.78), channel_id=1, source_target_pairs={{0,2},{1,3},{2,0},{3,1},{4,6},{5,7},{6,4},{7,5},{8,10},{9,11},{10,... | collective-permute-start | bytes 1572872 | tf_op jit(solution)/shard_map/ppermute | solution.py:31
  13.8 23.2 %collective-permute-start.10 = (bf16[256,1024]{1,0:T(8,128)(2,1)S(1)}, bf16[256,1024]{1,0:T(8,128)(2,1)S(1)}, u32[]{:S(2)}, u32[]{:S(2)}) collective-permute-start(bf16[256,1024]{1,0:T(8,128)(2,1)S(1)} %get-tuple-element.77), channel_id=1, source_target_pairs={{0,2},{1,3},{2,0},{3,1},{4,6},{5,7},{6,4},{7,5},{8,10},{9,11},{10,... | collective-permute-start | bytes 1572872 | tf_op jit(solution)/shard_map/ppermute | solution.py:31
  13.9 23.1 %collective-permute-start = (bf16[256,1024]{1,0:T(8,128)(2,1)S(1)}, bf16[256,1024]{1,0:T(8,128)(2,1)S(1)}, u32[]{:S(2)}, u32[]{:S(2)}) collective-permute-start(bf16[256,1024]{1,0:T(8,128)(2,1)S(1)} %get-tuple-element.78), channel_id=1, source_target_pairs={{0,1},{1,0},{2,3},{3,2},{4,5},{5,4},{6,7},{7,6},{8,9},{9,8},{10,11... | collective-permute-start | bytes 1572872 | tf_op jit(solution)/shard_map/ppermute | solution.py:31
  26.6 10.4 %collective-permute-start.2 = (bf16[256,1024]{1,0:T(8,128)(2,1)S(1)}, bf16[256,1024]{1,0:T(8,128)(2,1)}, u32[]{:S(2)}, u32[]{:S(2)}) collective-permute-start(bf16[256,1024]{1,0:T(8,128)(2,1)S(1)} %collective-permute-done.1), channel_id=1, source_target_pairs={{0,1},{1,0},{2,3},{3,2},{4,5},{5,4},{6,7},{7,6},{8,9},{9,8},{10,11... | collective-permute-start | bytes 1572872 | tf_op jit(solution)/shard_map/ppermute | solution.py:31
  26.6 13.1 %collective-permute-start.9 = (bf16[256,1024]{1,0:T(8,128)(2,1)S(1)}, bf16[256,1024]{1,0:T(8,128)(2,1)S(1)}, u32[]{:S(2)}, u32[]{:S(2)}) collective-permute-start(bf16[256,1024]{1,0:T(8,128)(2,1)S(1)} %get-tuple-element.77), channel_id=1, source_target_pairs={{0,1},{1,0},{2,3},{3,2},{4,5},{5,4},{6,7},{7,6},{8,9},{9,8},{10,11... | collective-permute-start | bytes 1572872 | tf_op jit(solution)/shard_map/ppermute | solution.py:31
  37.0 2.7 collective-permute-start.11
  38.2 32.4 %copy-start.53 = (bf16[1024,1024]{1,0:T(8,128)(2,1)}, bf16[1024,1024]{1,0:T(8,128)(2,1)S(1)}, u32[]{:S(2)}) copy-start(bf16[1024,1024]{1,0:T(8,128)(2,1)S(1)} %pad_maximum_fusion.1.full0) | copy-start | bytes 6291460
  39.9 30.1 %copy-start.54 = (bf16[1024,1024]{1,0:T(8,128)(2,1)}, bf16[1024,1024]{1,0:T(8,128)(2,1)S(1)}, u32[]{:S(2)}) copy-start(bf16[1024,1024]{1,0:T(8,128)(2,1)S(1)} %pad_maximum_fusion.2.full1) | copy-start | bytes 6291460
  40.6 72.1 %copy-start.2 = (bf16[1024,256]{1,0:T(8,128)(2,1)}, bf16[1024,256]{1,0:T(8,128)(2,1)S(1)}, u32[]{:S(2)}) copy-start(bf16[1024,256]{1,0:T(8,128)(2,1)S(1)} %convolution_convert_fusion.1.rest_0_) | copy-start | bytes 1572868
  40.6 14.8 %collective-permute-start.12 = (bf16[1024,256]{1,0:T(8,128)(2,1)S(1)}, bf16[1024,256]{1,0:T(8,128)(2,1)S(1)}, u32[]{:S(2)}, u32[]{:S(2)}) collective-permute-start(bf16[1024,256]{1,0:T(8,128)(2,1)S(1)} %convolution_convert_fusion.1.rest_0_), channel_id=1, source_target_pairs={{0,4},{4,0},{8,12},{12,8},{16,20},{20,16},{24,28},{28,24},{1,5},{5... | collective-permute-start | bytes 1572872 | tf_op jit(solution)/shard_map/ppermute | solution.py:31
  42.4 24.2 %collective-permute-start.3 = (bf16[1024,256]{1,0:T(8,128)(2,1)S(1)}, bf16[1024,256]{1,0:T(8,128)(2,1)S(1)}, u32[]{:S(2)}, u32[]{:S(2)}) collective-permute-start(bf16[1024,256]{1,0:T(8,128)(2,1)S(1)} %convolution_convert_fusion.4.rest_0_), channel_id=1, source_target_pairs={{0,4},{4,0},{8,12},{12,8},{16,20},{20,16},{24,28},{28,24},{1,5},{5... | collective-permute-start | bytes 1572872 | tf_op jit(solution)/shard_map/ppermute | solution.py:31
  42.7 25.7 %collective-permute-start.7 = (bf16[1024,256]{1,0:T(8,128)(2,1)S(1)}, bf16[1024,256]{1,0:T(8,128)(2,1)S(1)}, u32[]{:S(2)}, u32[]{:S(2)}) collective-permute-start(bf16[1024,256]{1,0:T(8,128)(2,1)S(1)} %convolution_convert_fusion.3.rest_4_), channel_id=1, source_target_pairs={{0,8},{4,12},{8,0},{12,4},{16,24},{20,28},{24,16},{28,20},{1,9},{5... | collective-permute-start | bytes 1572872 | tf_op jit(solution)/shard_map/ppermute | solution.py:31
  44.7 68.1 %copy-start = (s32[3]{0:T(128)}, s32[3]{0:T(128)S(1)}, u32[]{:S(2)}) copy-start(s32[3]{0:T(128)S(1)} %add_add_fusion.1.place) | copy-start | bytes 40
  44.7 37.1 %collective-permute-start.4 = (bf16[1024,256]{1,0:T(8,128)(2,1)S(1)}, bf16[1024,256]{1,0:T(8,128)(2,1)S(1)}, u32[]{:S(2)}, u32[]{:S(2)}) collective-permute-start(bf16[1024,256]{1,0:T(8,128)(2,1)S(1)} %convolution_convert_fusion.4.rest_0_), channel_id=1, source_target_pairs={{0,8},{4,12},{8,0},{12,4},{16,24},{20,28},{24,16},{28,20},{1,9},{5... | collective-permute-start | bytes 1572872 | tf_op jit(solution)/shard_map/ppermute | solution.py:31
  44.9 38.4 %collective-permute-start.6 = (bf16[1024,256]{1,0:T(8,128)(2,1)S(1)}, bf16[1024,256]{1,0:T(8,128)(2,1)S(1)}, u32[]{:S(2)}, u32[]{:S(2)}) collective-permute-start(bf16[1024,256]{1,0:T(8,128)(2,1)S(1)} %convolution_convert_fusion.3.rest_4_), channel_id=1, source_target_pairs={{0,4},{4,0},{8,12},{12,8},{16,20},{20,16},{24,28},{28,24},{1,5},{5... | collective-permute-start | bytes 1572872 | tf_op jit(solution)/shard_map/ppermute | solution.py:31
  47.3 65.4 %copy-start.6 = (bf16[1024,256]{1,0:T(8,128)(2,1)}, bf16[1024,256]{1,0:T(8,128)(2,1)S(1)}, u32[]{:S(2)}) copy-start(bf16[1024,256]{1,0:T(8,128)(2,1)S(1)} %convolution_convert_fusion.rest_4_) | copy-start | bytes 1572868
  55.4 57.3 %copy-start.4 = (bf16[1024,256]{1,0:T(8,128)(2,1)}, bf16[1024,256]{1,0:T(8,128)(2,1)S(1)}, u32[]{:S(2)}) copy-start(bf16[1024,256]{1,0:T(8,128)(2,1)S(1)} %collective-permute-done.12.rest_1_) | copy-start | bytes 1572868
  55.4 24.6 %collective-permute-start.16 = (bf16[1024,256]{1,0:T(8,128)(2,1)S(1)}, bf16[1024,256]{1,0:T(8,128)(2,1)S(1)}, u32[]{:S(2)}, u32[]{:S(2)}) collective-permute-start(bf16[1024,256]{1,0:T(8,128)(2,1)S(1)} %convolution_convert_fusion.rest_4_), channel_id=1, source_target_pairs={{0,8},{4,12},{8,0},{12,4},{16,24},{20,28},{24,16},{28,20},{1,9},{5... | collective-permute-start | bytes 1572872 | tf_op jit(solution)/shard_map/ppermute | solution.py:31
  66.6 26.3 %copy-start.8 = (bf16[1024,256]{1,0:T(8,128)(2,1)}, bf16[1024,256]{1,0:T(8,128)(2,1)S(1)}, u32[]{:S(2)}) copy-start(bf16[1024,256]{1,0:T(8,128)(2,1)S(1)} %collective-permute-done.3.rest_1_) | copy-start | bytes 1572868
  66.7 24.6 %collective-permute-start.5 = (bf16[1024,256]{1,0:T(8,128)(2,1)S(1)}, bf16[1024,256]{1,0:T(8,128)(2,1)S(1)}, u32[]{:S(2)}, u32[]{:S(2)}) collective-permute-start(bf16[1024,256]{1,0:T(8,128)(2,1)S(1)} %collective-permute-done.3.rest_1_), channel_id=1, source_target_pairs={{0,8},{4,12},{8,0},{12,4},{16,24},{20,28},{24,16},{28,20},{1,9},{5... | collective-permute-start | bytes 1572872 | tf_op jit(solution)/shard_map/ppermute | solution.py:31
  68.4 24.5 %copy-start.12 = (bf16[1024,256]{1,0:T(8,128)(2,1)}, bf16[1024,256]{1,0:T(8,128)(2,1)S(1)}, u32[]{:S(2)}) copy-start(bf16[1024,256]{1,0:T(8,128)(2,1)S(1)} %collective-permute-done.7.rest_6_) | copy-start | bytes 1572868
  68.4 24.5 %collective-permute-start.8 = (bf16[1024,256]{1,0:T(8,128)(2,1)S(1)}, bf16[1024,256]{1,0:T(8,128)(2,1)S(1)}, u32[]{:S(2)}, u32[]{:S(2)}) collective-permute-start(bf16[1024,256]{1,0:T(8,128)(2,1)S(1)} %collective-permute-done.7.rest_6_), channel_id=1, source_target_pairs={{0,4},{4,0},{8,12},{12,8},{16,20},{20,16},{24,28},{28,24},{1,5},{5... | collective-permute-start | bytes 1572872 | tf_op jit(solution)/shard_map/ppermute | solution.py:31
  70.7 42.1 %copy-start.34 = (bf16[1024,256]{1,0:T(8,128)(2,1)}, bf16[1024,256]{1,0:T(8,128)(2,1)S(1)}, u32[]{:S(2)}) copy-start(bf16[1024,256]{1,0:T(8,128)(2,1)S(1)} %convolution_convert_fusion.2.q_ref) | copy-start | bytes 1572868
  71.4 34.3 %copy-start.36 = (bf16[1024,256]{1,0:T(8,128)(2,1)}, bf16[1024,256]{1,0:T(8,128)(2,1)S(1)}, u32[]{:S(2)}) copy-start(bf16[1024,256]{1,0:T(8,128)(2,1)S(1)} %convolution_convert_fusion.5.q_ref) | copy-start | bytes 1572868
  80.0 32.8 %copy-start.10 = (bf16[1024,256]{1,0:T(8,128)(2,1)}, bf16[1024,256]{1,0:T(8,128)(2,1)S(1)}, u32[]{:S(2)}) copy-start(bf16[1024,256]{1,0:T(8,128)(2,1)S(1)} %collective-permute-done.16.rest_6_) | copy-start | bytes 1572868
  80.0 26.5 %collective-permute-start.13 = (bf16[1024,256]{1,0:T(8,128)(2,1)S(1)}, bf16[1024,256]{1,0:T(8,128)(2,1)S(1)}, u32[]{:S(2)}, u32[]{:S(2)}) collective-permute-start(bf16[1024,256]{1,0:T(8,128)(2,1)S(1)} %convolution_convert_fusion.1.rest_0_), channel_id=1, source_target_pairs={{0,8},{4,12},{8,0},{12,4},{16,24},{20,28},{24,16},{28,20},{1,9},{5... | collective-permute-start | bytes 1572872 | tf_op jit(solution)/shard_map/ppermute | solution.py:31
  81.8 23.9 %copy-start.14 = (bf16[1024,256]{1,0:T(8,128)(2,1)}, bf16[1024,256]{1,0:T(8,128)(2,1)S(1)}, u32[]{:S(2)}) copy-start(bf16[1024,256]{1,0:T(8,128)(2,1)S(1)} %collective-permute-done.4.rest_2_) | copy-start | bytes 1572868
  81.8 24.7 %collective-permute-start.15 = (bf16[1024,256]{1,0:T(8,128)(2,1)S(1)}, bf16[1024,256]{1,0:T(8,128)(2,1)S(1)}, u32[]{:S(2)}, u32[]{:S(2)}) collective-permute-start(bf16[1024,256]{1,0:T(8,128)(2,1)S(1)} %convolution_convert_fusion.rest_4_), channel_id=1, source_target_pairs={{0,4},{4,0},{8,12},{12,8},{16,20},{20,16},{24,28},{28,24},{1,5},{5... | collective-permute-start | bytes 1572872 | tf_op jit(solution)/shard_map/ppermute | solution.py:31
  83.3 22.4 %copy-start.16 = (bf16[1024,256]{1,0:T(8,128)(2,1)}, bf16[1024,256]{1,0:T(8,128)(2,1)S(1)}, u32[]{:S(2)}) copy-start(bf16[1024,256]{1,0:T(8,128)(2,1)S(1)} %collective-permute-done.6.rest_5_) | copy-start | bytes 1572868
  83.3 29.4 %collective-permute-start.14 = (bf16[1024,256]{1,0:T(8,128)(2,1)S(1)}, bf16[1024,256]{1,0:T(8,128)(2,1)S(1)}, u32[]{:S(2)}, u32[]{:S(2)}) collective-permute-start(bf16[1024,256]{1,0:T(8,128)(2,1)S(1)} %collective-permute-done.12.rest_1_), channel_id=1, source_target_pairs={{0,8},{4,12},{8,0},{12,4},{16,24},{20,28},{24,16},{28,20},{1,9},{5... | collective-permute-start | bytes 1572872 | tf_op jit(solution)/shard_map/ppermute | solution.py:31
  91.2 21.5 %collective-permute-start.17 = (bf16[1024,256]{1,0:T(8,128)(2,1)S(1)}, bf16[1024,256]{1,0:T(8,128)(2,1)S(1)}, u32[]{:S(2)}, u32[]{:S(2)}) collective-permute-start(bf16[1024,256]{1,0:T(8,128)(2,1)S(1)} %collective-permute-done.16.rest_6_), channel_id=1, source_target_pairs={{0,4},{4,0},{8,12},{12,8},{16,20},{20,16},{24,28},{28,24},{1,5},{5... | collective-permute-start | bytes 1572872 | tf_op jit(solution)/shard_map/ppermute | solution.py:31
  106.5 18.5 %copy-start.22 = (bf16[1024,256]{1,0:T(8,128)(2,1)}, bf16[1024,256]{1,0:T(8,128)(2,1)S(1)}, u32[]{:S(2)}) copy-start(bf16[1024,256]{1,0:T(8,128)(2,1)S(1)} %collective-permute-done.15.rest_5_) | copy-start | bytes 1572868
  258.8 301.2 %collective-permute-start.18 = (bf16[2,256,1024]{2,1,0:T(8,128)(2,1)}, bf16[2,256,1024]{2,1,0:T(8,128)(2,1)}, u32[]{:S(2)}, u32[]{:S(2)}) collective-permute-start(bf16[2,256,1024]{2,1,0:T(8,128)(2,1)} %get-tuple-element.43), channel_id=1, source_target_pairs={{0,2},{1,3},{2,0},{3,1},{4,6},{5,7},{6,4},{7,5},{8,10},{9,11},{10,... | collective-permute-start | bytes 3145736 | tf_op jit(solution)/shard_map/ppermute | solution.py:31
  288.1 29.0 %copy-start.1 = (s32[3]{0:T(128)S(1)}, s32[3]{0:T(128)}, u32[]{:S(2)}) copy-start(s32[3]{0:T(128)} %copy-done) | copy-start | bytes 40
  288.1 29.0 %copy-start.3 = (bf16[1024,256]{1,0:T(8,128)(2,1)S(1)}, bf16[1024,256]{1,0:T(8,128)(2,1)}, u32[]{:S(2)}) copy-start(bf16[1024,256]{1,0:T(8,128)(2,1)} %copy-done.2) | copy-start | bytes 1572868
  288.1 29.0 %copy-start.5 = (bf16[1024,256]{1,0:T(8,128)(2,1)S(1)}, bf16[1024,256]{1,0:T(8,128)(2,1)}, u32[]{:S(2)}) copy-start(bf16[1024,256]{1,0:T(8,128)(2,1)} %copy-done.4) | copy-start | bytes 1572868
  288.1 29.0 %copy-start.7 = (bf16[1024,256]{1,0:T(8,128)(2,1)S(1)}, bf16[1024,256]{1,0:T(8,128)(2,1)}, u32[]{:S(2)}) copy-start(bf16[1024,256]{1,0:T(8,128)(2,1)} %copy-done.6) | copy-start | bytes 1572868
  288.1 29.0 %copy-start.11 = (bf16[1024,256]{1,0:T(8,128)(2,1)S(1)}, bf16[1024,256]{1,0:T(8,128)(2,1)}, u32[]{:S(2)}) copy-start(bf16[1024,256]{1,0:T(8,128)(2,1)} %copy-done.10) | copy-start | bytes 1572868
  288.1 29.0 %copy-start.19 = (bf16[1024,256]{1,0:T(8,128)(2,1)S(1)}, bf16[1024,256]{1,0:T(8,128)(2,1)}, u32[]{:S(2)}) copy-start(bf16[1024,256]{1,0:T(8,128)(2,1)} %copy-done.18) | copy-start | bytes 1572868
  288.1 29.0 %copy-start.23 = (bf16[1024,256]{1,0:T(8,128)(2,1)S(1)}, bf16[1024,256]{1,0:T(8,128)(2,1)}, u32[]{:S(2)}) copy-start(bf16[1024,256]{1,0:T(8,128)(2,1)} %copy-done.22) | copy-start | bytes 1572868
  288.1 29.0 %copy-start.27 = (bf16[1024,256]{1,0:T(8,128)(2,1)S(1)}, bf16[1024,256]{1,0:T(8,128)(2,1)}, u32[]{:S(2)}) copy-start(bf16[1024,256]{1,0:T(8,128)(2,1)} %copy-done.26) | copy-start | bytes 1572868
  288.1 29.0 %copy-start.29 = (bf16[1024,256]{1,0:T(8,128)(2,1)S(1)}, bf16[1024,256]{1,0:T(8,128)(2,1)}, u32[]{:S(2)}) copy-start(bf16[1024,256]{1,0:T(8,128)(2,1)} %copy-done.28) | copy-start | bytes 1572868
  288.1 29.0 %copy-start.35 = (bf16[1024,256]{1,0:T(8,128)(2,1)S(1)}, bf16[1024,256]{1,0:T(8,128)(2,1)}, u32[]{:S(2)}) copy-start(bf16[1024,256]{1,0:T(8,128)(2,1)} %copy-done.34) | copy-start | bytes 1572868
  288.1 29.0 %copy-start.39 = (f32[1024,256]{1,0:T(8,128)S(1)}, f32[1024,256]{1,0:T(8,128)}, u32[]{:S(2)}) copy-start(f32[1024,256]{1,0:T(8,128)} %copy-done.38) | copy-start | bytes 3145732
  345.9 214.0 %copy-start.55 = (f32[2,256,1024]{2,1,0:T(8,128)S(1)}, f32[2,256,1024]{2,1,0:T(8,128)}, u32[]{:S(2)}) copy-start(f32[2,256,1024]{2,1,0:T(8,128)} %get-tuple-element.42) | copy-start | bytes 6291460
  (36 other events, 169.0 us)
Sparse Core Ops, SparseCore 0:
  279.5 220.6 all-reduce.2

commit v3 on v2

v3 whole, which is shorter than its diff:
```python
from functools import partial

import jax
import jax.numpy as jnp
from jax import lax
from jax.experimental import pallas as pl
from jax.experimental.pallas import tpu as pltpu
from jax.sharding import PartitionSpec as P

HEAD_DIM = 64
FFN = 4096
SEG = 256
SEGS = 16
DEPTH = 5
MICRO = 2

EPSILON = 1e-05
NEGATIVE = -1e30
F32 = jnp.float32
BF = jnp.bfloat16
NN = (((1,), (0,)), ((), ()))
NT = (((1,), (1,)), ((), ()))
TN = (((0,), (0,)), ((), ()))


def mm(a, b, dims=NN):
    return lax.dot_general(a, b, dims, preferred_element_type=F32)


def swap(value, axis, mask):
    return lax.ppermute(value, axis, [(i, i ^ mask) for i in range(lax.axis_size(axis))])


def normalize(values):
    center = values - jnp.mean(values, axis=-1, keepdims=True)
    inverse = lax.rsqrt(jnp.mean(center * center, axis=-1, keepdims=True) + EPSILON)
    return (center * inverse, inverse)


def norm_backward(grad_hat, normed, inverse):
    mean_grad = jnp.mean(grad_hat, axis=-1, keepdims=True)
    mean_cross = jnp.mean(grad_hat * normed, axis=-1, keepdims=True)
    return inverse * (grad_hat - mean_grad - normed * mean_cross)


def climb(parents, base, seg):
    found = []
    current = seg
    count = jnp.int32(0)
    for _ in range(DEPTH):
        up = parents[base + current]
        valid = up >= 0
        count = count + valid.astype(jnp.int32)
        current = jnp.where(valid, up, current)
        found.append(current)
    return count, found


def place_of(seg, per, member, shard):
    return ((seg // per) ^ member) * per + ((seg % per) ^ shard)


def attend_backward(micro, place, parents, q_ref, dos_ref, o_ref, lse_ref, scale_ref, keys, values, *rest):
    dq_ref, dks, dvs, sg_ref = rest[0], rest[1:5], rest[5:9], rest[9]
    key_tree, value_tree, acc, dqt, sems = rest[10:]
    step = pl.program_id(0)
    width = q_ref.shape[1]
    heads = width // HEAD_DIM
    tokens = keys.shape[2]
    per = tokens // SEG
    base, member, shard = place[0], place[1], place[2]

    @pl.when(step == 0)
    def _():
        copies = [
            pltpu.make_async_copy(keys.at[micro], key_tree, sems.at[0]),
            pltpu.make_async_copy(values.at[micro], value_tree, sems.at[1]),
        ]
        for copy in copies:
            copy.start()
        acc[...] = jnp.zeros_like(acc)
        sg_ref[...] = jnp.zeros_like(sg_ref)
        for copy in copies:
            copy.wait()

    dos = dos_ref[...].astype(F32)
    cross = dos * o_ref[...]
    sg_ref[...] += jnp.sum(cross.reshape(SEG // 8, 8, width), axis=0)
    scale = scale_ref[...]
    go = (dos * scale).astype(BF)
    cross_t = jnp.transpose(cross * scale)
    lane = lax.broadcasted_iota(jnp.int32, (SEG, width), 1) // HEAD_DIM
    q = q_ref[...] * BF(HEAD_DIM ** -0.5)
    zero = jnp.zeros_like(q)
    q_heads = [jnp.where(lane == h, q, zero) for h in range(heads)]
    g_heads = [jnp.where(lane == h, go, zero) for h in range(heads)]
    deltas = [
        jnp.sum(cross_t[h * HEAD_DIM:(h + 1) * HEAD_DIM], axis=0, keepdims=True) for h in range(heads)
    ]
    lses = [lse_ref[0, h:h + 1, :] for h in range(heads)]
    dqt[...] = jnp.zeros_like(dqt)

    def block(start, own):
        rows = pl.ds(pl.multiple_of(start, SEG), SEG)
        part = pl.ds(pl.multiple_of(start % tokens, SEG), SEG)
        k = key_tree[start // tokens, part, :]
        v = value_tree[start // tokens, part, :]
        kt = jnp.transpose(k)
        dk = jnp.zeros((SEG, width), F32)
        dv = jnp.zeros((SEG, width), F32)
        for h in range(heads):
            p = jnp.exp(mm(k, q_heads[h], NT) - lses[h])
            if own:
                key_row = lax.broadcasted_iota(jnp.int32, (SEG, SEG), 0)
                query_col = lax.broadcasted_iota(jnp.int32, (SEG, SEG), 1)
                p = jnp.where(key_row <= query_col, p, 0.0)
            dv += mm(p.astype(BF), g_heads[h])
            dp = mm(v, g_heads[h], NT)
            ds = (p * (dp - deltas[h])).astype(BF)
            dk += mm(ds, q_heads[h])
            dqt[pl.ds(h * HEAD_DIM, HEAD_DIM), :] += mm(kt[h * HEAD_DIM:(h + 1) * HEAD_DIM], ds)
        acc[rows, 0:width] += dk
        acc[rows, width:2 * width] += dv

    def upward(j, current):
        up = parents[base + current]
        block(place_of(up, per, member, shard) * SEG, False)
        return up

    seg = member * per + (step ^ shard)
    count, _ = climb(parents, base, seg)
    lax.fori_loop(0, count, upward, seg)
    block(step * SEG, True)
    dq_ref[...] = (jnp.transpose(dqt[...]) * HEAD_DIM ** -0.5).astype(BF)

    @pl.when(step == pl.num_programs(0) - 1)
    def _():
        for r in range(4):
            dks[r][...] = acc[r * tokens:(r + 1) * tokens, 0:width].astype(BF)
            dvs[r][...] = acc[r * tokens:(r + 1) * tokens, width:2 * width].astype(BF)


ROW = lambda i, *s: (i, 0)
FIX = lambda i, *s: (0, 0)
HBM = pl.BlockSpec(memory_space=pl.ANY)


def attention_grad(micro, place, parents, q, dos, o, lse, scale_row, keys, values):
    tokens, width = q.shape
    segs = tokens // SEG
    piece = jax.ShapeDtypeStruct((tokens, width), BF)
    whole = pl.BlockSpec((tokens, width), FIX)
    return pl.pallas_call(
        partial(attend_backward, micro),
        out_shape=(piece,) * 9 + (jax.ShapeDtypeStruct((8, width), F32),),
        grid_spec=pltpu.PrefetchScalarGridSpec(
            num_scalar_prefetch=2,
            grid=(segs,),
            in_specs=[
                pl.BlockSpec((SEG, width), ROW),
                pl.BlockSpec((SEG, width), ROW),
                pl.BlockSpec((SEG, width), ROW),
                pl.BlockSpec((1, 8, SEG), lambda i, *s: (i, 0, 0)),
                pl.BlockSpec((1, width), FIX),
            ]
            + [HBM] * 2,
            out_specs=[pl.BlockSpec((SEG, width), ROW)] + [whole] * 8 + [pl.BlockSpec((8, width), FIX)],
            scratch_shapes=[
                pltpu.VMEM((4, tokens, width), BF),
                pltpu.VMEM((4, tokens, width), BF),
                pltpu.VMEM((4 * tokens, 2 * width), F32),
                pltpu.VMEM((width, SEG), F32),
                pltpu.SemaphoreType.DMA((2,)),
            ],
        ),
        compiler_params=pltpu.CompilerParams(
            dimension_semantics=("arbitrary",), vmem_limit_bytes=61 << 20
        ),
        cost_estimate=pl.CostEstimate(flops=4 * 10**9, transcendentals=0, bytes_accessed=12 << 20),
        name="attend_backward",
    )(place, parents, q, dos, o, lse, scale_row, keys, values)


def gelu_parts(c):
    root = 0.7978845608028654
    square = c * c
    tanh = jnp.tanh(root * (c + 0.044715 * (square * c)))
    act = 0.5 * c * (1.0 + tanh)
    slope = 0.5 * (1.0 + tanh) + 0.5 * c * (1.0 - tanh * tanh) * (root * (1.0 + 3 * 0.044715 * square))
    return act, slope


def other(shard, mask):
    near = shard + 1 - 2 * (shard % 2)
    return {0: shard, 1: near, 2: (shard + 2) % 4, 3: (near + 2) % 4}[mask]


def xor4(a, b):
    return 2 * lax.rem(lax.div(a, 2) + lax.div(b, 2), 2) + lax.rem(a + b, 2)


def opening(
    parents, x, gain, weight, scale_ref, out_w,
    q0, q1, o0, o1, os0, os1, lse0, lse1, mixed, full_hbm, kt_hbm, vt_hbm,
    full, kt0, kt1, vt0, vt1, picked_k, picked_v, core_out, core_in, y_out, y_in, send, recv, local,
):
    shard = lax.axis_index("tensor")
    index = lax.axis_index("dp")
    near, far = {"tensor": other(shard, 1)}, {"tensor": other(shard, 2)}
    beside, beyond = [{"dp": index + mask - 2 * mask * ((index // mask) % 2)} for mask in (1, 2)]
    rows, model = x.shape[1], x.shape[2]
    width = q0.shape[1]
    heads = width // HEAD_DIM
    tokens = 4 * rows
    per = tokens // SEG
    member, tree = index % 4, index // 4
    trees = parents.shape[0] // (MICRO * SEGS)
    qs, os_, oss, lses = (q0, q1), (o0, o1), (os0, os1), (lse0, lse1)
    kts, vts = (kt0, kt1), (vt0, vt1)
    used = [0]
    pending = []

    def remote(src, dst, target):
        i = used[0]
        used[0] += 1
        copy = pltpu.make_async_remote_copy(
            src_ref=src, dst_ref=dst, send_sem=send.at[i], recv_sem=recv.at[i],
            device_id=target, device_id_type=pl.DeviceIdType.MESH,
        )
        copy.start()
        pending.append(copy)
        return copy

    stores = []

    def store(src, dst):
        copy = pltpu.make_async_copy(src, dst, local.at[len(stores)])
        copy.start()
        stores.append(copy)

    def each(count, fn):
        lax.fori_loop(0, count, lambda i, c: (fn(i), c)[1], 0)

    barrier = pltpu.get_barrier_semaphore()
    for target in (near, far, beside, beyond):
        pl.semaphore_signal(barrier, inc=1, device_id=target, device_id_type=pl.DeviceIdType.MESH)

    chunk = 32

    def norms(m):
        def one(i):
            at = pl.ds(pl.multiple_of(i * chunk, chunk), chunk)
            values = x[m, at].astype(F32)
            center = values - jnp.mean(values, axis=-1, keepdims=True)
            inverse = lax.rsqrt(jnp.mean(center * center, axis=-1, keepdims=True) + EPSILON)
            full[m, 0, at] = (center * inverse * gain[...]).astype(BF)

        each(rows // chunk, one)

    def spread(m):
        return remote(full.at[m, 0], full.at[m, 2], far), remote(full.at[m, 0], full.at[m, 1], near)

    def project(m, first):
        for r in (first, first + 1):
            kts[m][r] = mm(full[m, r], weight[1]).astype(BF)
            vts[m][r] = mm(full[m, r], weight[2]).astype(BF)

    def queries(m):
        for r in range(4):
            qs[m][r * rows:(r + 1) * rows, :] = mm(full[m, r], weight[0]).astype(BF)

    def piece(ref, r, half):
        return ref.at[pl.ds(4 * r + 2 * half, 2)]

    def share(m, half):
        k, v = kts[m], vts[m]
        return [
            remote(piece(k, 0, half), piece(k, 1, half), beside),
            remote(piece(v, 0, half), piece(v, 2, half), beyond),
            remote(piece(k, 0, half), piece(k, 2, half), beyond),
            remote(piece(v, 0, half), piece(v, 1, half), beside),
        ]

    def forward(m, half, copies):
        copies[0].wait_recv()
        one = remote(piece(kts[m], 1, half), piece(kts[m], 3, half), beyond)
        copies[1].wait_recv()
        return copies[2:] + [one, remote(piece(vts[m], 2, half), piece(vts[m], 3, half), beside)]

    def settle(*groups):
        for copies in groups:
            for copy in copies:
                copy.wait_recv()

    def attend(m, step):
        seg = member * per + xor4(step, shard)
        count, found = climb(parents, (m * trees + tree) * SEGS, seg)
        past = DEPTH * SEG
        for slot in range(DEPTH):
            s = found[slot]
            at = 4 * xor4(lax.div(s, 4), member) + xor4(lax.rem(s, 4), shard)
            picked_k[slot * SEG:(slot + 1) * SEG, :] = kts[m][at]
            picked_v[slot * SEG:(slot + 1) * SEG, :] = vts[m][at]
        here = pl.ds(pl.multiple_of(step * SEG, SEG), SEG)
        picked_k[past:past + SEG, :] = kts[m][step]
        picked_v[past:past + SEG, :] = vts[m][step]
        lane = lax.broadcasted_iota(jnp.int32, (SEG, width), 1) // HEAD_DIM
        row = lax.broadcasted_iota(jnp.int32, (SEG, SEG), 0)
        col = lax.broadcasted_iota(jnp.int32, (SEG, SEG), 1)
        slot_of = lax.broadcasted_iota(jnp.int32, (1, past), 1) // SEG
        bias = jnp.where(slot_of < count, 0.0, NEGATIVE).astype(F32)
        q = qs[m][here, :] * BF(HEAD_DIM ** -0.5)
        lse_lane = lax.broadcasted_iota(jnp.int32, (SEG, 128), 1)
        lse_all = jnp.zeros((SEG, 128), F32)
        out = jnp.zeros((SEG, width), F32)
        for head in range(heads):
            qh = jnp.where(lane == head, q, jnp.zeros_like(q))
            s_past = mm(qh, picked_k[0:past, :], NT) + bias
            s_own = jnp.where(col <= row, mm(qh, picked_k[past:past + SEG, :], NT), NEGATIVE)
            top = jnp.maximum(
                jnp.max(s_past, axis=1, keepdims=True), jnp.max(s_own, axis=1, keepdims=True)
            )
            p_past = jnp.exp(s_past - top)
            p_own = jnp.exp(s_own - top)
            total = jnp.sum(p_past, axis=1, keepdims=True) + jnp.sum(p_own, axis=1, keepdims=True)
            got = mm(p_past.astype(BF), picked_v[0:past, :]) + mm(p_own.astype(BF), picked_v[past:past + SEG, :])
            out = jnp.where(lane == head, got / total, out)
            lse_all = jnp.where(lse_lane == head, top + jnp.log(total), lse_all)
        os_[m][here, :] = out
        oss[m][here, :] = (out * scale_ref[...]).astype(BF)
        lses[m][pl.ds(step, 1)] = jnp.transpose(lse_all)[0:8].reshape(1, 8, SEG)

    norms(0)
    pl.semaphore_wait(barrier, 4)
    far0, near0 = spread(0)
    norms(1)
    far1, near1 = spread(1)
    near0.wait_recv()
    project(0, 0)
    a0 = share(0, 0)
    near1.wait_recv()
    project(1, 0)
    far0.wait_recv()
    cross0 = remote(full.at[0, 2], full.at[0, 3], near)
    cross0.wait_recv()
    project(0, 2)
    b0 = share(0, 1)
    a0 = forward(0, 0, a0)
    queries(0)
    far1.wait_recv()
    cross1 = remote(full.at[1, 2], full.at[1, 3], near)
    b0 = forward(0, 1, b0)
    a1 = share(1, 0)
    cross1.wait_recv()
    project(1, 2)
    b1 = share(1, 1)
    queries(1)
    for m in range(MICRO):
        store(full.at[m], full_hbm.at[m])
    settle(a0, b0)
    lax.fori_loop(0, 2, lambda i, c: (attend(0, i), c)[1], 0)
    a1 = forward(1, 0, a1)
    lax.fori_loop(2, 4, lambda i, c: (attend(0, i), c)[1], 0)
    b1 = forward(1, 1, b1)

    def mix(r):
        return mm(os0[r * rows:(r + 1) * rows, :], out_w[...])

    core_out[0] = mix(3).astype(BF)
    hop3 = remote(core_out.at[0], core_in.at[0], near)
    core_out[1] = mix(1).astype(BF)
    hop1 = remote(core_out.at[1], core_in.at[1], near)
    mixed[...] = mix(2)
    hop3.wait_recv()
    y_out[...] = (mixed[...] + core_in[0].astype(F32)).astype(BF)
    hop2 = remote(y_out, y_in, far)
    hop1.wait_recv()
    mixed[...] = mix(0) + core_in[1].astype(F32)
    store(kt0, kt_hbm.at[0])
    store(vt0, vt_hbm.at[0])
    settle(a1, b1)
    store(kt1, kt_hbm.at[1])
    store(vt1, vt_hbm.at[1])
    lax.fori_loop(0, 4, lambda i, c: (attend(1, i), c)[1], 0)
    hop2.wait_recv()
    mixed[...] = mixed[...] + y_in[...].astype(F32)
    for copy in pending:
        copy.wait_send()
    for copy in stores:
        copy.wait()


def opening_call(parents, x, gain, weight, scale_row, out_w):
    micro, rows, model = x.shape
    width = weight.shape[2]
    tokens = 4 * rows
    vmem = pl.BlockSpec(memory_space=pltpu.VMEM)
    narrow = jax.ShapeDtypeStruct((tokens, width), BF)
    narrow_wide = jax.ShapeDtypeStruct((tokens, width), F32)
    tops = jax.ShapeDtypeStruct((tokens // SEG, 8, SEG), F32)
    trees = jax.ShapeDtypeStruct((micro, 4 * tokens // SEG, SEG, width), BF)
    return pl.pallas_call(
        opening,
        out_shape=(
            narrow, narrow, narrow_wide, narrow_wide, narrow, narrow, tops, tops,
            jax.ShapeDtypeStruct((rows, model), F32),
            jax.ShapeDtypeStruct((micro, 4, rows, model), BF),
            trees, trees,
        ),
        in_specs=[pl.BlockSpec(memory_space=pltpu.SMEM)] + [vmem] * 5,
        out_specs=(vmem,) * 9 + (HBM,) * 3,
        scratch_shapes=[pltpu.VMEM((micro, 4, rows, model), BF)]
        + [pltpu.VMEM((4 * tokens // SEG, SEG, width), BF)] * 4
        + [pltpu.VMEM(((DEPTH + 1) * SEG, width), BF)] * 2
        + [pltpu.VMEM((2, rows, model), BF)] * 2
        + [pltpu.VMEM((rows, model), BF)] * 2
        + [
            pltpu.SemaphoreType.DMA((36,)),
            pltpu.SemaphoreType.DMA((36,)),
            pltpu.SemaphoreType.DMA((8,)),
        ],
        compiler_params=pltpu.CompilerParams(
            collective_id=2, has_side_effects=True, vmem_limit_bytes=61 << 20
        ),
        cost_estimate=pl.CostEstimate(flops=60 * 10**9, transcendentals=0, bytes_accessed=20 << 20),
        name="opening",
    )(parents, x, gain, weight, scale_row, out_w)


def middle(
    bits, os0, os1, mixed0, x, g_hbm, fc1_hbm, fc2_hbm, out_w, post, pre, wide,
    du_hbm, dos, dr1, f_own, f_far, gains, shares,
    fc1, fc2, gd, du, act, slz, dzc, full, core_out, core_in, y_out, y_in, nu, inv, st_out, st_in, sums, cols,
    arrived, send, recv, local,
):
    shard = lax.axis_index("tensor")
    index = lax.axis_index("dp")

    def bit_of(mask):
        return (index // mask) % 2

    def dp_peer(mask):
        return {"dp": index + mask - 2 * mask * bit_of(mask)}

    peers = [other(shard, k) for k in range(4)]
    rows = x.shape[1]
    model = x.shape[2]
    hidden = fc1.shape[1]
    parts = hidden // SEG
    used = [0]
    pending = []

    def remote(src, dst, target):
        i = used[0]
        used[0] += 1
        if not isinstance(target, dict):
            target = {"tensor": peers[target]}
        copy = pltpu.make_async_remote_copy(
            src_ref=src, dst_ref=dst, send_sem=send.at[i], recv_sem=recv.at[i],
            device_id=target, device_id_type=pl.DeviceIdType.MESH,
        )
        copy.start()
        pending.append(copy)
        return copy

    stored = [0]
    stores = []

    def store(src, dst):
        i = stored[0]
        stored[0] += 1
        copy = pltpu.make_async_copy(src, dst, local.at[i])
        copy.start()
        stores.append(copy)

    def fetch(src, dst):
        i = stored[0]
        stored[0] += 1
        copy = pltpu.make_async_copy(src, dst, local.at[i])
        copy.start()
        return copy

    got_fc2 = fetch(fc2_hbm, fc2)
    got_g = [
        [fetch(g_hbm.at[m, pl.ds(peers[r] * rows, rows), :], gd.at[m, r]) for r in range(4)] for m in range(MICRO)
    ]
    got_fc1 = fetch(fc1_hbm, fc1)
    barrier = pltpu.get_barrier_semaphore()
    targets = [{"tensor": peers[mask]} for mask in (1, 2, 3)] + [dp_peer(mask) for mask in bits]
    for target in targets:
        pl.semaphore_signal(barrier, inc=1, device_id=target, device_id_type=pl.DeviceIdType.MESH)
    pl.semaphore_wait(barrier, len(targets))
    gains[...] = jnp.zeros_like(gains)

    def each(count, fn):
        lax.fori_loop(0, count, lambda i, c: (fn(i), c)[1], 0)

    def tile(n):
        return pl.ds(pl.multiple_of(n * SEG, SEG), SEG)

    def merge(value):
        return value.reshape((-1,) + value.shape[2:])

    def reuse(*groups):
        for copies in groups:
            for copy in copies if isinstance(copies, tuple) else (copies,):
                copy.wait_send()
                pending[:] = [other_copy for other_copy in pending if other_copy is not copy]

    def first_hop(kind, m, block, out):
        block(3, core_out.at[m, 0])
        hop3 = remote(core_out.at[m, 0], core_in.at[kind, m, 0], 1)
        block(1, core_out.at[m, 1])
        hop1 = remote(core_out.at[m, 1], core_in.at[kind, m, 1], 1)
        block(2, None)
        block(0, out)
        return hop3, hop1

    chunk = 32

    def chunks(fn):
        each(rows // chunk, lambda i: fn(pl.ds(pl.multiple_of(i * chunk, chunk), chunk)))

    def add_far(kind, m):
        def one(at):
            y_out[m, at] = (sums_far[m][at] + core_in[kind, m, 0, at].astype(F32)).astype(BF)

        chunks(one)

    sums_far = [f_own.at[m] for m in range(MICRO)]
    def mixed_block():
        def block(r, out):
            part = mm(os1[r * rows:(r + 1) * rows, :], out_w[...])
            if r == 2:
                sums_far[1][...] = part
            else:
                out[...] = part.astype(out.dtype)

        return block

    hops = first_hop(0, 1, mixed_block(), nu.at[1])
    hops[0].wait_recv()
    add_far(0, 1)
    far_hop = remote(y_out.at[1], y_in.at[0, 1], 2)
    def project_grad(m):
        for r in range(4):
            got_g[m][r].wait()

        def one(i):
            r, n = i // parts, i % parts
            dzc[m, pl.ds(pl.multiple_of(r * rows, rows), rows), tile(n)] = mm(gd[m, r], fc2[tile(n), :], NT).astype(BF)

        each(4 * parts, one)

    def own_sum(kind, m, base, at):
        return base + core_in[kind, m, 1, at].astype(F32) + y_in[kind, m, at].astype(F32)

    def norm_two(m, at, residual):
        center = residual - jnp.mean(residual, axis=-1, keepdims=True)
        inverse = lax.rsqrt(jnp.mean(center * center, axis=-1, keepdims=True) + EPSILON)
        return center * inverse, inverse

    def forward_norms(m):
        if m:
            hops[1].wait_recv()
            far_hop.wait_recv()

        def one(at):
            mixed, inverse = norm_two(m, at, own_sum(0, m, nu[m, at], at) if m else mixed0[at, :])
            nu[m, at] = mixed
            inv[m, at] = jnp.broadcast_to(inverse, (chunk, 128))
            residual = x[m, at].astype(F32) + mixed * post[...]
            normed, _ = norm_two(m, at, residual)
            full[m, 0, at] = (normed * pre[...]).astype(BF)

        chunks(one)

    def spread(m, buf):
        return remote(buf.at[m, 0], buf.at[m, 2], 2), remote(buf.at[m, 0], buf.at[m, 1], 1)

    def ffn_forward(m, r):
        sums[...] = jnp.zeros_like(sums)

        def one(n):
            value, slope = gelu_parts(mm(full[m, r], fc1[:, tile(n)]))
            act[m, r * rows:(r + 1) * rows, tile(n)] = value
            slz[m, r, :, tile(n)] = slope.astype(BF)
            dna = dzc[m, pl.ds(pl.multiple_of(r * rows, rows), rows), tile(n)].astype(F32) * wide[:, tile(n)]
            for i, term in enumerate((value, value * value, dna, dna * value)):
                sums[i] += term[:, 0:128] + term[:, 128:256]

        each(parts, one)
        lane = lax.broadcasted_iota(jnp.int32, (rows, 128), 1)
        merged = jnp.zeros((rows, 128), F32)
        for i in range(4):
            merged = jnp.where(lane == i, jnp.sum(sums[i], axis=-1, keepdims=True), merged)
        st_out[m, :, r * rows:(r + 1) * rows] = jnp.transpose(merged)[0:8]

    def send_stats(m):
        return [remote(st_out.at[m], st_in.at[m, mask - 1], mask) for mask in (1, 2, 3)]

    def ffn_backward_rows(m, r):
        total = st_out[m, :, r * rows:(r + 1) * rows]
        for mask in (1, 2, 3):
            b = r ^ mask
            total = total + st_in[m, mask - 1, :, b * rows:(b + 1) * rows]
        cols[0:8, :] = total * (1.0 / FFN)
        flipped = jnp.transpose(cols[...])
        mu, square, m_dna, m_cross = [flipped[:, i:i + 1] for i in range(4)]
        rw = lax.rsqrt(square - mu * mu + EPSILON)
        m_both = (m_cross - mu * m_dna) * rw

        def one(n):
            gain = wide[:, tile(n)]
            dz = dzc[m, pl.ds(pl.multiple_of(r * rows, rows), rows), tile(n)].astype(F32)
            na = (act[m, r * rows:(r + 1) * rows, tile(n)] - mu) * rw
            slope = slz[m, r, :, tile(n)].astype(F32)
            slz[m, r, :, tile(n)] = (na * gain).astype(BF)
            gains[16:24, tile(n)] += jnp.sum((dz * na).reshape(rows // 8, 8, SEG), axis=0)
            dzc[m, pl.ds(pl.multiple_of(r * rows, rows), rows), tile(n)] = (rw * (dz * gain - m_dna - na * m_both) * slope).astype(BF)

        each(parts, one)

    def grad_block(m):
        def block(r, out):
            ffn_backward_rows(m, r)
            if r == 2:
                out = sums_far[m]

            def one(n):
                out[:, tile(n)] = mm(dzc[m, r * rows:(r + 1) * rows, :], fc1[tile(n), :], NT).astype(out.dtype)

            each(model // SEG, one)

        return block

    def ffn_out_block(m):
        def block(r, out):
            def one(n):
                out[:, tile(n)] = mm(slz[m, r], fc2[:, tile(n)]).astype(out.dtype)

            each(model // SEG, one)

        return block

    def backward_norms(m, hop1, far_hop):
        hop1.wait_recv()
        far_hop.wait_recv()

        def one(at):
            dh2 = own_sum(1, m, dr1[m, at], at)
            mixed = nu[m, at]
            residual = x[m, at].astype(F32) + mixed * post[...]
            normed, inverse = norm_two(m, at, residual)
            gains[8:16, :] += jnp.sum((dh2 * normed).reshape(chunk // 8, 8, model), axis=0)
            grad = gd[m, 0, at].astype(F32) + norm_backward(dh2 * pre[...], normed, inverse)
            gains[0:8, :] += jnp.sum((grad * mixed).reshape(chunk // 8, 8, model), axis=0)
            dr1[m, at] = grad
            back = norm_backward(grad * post[...], mixed, inv[m, at][:, 0:1])
            du[m, 0, at] = back.astype(BF)

        chunks(one)

    def unmix(m, r):
        dos[m, r * rows:(r + 1) * rows, :] = mm(du[m, r], out_w[...], NT)

    forward_norms(0)
    far0, near0 = spread(0, full)
    got_fc2.wait()
    project_grad(0)
    got_fc1.wait()
    ffn_forward(0, 0)
    near0.wait_recv()
    ffn_forward(0, 1)
    project_grad(1)
    forward_norms(1)
    far1, near1 = spread(1, full)
    ffn_forward(1, 0)
    far0.wait_recv()
    cross0 = remote(full.at[0, 2], full.at[0, 3], 1)
    ffn_forward(0, 2)
    cross0.wait_recv()
    ffn_forward(0, 3)
    stats0 = send_stats(0)
    near1.wait_recv()
    ffn_forward(1, 1)
    far1.wait_recv()
    cross1 = remote(full.at[1, 2], full.at[1, 3], 1)
    ffn_forward(1, 2)
    for copy in stats0:
        copy.wait_recv()
    hop_a = first_hop(1, 0, grad_block(0), dr1.at[0])
    hop_a[0].wait_recv()
    add_far(1, 0)
    far_a = remote(y_out.at[0], y_in.at[1, 0], 2)
    cross1.wait_recv()
    ffn_forward(1, 3)
    stats1 = send_stats(1)

    def first_grad(m):
        def one(n):
            part = mm(merge(full[m, :, :, tile(n)]), dzc[m], TN)
            act[0, tile(n), :] = part if m == 0 else act[0, tile(n), :] + part

        each(parts, one)

    def second_grad(n):
        part = mm(merge(slz[0, :, :, tile(n)]), merge(gd[0]), TN)
        act[1, tile(n), :] = part + mm(merge(slz[1, :, :, tile(n)]), merge(gd[1]), TN)

    first_grad(0)
    for copy in stats1:
        copy.wait_recv()
    reuse(hops, far_hop)
    hop_b = first_hop(1, 1, grad_block(1), dr1.at[1])
    hop_b[0].wait_recv()
    add_far(1, 1)
    far_b = remote(y_out.at[1], y_in.at[1, 1], 2)
    backward_norms(0, hop_a[1], far_a)
    du_far0, du_near0 = spread(0, du)
    first_grad(1)
    group = hidden // (shares.shape[0] // 2)

    class Chain:
        def __init__(self, number):
            self.number, self.which = number, number // (hidden // group)
            self.start = (number % (hidden // group)) * group
            self.base, self.size, self.at, self.step = self.start, group, self.start, 0

        def send(self):
            mask = bits[self.step]
            half = self.size // 2
            away = self.base + (1 - bit_of(mask)) * half
            where = self.at

            def one(i):
                src = pl.ds(pl.multiple_of(away + i * 16, 16), 16)
                staged[self.which, pl.ds(pl.multiple_of(where + i * 16, 16), 16), :] = act[
                    self.which, src, :
                ].astype(BF)

            each(half // 16, one)
            slot = pl.ds(where, half)
            self.copy = remote(
                staged.at[self.which, slot, :], arrived.at[self.which, slot, :], dp_peer(mask)
            )
            self.base, self.size = self.base + bit_of(mask) * half, half

        def wait(self):
            self.copy.wait_recv()
            self.step += 1
            base, where, last = self.base, self.at, self.step == len(bits)

            def one(i):
                mine = pl.ds(pl.multiple_of(base + i * 16, 16), 16)
                total = act[self.which, mine, :] + arrived[
                    self.which, pl.ds(pl.multiple_of(where + i * 16, 16), 16), :
                ].astype(F32)
                if last:
                    shares[self.number, pl.ds(pl.multiple_of(i * 16, 16), 16), :] = total.astype(BF)
                else:
                    act[self.which, mine, :] = total

            each(self.size // 16, one)
            self.at += self.size

        def go(self):
            self.wait()
            if self.step < len(bits):
                self.send()

    chains = [Chain(i) for i in range(shares.shape[0])]
    half_chains = len(chains) // 2
    staged = dzc
    for chain in chains[:half_chains]:
        chain.send()
    per_chain = parts // half_chains
    for i, chain in enumerate(chains[half_chains:]):
        each(per_chain, lambda n: second_grad(n + i * per_chain))
        chain.send()
    backward_norms(1, hop_b[1], far_b)
    du_far1, du_near1 = spread(1, du)

    def ffn_out(m, hop_old):
        reuse(hop_old, ())
        block = ffn_out_block(m)
        block(3, core_out.at[m, 0])
        hop3 = remote(core_out.at[m, 0], core_in.at[0, m, 0], 1)
        block(1, core_out.at[m, 1])
        hop1 = remote(core_out.at[m, 1], core_in.at[0, m, 1], 1)
        block(2, f_own.at[m])
        hop3.wait_recv()

        def one(at):
            f_far[m, at] = (f_own[m, at] + core_in[0, m, 0, at].astype(F32)).astype(BF)

        chunks(one)
        block(0, f_own.at[m])
        hop1.wait_recv()

        def two(at):
            residual = x[m, at].astype(F32) + nu[m, at] * post[...]
            f_own[m, at] = residual + f_own[m, at] + core_in[0, m, 1, at].astype(F32)

        chunks(two)

    todo = [
        chains[turn - level]
        for turn in range(len(chains) + len(bits) - 1)
        for level in range(len(bits))
        if 0 <= turn - level < len(chains)
    ]

    def advance(count):
        for _ in range(min(count, len(todo))):
            todo.pop(0).go()

    slice_of = -(-len(todo) // 5)
    ffn_out(0, hop_a)
    unmix(0, 0)
    du_near0.wait_recv()
    unmix(0, 1)
    du_far0.wait_recv()
    du_cross0 = remote(du.at[0, 2], du.at[0, 3], 1)
    unmix(0, 2)
    advance(slice_of)
    du_cross0.wait_recv()
    unmix(0, 3)
    ffn_out(1, hop_b)
    advance(slice_of)
    unmix(1, 0)
    du_near1.wait_recv()
    unmix(1, 1)
    for r in range(4):
        store(du.at[0, r], du_hbm.at[0, pl.ds(r * rows, rows), :])
    du_far1.wait_recv()
    du_cross1 = remote(du.at[1, 2], du.at[1, 3], 1)
    unmix(1, 2)
    advance(slice_of)
    du_cross1.wait_recv()
    unmix(1, 3)
    for r in range(4):
        store(du.at[1, r], du_hbm.at[1, pl.ds(r * rows, rows), :])
    advance(len(todo))
    for copy in pending:
        copy.wait_send()
    for copy in stores:
        copy.wait()


def middle_call(os_pair, mixed, x, g, fc1, fc2, out_w, post, pre, wide):
    micro, rows, model = x.shape
    hidden = fc1.shape[1]
    width = out_w.shape[0]
    tokens = 4 * rows
    vmem = pl.BlockSpec(memory_space=pltpu.VMEM)
    wide_rows = jax.ShapeDtypeStruct((micro, tokens, model), BF)
    own = jax.ShapeDtypeStruct((micro, rows, model), F32)
    size = lax.axis_size("dp")
    bits = tuple(2**b for b in range(size.bit_length() - 1))
    group = max(SEG, 16 * size)
    count = 2 * hidden // group
    return pl.pallas_call(
        partial(middle, bits),
        out_shape=(
            wide_rows,
            jax.ShapeDtypeStruct((micro, tokens, width), F32),
            own, own,
            jax.ShapeDtypeStruct((micro, rows, model), BF),
            jax.ShapeDtypeStruct((24, model), F32),
            jax.ShapeDtypeStruct((count, group // size, model), BF),
        ),
        in_specs=[vmem, vmem, vmem, vmem, HBM, HBM, HBM, vmem, vmem, vmem, vmem],
        out_specs=(HBM, vmem, vmem, vmem, vmem, vmem, vmem),
        scratch_shapes=[
            pltpu.VMEM((model, hidden), BF),
            pltpu.VMEM((hidden, model), BF),
            pltpu.VMEM((micro, 4, rows, model), BF),
            pltpu.VMEM((micro, 4, rows, model), BF),
            pltpu.VMEM((micro, tokens, hidden), F32),
            pltpu.VMEM((micro, 4, rows, hidden), BF),
            pltpu.VMEM((micro, tokens, hidden), BF),
            pltpu.VMEM((micro, 4, rows, model), BF),
            pltpu.VMEM((micro, 2, rows, model), BF),
            pltpu.VMEM((2, micro, 2, rows, model), BF),
            pltpu.VMEM((micro, rows, model), BF),
            pltpu.VMEM((2, micro, rows, model), BF),
            pltpu.VMEM((micro, rows, model), F32),
            pltpu.VMEM((micro, rows, 128), F32),
            pltpu.VMEM((micro, 8, tokens), F32),
            pltpu.VMEM((micro, 3, 8, tokens), F32),
            pltpu.VMEM((4, rows, 128), F32),
            pltpu.VMEM((128, rows), F32),
            pltpu.VMEM((2, hidden, model), BF),
            pltpu.SemaphoreType.DMA((40 + count * len(bits),)),
            pltpu.SemaphoreType.DMA((40 + count * len(bits),)),
            pltpu.SemaphoreType.DMA((20,)),
        ],
        compiler_params=pltpu.CompilerParams(
            collective_id=0, has_side_effects=True, vmem_limit_bytes=61 << 20
        ),
        cost_estimate=pl.CostEstimate(flops=100 * 10**9, transcendentals=0, bytes_accessed=40 << 20),
        name="middle",
    )(*os_pair, mixed, x, g, fc1, fc2, out_w, post, pre, wide)


def finish(bits, *refs):
    dq0, dq1, os0, os1, weight, pre, mid_gains, head0, head1 = refs[0:9]
    held, came, dk1, dv1 = refs[9:13], refs[13:17], refs[17:21], refs[21:25]
    full_hbm, du_hbm, x_hbm, dr1_hbm = refs[25:29]
    din, grad, out_grad, small_out = refs[29:33]
    piece, inbox, inner, grads, acc, stage, arrived, res, core_out, core_in, y_out, y_in, small, small_in = refs[33:47]
    full, du, x, dr1, send, recv, local = refs[47:54]
    shard = lax.axis_index("tensor")
    index = lax.axis_index("dp")
    near, far = other(shard, 1), other(shard, 2)
    rows, model = x.shape[1], x.shape[2]
    tokens, width = dq0.shape
    dqs = (dq0, dq1)

    def bit_of(mask):
        return (index // mask) % 2

    def dp_peer(mask):
        return {"dp": index + mask - 2 * mask * bit_of(mask)}

    used = [0]
    pending = []

    def remote(src, dst, target):
        i = used[0]
        used[0] += 1
        copy = pltpu.make_async_remote_copy(
            src_ref=src, dst_ref=dst, send_sem=send.at[i], recv_sem=recv.at[i],
            device_id=target, device_id_type=pl.DeviceIdType.MESH,
        )
        copy.start()
        pending.append(copy)
        return copy

    fetched = [0]

    def fetch(src, dst):
        i = fetched[0]
        fetched[0] += 1
        copy = pltpu.make_async_copy(src, dst, local.at[i])
        copy.start()
        return copy

    def each(count, fn):
        lax.fori_loop(0, count, lambda i, c: (fn(i), c)[1], 0)

    def tile(n):
        return pl.ds(pl.multiple_of(n * SEG, SEG), SEG)

    barrier = pltpu.get_barrier_semaphore()
    targets = [{"tensor": near}, {"tensor": far}] + [dp_peer(mask) for mask in bits]
    for target in targets:
        pl.semaphore_signal(barrier, inc=1, device_id=target, device_id_type=pl.DeviceIdType.MESH)
    mine1 = (dk1[0], dk1[1], dv1[0], dv1[2])
    in_came = [fetch(came[i], inbox.at[0, i]) for i in range(4)]
    got = [[fetch(src, piece.at[0, i]) for i, src in enumerate(held)]]
    in_full = [fetch(full_hbm, full)]
    got.append([fetch(src, piece.at[1, i]) for i, src in enumerate(mine1)])
    in_rest = [fetch(du_hbm, du), fetch(x_hbm, x), fetch(dr1_hbm, dr1)]
    pl.semaphore_wait(barrier, len(targets))

    def first_sends():
        return [
            remote(dk1[3], inbox.at[1, 0], dp_peer(2)),
            remote(dv1[3], inbox.at[1, 1], dp_peer(1)),
            remote(dk1[2], inbox.at[1, 2], dp_peer(2)),
            remote(dv1[1], inbox.at[1, 3], dp_peer(1)),
        ]

    class Here:
        def __init__(self, copy):
            self.copy = copy

        def wait_recv(self):
            self.copy.wait()

    def add_rows(out, terms):
        def one(n):
            total = terms[0][tile(n), :].astype(F32)
            for term in terms[1:]:
                total = total + term[tile(n), :].astype(F32)
            out[tile(n), :] = total.astype(out.dtype)

        each(tokens // SEG, one)

    def second_sends(m, first):
        for copy in got[m]:
            copy.wait()
        first[0].wait_recv()
        add_rows(inner.at[m, 0], [piece.at[m, 1], inbox.at[m, 0]])
        one = remote(inner.at[m, 0], inbox.at[m, 4], dp_peer(1))
        first[1].wait_recv()
        add_rows(inner.at[m, 1], [piece.at[m, 3], inbox.at[m, 1]])
        two = remote(inner.at[m, 1], inbox.at[m, 5], dp_peer(2))
        return one, two

    def own_key(m, first, second):
        first[2].wait_recv()
        second[0].wait_recv()
        add_rows(grads.at[m, :, width:2 * width], [piece.at[m, 0], inbox.at[m, 2], inbox.at[m, 4]])

    def own_value(m, first, second):
        first[3].wait_recv()
        second[1].wait_recv()
        add_rows(grads.at[m, :, 2 * width:3 * width], [piece.at[m, 2], inbox.at[m, 3], inbox.at[m, 5]])

    def out_rows(n):
        acc[3, tile(n), :] = mm(du[0, :, tile(n)], os0[...], TN) + mm(du[1, :, tile(n)], os1[...], TN)

    def weight_rows(m, kind):
        cols = slice(kind * width, (kind + 1) * width)

        def one(n):
            part = mm(full[m, :, tile(n)], grads[m, :, cols], TN)
            acc[kind, tile(n), :] = part if m == 0 else acc[kind, tile(n), :] + part

        each(model // SEG, one)

    def input_rows(m):
        def block(r, out):
            def one(n):
                part = jnp.zeros((rows, SEG), F32)
                for kind in range(3):
                    part += mm(
                        grads[m, r * rows:(r + 1) * rows, kind * width:(kind + 1) * width],
                        weight[kind, tile(n), :],
                        NT,
                    )
                out[:, tile(n)] = part.astype(out.dtype)

            each(model // SEG, one)

        block(3, core_out.at[m, 0])
        hop3 = remote(core_out.at[m, 0], core_in.at[m, 0], {"tensor": near})
        block(1, core_out.at[m, 1])
        hop1 = remote(core_out.at[m, 1], core_in.at[m, 1], {"tensor": near})
        block(2, din.at[m])
        hop3.wait_recv()
        y_out[m] = (din[m] + core_in[m, 0].astype(F32)).astype(BF)
        hop = remote(y_out.at[m], y_in.at[m], {"tensor": far})
        block(0, din.at[m])
        return hop1, hop

    chunk = 32

    def input_norms(m, hops):
        hops[0].wait_recv()
        hops[1].wait_recv()

        def one(i):
            at = pl.ds(pl.multiple_of(i * chunk, chunk), chunk)
            dh1 = din[m, at] + core_in[m, 1, at].astype(F32) + y_in[m, at].astype(F32)
            values = x[m, at].astype(F32)
            center = values - jnp.mean(values, axis=-1, keepdims=True)
            inverse = lax.rsqrt(jnp.mean(center * center, axis=-1, keepdims=True) + EPSILON)
            normed = center * inverse
            small[0] += jnp.sum((dh1 * normed).reshape(chunk // 8, 8, model), axis=0)
            din[m, at] = dr1[m, at] + norm_backward(dh1 * pre[...], normed, inverse)

        each(rows // chunk, one)

    class Chain:
        def __init__(self, kind):
            self.kind, self.base, self.size, self.at, self.step = kind, 0, model, 0, 0
            self.copy, self.back, self.done = None, False, False

        def reduce_send(self):
            mask = bits[self.step]
            half = self.size // 2
            out = pl.ds(pl.multiple_of(self.base + (1 - bit_of(mask)) * half, 16), half)
            slot = pl.ds(self.at, half)
            stage[self.kind, slot, :] = acc[self.kind, out, :].astype(BF)
            self.copy = remote(stage.at[self.kind, slot, :], arrived.at[self.kind, slot, :], dp_peer(mask))
            self.base, self.size = self.base + bit_of(mask) * half, half

        def reduce_wait(self):
            self.copy.wait_recv()
            mine = pl.ds(pl.multiple_of(self.base, 16), self.size)
            total = acc[self.kind, mine, :] + arrived[self.kind, pl.ds(self.at, self.size), :].astype(F32)
            self.at += self.size
            self.step += 1
            if self.step < len(bits):
                acc[self.kind, mine, :] = total
            else:
                res[self.kind, mine, :] = total.astype(BF)

        def gather_send(self):
            self.step -= 1
            mask = bits[self.step]
            mine = pl.ds(pl.multiple_of(self.base, 16), self.size)
            self.copy = remote(res.at[self.kind, mine, :], res.at[self.kind, mine, :], dp_peer(mask))
            self.base, self.size = self.base - bit_of(mask) * self.size, 2 * self.size

        def go(self):
            if self.back:
                self.copy.wait_recv()
                if self.step:
                    self.gather_send()
                else:
                    self.done = True
            else:
                self.reduce_wait()
                if self.step < len(bits):
                    self.reduce_send()
                else:
                    self.back = True
                    self.gather_send()

    for m in range(MICRO):
        grads[m, :, 0:width] = dqs[m][...]
    small[...] = jnp.zeros_like(small)
    small[1:4] = mid_gains[...].reshape(3, 8, model)
    small[4, :, 0:width] = head0[...] + head1[...]

    first0 = [Here(copy) for copy in in_came]
    second0 = second_sends(0, first0)
    first1 = first_sends()
    for copy in in_full:
        copy.wait()
    weight_rows(0, 0)
    weight_rows(1, 0)
    query, mixer, key, value = [Chain(kind) for kind in (0, 3, 1, 2)]
    query.reduce_send()
    for copy in in_rest:
        copy.wait()
    each(model // SEG, out_rows)
    mixer.reduce_send()
    own_key(0, first0, second0)
    own_value(0, first0, second0)
    hops0 = input_rows(0)
    weight_rows(0, 1)
    weight_rows(0, 2)
    second1 = second_sends(1, first1)
    query.go()
    mixer.go()
    input_norms(0, hops0)
    query.go()
    mixer.go()
    own_key(1, first1, second1)
    weight_rows(1, 1)
    key.reduce_send()
    own_value(1, first1, second1)
    weight_rows(1, 2)
    value.reduce_send()
    hops1 = input_rows(1)
    query.go()
    mixer.go()
    key.go()
    value.go()
    query.go()
    mixer.go()
    input_norms(1, hops1)
    totals = jnp.zeros((8, model), F32)
    place_row = lax.broadcasted_iota(jnp.int32, (8, model), 0)
    for i in range(5):
        totals = jnp.where(place_row == i, jnp.sum(small[i], axis=0, keepdims=True), totals)
    small[0] = totals
    small_copy = remote(small.at[0], small_in.at[0], {"tensor": near})
    key.go()
    value.go()
    query.go()
    mixer.go()
    small_copy.wait_recv()
    small[1] = small[0] + jnp.where(place_row < 3, small_in[0], 0.0)
    small_copy = remote(small.at[1], small_in.at[1], {"tensor": far})
    key.go()
    value.go()
    small_copy.wait_recv()
    small[2] = small[1] + jnp.where(place_row < 3, small_in[1], 0.0)
    for step, mask in enumerate(bits):
        small_copy = remote(small.at[2 + step], small_in.at[2 + step], dp_peer(mask))
        for chain in (key, value, query, mixer):
            if not chain.done:
                chain.go()
        small_copy.wait_recv()
        small[3 + step] = small[2 + step] + small_in[2 + step]
    while not (key.done and value.done and query.done and mixer.done):
        for chain in (key, value, query, mixer):
            if not chain.done:
                chain.go()
    small_out[...] = small[2 + len(bits)]

    def widen(n):
        for kind in range(3):
            grad[kind, tile(n), :] = res[kind, tile(n), :].astype(F32)
        out_grad[:, tile(n)] = jnp.transpose(res[3, tile(n), :].astype(F32))

    each(model // SEG, widen)
    for copy in pending:
        copy.wait_send()


def finish_call(dqs, held, came, dk1, dv1, full, os_pair, du, x, dr1, weight, pre, mid_gains, heads):
    micro, rows, model = x.shape
    tokens, width = dqs[0].shape
    bits = tuple(2**b for b in range(lax.axis_size("dp").bit_length() - 1))
    vmem = pl.BlockSpec(memory_space=pltpu.VMEM)
    return pl.pallas_call(
        partial(finish, bits),
        out_shape=(
            jax.ShapeDtypeStruct((micro, rows, model), F32),
            jax.ShapeDtypeStruct((3, model, width), F32),
            jax.ShapeDtypeStruct((width, model), F32),
            jax.ShapeDtypeStruct((8, model), F32),
        ),
        in_specs=[vmem] * 9 + [HBM] * 20,
        out_specs=(vmem,) * 4,
        scratch_shapes=[
            pltpu.VMEM((micro, 4, tokens, width), BF),
            pltpu.VMEM((micro, 6, tokens, width), BF),
            pltpu.VMEM((micro, 2, tokens, width), BF),
            pltpu.VMEM((micro, tokens, 3 * width), BF),
            pltpu.VMEM((4, model, width), F32),
            pltpu.VMEM((4, model, width), BF),
            pltpu.VMEM((4, model, width), BF),
            pltpu.VMEM((4, model, width), BF),
            pltpu.VMEM((micro, 2, rows, model), BF),
            pltpu.VMEM((micro, 2, rows, model), BF),
            pltpu.VMEM((micro, rows, model), BF),
            pltpu.VMEM((micro, rows, model), BF),
            pltpu.VMEM((3 + len(bits) + 2, 8, model), F32),
            pltpu.VMEM((2 + len(bits), 8, model), F32),
            pltpu.VMEM((micro, tokens, model), BF),
            pltpu.VMEM((micro, tokens, model), BF),
            pltpu.VMEM((micro, rows, model), BF),
            pltpu.VMEM((micro, rows, model), F32),
            pltpu.SemaphoreType.DMA((24 + 9 * len(bits),)),
            pltpu.SemaphoreType.DMA((24 + 9 * len(bits),)),
            pltpu.SemaphoreType.DMA((20,)),
        ],
        compiler_params=pltpu.CompilerParams(
            collective_id=1, has_side_effects=True, vmem_limit_bytes=61 << 20
        ),
        cost_estimate=pl.CostEstimate(flops=60 * 10**9, transcendentals=0, bytes_accessed=30 << 20),
        name="finish",
    )(
        *dqs, *os_pair, weight, pre, mid_gains, *heads, *held, *came, *dk1, *dv1, full, du, x, dr1
    )


def body(
    block_input,
    cotangent,
    parent,
    pre_attn_gain,
    qkv_weight,
    head_scale,
    out_weight,
    post_attn_gain,
    pre_ffn_gain,
    fc1_weight,
    ffn_norm_gain,
    fc2_weight,
):
    trees = parent.shape[1]
    group = lax.axis_size("dp") // trees
    member = lax.axis_index("dp") % group
    tree_index = lax.axis_index("dp") // group
    shard = lax.axis_index("tensor")
    row_count = block_input.shape[1]
    tokens = cotangent.shape[1]
    width = qkv_weight.shape[2]
    parents = parent.reshape(-1)
    scale_row = jnp.repeat(head_scale, HEAD_DIM)[None, :]

    def place(micro):
        return jnp.stack([(micro * trees + tree_index) * SEGS, member, shard]).astype(jnp.int32)

    q0, q1, o0, o1, os0, os1, lse0, lse1, mixed, full1, keys, values = opening_call(
        parents, block_input, pre_attn_gain[None], qkv_weight, scale_row, out_weight
    )
    full1 = full1.reshape(MICRO, tokens, -1)
    keys, values = [tree.reshape(MICRO, 4, tokens, width) for tree in (keys, values)]
    du, dos, dr1, f_own, f_far, mid_gains, shares = middle_call(
        (os0, os1),
        mixed,
        block_input,
        cotangent,
        fc1_weight,
        fc2_weight,
        out_weight,
        post_attn_gain[None],
        pre_ffn_gain[None],
        ffn_norm_gain[None],
    )
    count, lines, model = shares.shape
    whole = lax.all_gather(shares, "dp", axis=0)
    f_got = swap(f_far, "tensor", 2)
    outputs = (f_own + f_got.astype(F32)).astype(BF)
    backs = [
        attention_grad(m, place(m), parents, q, dos[m], o, lse, scale_row, keys, values)
        for m, (q, o, lse) in enumerate(((q0, o0, lse0), (q1, o1, lse1)))
    ]
    dk0, dv0 = backs[0][1:5], backs[0][5:9]
    came = (swap(dk0[3], "dp", 2), swap(dv0[3], "dp", 1), swap(dk0[2], "dp", 2), swap(dv0[1], "dp", 1))
    din, qkv_grad, out_grad, small = finish_call(
        [b[0] for b in backs],
        (dk0[0], dk0[1], dv0[0], dv0[2]),
        came,
        backs[1][1:5],
        backs[1][5:9],
        full1,
        (os0, os1),
        du,
        block_input,
        dr1,
        qkv_weight,
        pre_attn_gain[None],
        mid_gains,
        [b[9] for b in backs],
    )
    head_grad = small[4, 0:width].reshape(-1, HEAD_DIM).sum(-1)
    levels = lax.axis_size("dp").bit_length() - 1
    whole = whole.reshape((2,) * levels + (2, count // 2, lines, model))
    whole = jnp.transpose(whole, (levels, levels + 1) + tuple(range(levels))[::-1] + (levels + 2, levels + 3))
    whole = whole.reshape(2, -1, model)
    return (
        outputs,
        din,
        small[0],
        qkv_grad,
        head_grad,
        out_grad,
        small[1],
        small[2],
        whole[0].astype(F32),
        small[3],
        whole[1].astype(F32),
    )


def solution(mesh):
    in_specs = (
        P(None, ("dp", "tensor"), None),
        P(None, "dp", None),
        P(),
        P(),
        P(None, None, "tensor"),
        P("tensor"),
        P("tensor", None),
        P(),
        P(),
        P(None, "tensor"),
        P("tensor"),
        P("tensor", None),
    )
    out_specs = (
        P(None, ("dp", "tensor"), None),
        P(None, ("dp", "tensor"), None),
        P(),
        P(None, None, "tensor"),
        P("tensor"),
        P("tensor", None),
        P(),
        P(),
        P(None, "tensor"),
        P("tensor"),
        P("tensor", None),
    )
    return jax.shard_map(body, mesh=mesh, in_specs=in_specs, out_specs=out_specs, check_vma=False)
```

time: 588 us -> 495 us (0.84)
  waiting for transfers between devices: 62.1 us -> 9.54 us
  matrix products: 19.6 us -> 0 us
  starting transfers between devices: 21.8 us -> 4.16 us
  Pallas kernels: 417 us -> 433 us
  other arithmetic: 18.8 us -> 7.11 us
  local copies, waits for them, and re-layouts: 28 us -> 19.1 us
    pallas_call x5 -> x4, Pallas kernels: 206 us -> 319 us  [the longest x1 154 us: middle_call(): pl.pallas_call(partial(middle, bits), out_shape=(wide_rows, jax.ShapeDtyp...]
    pallas_call x1, Pallas kernels: 211 us -> 114 us  [finish_call(): pl.pallas_call(partial(finish, bits), out_shape=(jax.ShapeDtypeStruct((mi...]
    ppermute x19 -> x5, waiting for transfers between devices: 62.1 us -> 9.52 us  [swap(): lax.ppermute(value, axis, [(i, i ^ mask) for i in range(lax.axis_size(axi...]
    dot_general x9 -> x0, matrix products: 19.6 us -> none  [the longest x1 8.17 us: body(): lax.dot_general(z, cotangent, over, preferred_element_type=F32).astype(BF)]
    ppermute x19 -> x5, starting transfers between devices: 21.7 us -> 4.12 us  [swap(): lax.ppermute(value, axis, [(i, i ^ mask) for i in range(lax.axis_size(axi...]
    unnamed x130 -> x19, local copies, waits for them, and re-layouts: 23.8 us -> 6.55 us
    convert_element_type x4 -> x1, other arithmetic: 9.2 us -> 3.27 us  [body(): whole[1].astype(F32)]
  transfers between devices with their start and end apart: 20 -> 6, of which waited for: 7 -> 1; matrix products, arithmetic and copies ran while one was open for 5% -> 2% of each run, Pallas kernels for 47% -> 38%
where the time goes in v3:
time: 495 us; the launch traced here: 487 us
  Pallas kernels  433 us (87%)
  local copies, waits for them, and re-layouts  19.1 us (4%)
  between operations  14.6 us (3%)
  waiting for transfers between devices  9.54 us (2%)
  other arithmetic  7.11 us (1%)
    pallas_call x1, Pallas kernels, middle_call(): pl.pallas_call(partial(middle, bits), out_shape=(wide_rows, jax.ShapeDtyp...  154 us
    pallas_call x1, Pallas kernels, finish_call(): pl.pallas_call(partial(finish, bits), out_shape=(jax.ShapeDtypeStruct((mi...  114 us
    pallas_call x1, Pallas kernels, opening_call(): pl.pallas_call(opening, out_shape=(narrow, narrow, narrow_wide, narrow_wi...  92.9 us
    pallas_call x2, Pallas kernels, attention_grad(): pl.pallas_call(partial(attend_backward, micro), out_shape=(piece,) * 9 +...  71.8 us
  transfers between devices with their start and end apart: 6, of which 1 were waited for; matrix products, arithmetic and copies ran while one was open for 2% of the time, Pallas kernels for 38%

profile of v3, /device:TPU:0, one launch (start us, length us, event | category | flops | bytes accessed | tf_op | source)
XLA Modules:
  0.0 487.3 jit_solution(10099310640861056062)
XLA Ops:
  7.2 0.0 all-gather.3.cloned.1.call-start
  7.2 1.3 reshape.46.parents
  8.5 0.7 broadcast_in_dim.17
  9.2 0.6 broadcast_in_dim_reshape.3.scale_ref
  9.9 92.9 %opening.1 = (bf16[1024,256]{1,0:T(8,128)(2,1)}, bf16[1024,256]{1,0:T(8,128)(2,1)}, f32[1024,256]{1,0:T(8,128)}, f32[1024,256]{1,0:T(8,128)}, bf16[1024,256]{1,0...) custom-call(s32[64]{0:T(128)} %reshape.46.parents, ...), custom_call_target="tpu_custom_call" | custom-call | flops 60000002048 | bytes 20971520 | tf_op jit(solution)/shard_map/opening/pallas_call | solution.py:402
  102.8 153.8 %middle.1 = (bf16[2,1024,1024]{2,1,0:T(8,128)(2,1)}, f32[2,1024,256]{2,1,0:T(8,128)}, f32[2,256,1024]{2,1,0:T(8,128)}, f32[2,256,1024]{2,1,0:T(8,128)}, bf16[2,2...) custom-call(bf16[1024,256]{1,0:T(8,128)(2,1)} %get-tuple-element.54.os0.refs_2_, ...), custom_call_target="tpu_custom_call" | custom-call | flops 99999997952 | bytes 41943040 | tf_op jit(solution)/shard_map/middle/pallas_call | solution.py:863
  256.6 0.0 all-gather.3.cloned.1.call-update
  256.6 3.0 slice_bitcast_fusion
  259.6 0.7 add_add_fusion
  260.3 34.9 %attend_backward.2 = (bf16[1024,256]{1,0:T(8,128)(2,1)}, bf16[1024,256]{1,0:T(8,128)(2,1)}, bf16[1024,256]{1,0:T(8,128)(2,1)}, bf16[1024,256]{1,0:T(8,128)(2,1)}...) custom-call(s32[3]{0:T(128)} %get-tuple-element.105.place, ...), custom_call_target="tpu_custom_call" | custom-call | flops 4000000000 | bytes 12582912 | tf_op jit(solution)/shard_map/attend_backward/pallas_call | solution.py:153
  295.1 1.8 collective-permute-start.1
  297.0 0.0 collective-permute-start.2
  297.0 0.5 collective-permute-start.3
  297.5 1.8 collective-permute-start.4
  299.3 0.0 collective-permute-start
  299.3 37.0 %attend_backward.3 = (bf16[1024,256]{1,0:T(8,128)(2,1)}, bf16[1024,256]{1,0:T(8,128)(2,1)}, bf16[1024,256]{1,0:T(8,128)(2,1)}, bf16[1024,256]{1,0:T(8,128)(2,1)}...) custom-call(s32[3]{0:T(128)} %get-tuple-element.106.place, ...), custom_call_target="tpu_custom_call" | custom-call | flops 4000000000 | bytes 12582912 | tf_op jit(solution)/shard_map/attend_backward/pallas_call | solution.py:153
  336.2 0.0 collective-permute-done.1.refs_13_
  336.2 0.0 copy-start.4
  336.3 0.0 collective-permute-done.2.refs_14_
  336.3 0.0 copy-start.5
  336.3 9.5 %collective-permute-done.3.refs_15_ = bf16[1024,256]{1,0:T(8,128)(2,1)S(1)} collective-permute-done((bf16[1024,256]{1,0:T(8,128)(2,1)}, bf16[1024,256]{1,0:T(8,128)(2,1)S(1)}, u32[]{:S(2)}, u32[]{:S(2)}) %collective-permute-start.3) | collective-permute-done | bytes 524320 | tf_op jit(solution)/shard_map/ppermute | solution.py:31
  345.8 0.0 copy-start.6
  345.8 0.0 collective-permute-done.4.refs_16_
  345.8 0.0 copy-start.7
  345.8 0.0 copy-done.5
  345.8 0.8 copy-done.6
  346.6 0.2 copy-done.7
  346.8 0.0 copy-done.4
  346.8 0.0 copy-start.1
  346.8 114.2 %finish.1 = (f32[2,256,1024]{2,1,0:T(8,128)}, f32[3,1024,256]{2,1,0:T(8,128)}, f32[256,1024]{1,0:T(8,128)}, f32[8,1024]{1,0:T(8,128)}) custom-call(bf16[1024,256]{1,0:T(8,128)(2,1)} %get-tuple-element.65.refs_0_, bf16[1024,256]{1,0:T(8,128)(2,1)} %get-tuple-element.69.refs_1_, bf16[1024,256]{1,0:T(8,128)(2,1)} %get-tuple-element.54.os0.refs_2_, ...), custom_call_target="tpu_custom_call" | custom-call | flops 60000002048 | bytes 31457280 | tf_op jit(solution)/shard_map/finish/pallas_call | solution.py:1204
  461.0 0.7 slice_reduce_fusion
  461.7 0.1 reshape_squeeze.3
  461.8 0.6 reduce_sum.9
  462.4 1.5 fusion
  463.9 0.0 collective-permute-done
  463.9 0.0 copy-done.1
  463.9 2.5 add_convert_fusion
  466.5 0.0 all-gather.3.cloned.1.call-done
  466.5 3.3 slice_convert_fusion
  469.8 2.3 copy.25
  472.1 0.0 copy-start.2
  472.1 2.3 copy.26
  474.4 0.0 copy-done.2
  474.4 1.3 copy.30
  475.7 1.3 copy-done
  477.1 1.7 copy.31
  478.7 0.3 copy-done.3
  479.0 1.0 copy.32
  (2 shorter events, 0.0 us)
Async XLA Ops:
  7.2 459.3 %all-gather.3.cloned.1.call-start = ((), (), s32[]{:S(2)}) async-start(), calls=%async_computation | async-start | bytes 4718592 | tf_op jit(solution)/shard_map/all_gather | solution.py:1293
  295.1 41.1 %collective-permute-start.1 = (bf16[1024,256]{1,0:T(8,128)(2,1)}, bf16[1024,256]{1,0:T(8,128)(2,1)S(1)}, u32[]{:S(2)}, u32[]{:S(2)}) collective-permute-start(bf16[1024,256]{1,0:T(8,128)(2,1)} %get-tuple-element.77), channel_id=1, source_target_pairs={{0,8},{4,12},{8,0},{12,4},{16,24},{20,28},{24,16},{28,20},{1,9},{5... | collective-permute-start | bytes 1572872 | tf_op jit(solution)/shard_map/ppermute | solution.py:31
  297.0 39.3 %collective-permute-start.2 = (bf16[1024,256]{1,0:T(8,128)(2,1)}, bf16[1024,256]{1,0:T(8,128)(2,1)S(1)}, u32[]{:S(2)}, u32[]{:S(2)}) collective-permute-start(bf16[1024,256]{1,0:T(8,128)(2,1)} %get-tuple-element.78), channel_id=1, source_target_pairs={{0,4},{4,0},{8,12},{12,8},{16,20},{20,16},{24,28},{28,24},{1,5},{5... | collective-permute-start | bytes 1572872 | tf_op jit(solution)/shard_map/ppermute | solution.py:31
  297.0 48.8 %collective-permute-start.3 = (bf16[1024,256]{1,0:T(8,128)(2,1)}, bf16[1024,256]{1,0:T(8,128)(2,1)S(1)}, u32[]{:S(2)}, u32[]{:S(2)}) collective-permute-start(bf16[1024,256]{1,0:T(8,128)(2,1)} %get-tuple-element.79), channel_id=1, source_target_pairs={{0,8},{4,12},{8,0},{12,4},{16,24},{20,28},{24,16},{28,20},{1,9},{5... | collective-permute-start | bytes 1572872 | tf_op jit(solution)/shard_map/ppermute | solution.py:31
  297.5 48.3 %collective-permute-start.4 = (bf16[1024,256]{1,0:T(8,128)(2,1)}, bf16[1024,256]{1,0:T(8,128)(2,1)S(1)}, u32[]{:S(2)}, u32[]{:S(2)}) collective-permute-start(bf16[1024,256]{1,0:T(8,128)(2,1)} %get-tuple-element.80), channel_id=1, source_target_pairs={{0,4},{4,0},{8,12},{12,8},{16,20},{20,16},{24,28},{28,24},{1,5},{5... | collective-permute-start | bytes 1572872 | tf_op jit(solution)/shard_map/ppermute | solution.py:31
  299.3 164.7 %collective-permute-start = (bf16[2,256,1024]{2,1,0:T(8,128)(2,1)}, bf16[2,256,1024]{2,1,0:T(8,128)(2,1)}, u32[]{:S(2)}, u32[]{:S(2)}) collective-permute-start(bf16[2,256,1024]{2,1,0:T(8,128)(2,1)} %get-tuple-element.58), channel_id=1, source_target_pairs={{0,2},{1,3},{2,0},{3,1},{4,6},{5,7},{6,4},{7,5},{8,10},{9,11},{10,... | collective-permute-start | bytes 3145736 | tf_op jit(solution)/shard_map/ppermute | solution.py:31
  336.2 10.5 %copy-start.4 = (bf16[1024,256]{1,0:T(8,128)(2,1)}, bf16[1024,256]{1,0:T(8,128)(2,1)S(1)}, u32[]{:S(2)}) copy-start(bf16[1024,256]{1,0:T(8,128)(2,1)S(1)} %collective-permute-done.1.refs_13_) | copy-start | bytes 1572868
  336.3 9.5 %copy-start.5 = (bf16[1024,256]{1,0:T(8,128)(2,1)}, bf16[1024,256]{1,0:T(8,128)(2,1)S(1)}, u32[]{:S(2)}) copy-start(bf16[1024,256]{1,0:T(8,128)(2,1)S(1)} %collective-permute-done.2.refs_14_) | copy-start | bytes 1572868
  345.8 0.8 copy-start.6
  345.8 1.0 copy-start.7
  346.8 117.2 %copy-start.1 = (f32[2,256,1024]{2,1,0:T(8,128)S(1)}, f32[2,256,1024]{2,1,0:T(8,128)}, u32[]{:S(2)}) copy-start(f32[2,256,1024]{2,1,0:T(8,128)} %get-tuple-element.57) | copy-start | bytes 6291460
  472.1 2.3 copy-start.2
  474.4 2.7 copy-start
  477.1 2.0 copy-start.3
Sparse Core Ops, SparseCore 0:
  256.7 89.6 all-gather.2

commit v4 on v3

--- a/solution.py
+++ b/solution.py
@@ -56,129 +56,7 @@
     return count, found
 
 
-def place_of(seg, per, member, shard):
-    return ((seg // per) ^ member) * per + ((seg % per) ^ shard)
-
-
-def attend_backward(micro, place, parents, q_ref, dos_ref, o_ref, lse_ref, scale_ref, keys, values, *rest):
-    dq_ref, dks, dvs, sg_ref = rest[0], rest[1:5], rest[5:9], rest[9]
-    key_tree, value_tree, acc, dqt, sems = rest[10:]
-    step = pl.program_id(0)
-    width = q_ref.shape[1]
-    heads = width // HEAD_DIM
-    tokens = keys.shape[2]
-    per = tokens // SEG
-    base, member, shard = place[0], place[1], place[2]
-
-    @pl.when(step == 0)
-    def _():
-        copies = [
-            pltpu.make_async_copy(keys.at[micro], key_tree, sems.at[0]),
-            pltpu.make_async_copy(values.at[micro], value_tree, sems.at[1]),
-        ]
-        for copy in copies:
-            copy.start()
-        acc[...] = jnp.zeros_like(acc)
-        sg_ref[...] = jnp.zeros_like(sg_ref)
-        for copy in copies:
-            copy.wait()
-
-    dos = dos_ref[...].astype(F32)
-    cross = dos * o_ref[...]
-    sg_ref[...] += jnp.sum(cross.reshape(SEG // 8, 8, width), axis=0)
-    scale = scale_ref[...]
-    go = (dos * scale).astype(BF)
-    cross_t = jnp.transpose(cross * scale)
-    lane = lax.broadcasted_iota(jnp.int32, (SEG, width), 1) // HEAD_DIM
-    q = q_ref[...] * BF(HEAD_DIM ** -0.5)
-    zero = jnp.zeros_like(q)
-    q_heads = [jnp.where(lane == h, q, zero) for h in range(heads)]
-    g_heads = [jnp.where(lane == h, go, zero) for h in range(heads)]
-    deltas = [
-        jnp.sum(cross_t[h * HEAD_DIM:(h + 1) * HEAD_DIM], axis=0, keepdims=True) for h in range(heads)
-    ]
-    lses = [lse_ref[0, h:h + 1, :] for h in range(heads)]
-    dqt[...] = jnp.zeros_like(dqt)
-
-    def block(start, own):
-        rows = pl.ds(pl.multiple_of(start, SEG), SEG)
-        part = pl.ds(pl.multiple_of(start % tokens, SEG), SEG)
-        k = key_tree[start // tokens, part, :]
-        v = value_tree[start // tokens, part, :]
-        kt = jnp.transpose(k)
-        dk = jnp.zeros((SEG, width), F32)
-        dv = jnp.zeros((SEG, width), F32)
-        for h in range(heads):
-            p = jnp.exp(mm(k, q_heads[h], NT) - lses[h])
-            if own:
-                key_row = lax.broadcasted_iota(jnp.int32, (SEG, SEG), 0)
-                query_col = lax.broadcasted_iota(jnp.int32, (SEG, SEG), 1)
-                p = jnp.where(key_row <= query_col, p, 0.0)
-            dv += mm(p.astype(BF), g_heads[h])
-            dp = mm(v, g_heads[h], NT)
-            ds = (p * (dp - deltas[h])).astype(BF)
-            dk += mm(ds, q_heads[h])
-            dqt[pl.ds(h * HEAD_DIM, HEAD_DIM), :] += mm(kt[h * HEAD_DIM:(h + 1) * HEAD_DIM], ds)
-        acc[rows, 0:width] += dk
-        acc[rows, width:2 * width] += dv
-
-    def upward(j, current):
-        up = parents[base + current]
-        block(place_of(up, per, member, shard) * SEG, False)
-        return up
-
-    seg = member * per + (step ^ shard)
-    count, _ = climb(parents, base, seg)
-    lax.fori_loop(0, count, upward, seg)
-    block(step * SEG, True)
-    dq_ref[...] = (jnp.transpose(dqt[...]) * HEAD_DIM ** -0.5).astype(BF)
-
-    @pl.when(step == pl.num_programs(0) - 1)
-    def _():
-        for r in range(4):
-            dks[r][...] = acc[r * tokens:(r + 1) * tokens, 0:width].astype(BF)
-            dvs[r][...] = acc[r * tokens:(r + 1) * tokens, width:2 * width].astype(BF)
-
-
-ROW = lambda i, *s: (i, 0)
-FIX = lambda i, *s: (0, 0)
 HBM = pl.BlockSpec(memory_space=pl.ANY)
-
-
-def attention_grad(micro, place, parents, q, dos, o, lse, scale_row, keys, values):
-    tokens, width = q.shape
-    segs = tokens // SEG
-    piece = jax.ShapeDtypeStruct((tokens, width), BF)
-    whole = pl.BlockSpec((tokens, width), FIX)
-    return pl.pallas_call(
-        partial(attend_backward, micro),
-        out_shape=(piece,) * 9 + (jax.ShapeDtypeStruct((8, width), F32),),
-        grid_spec=pltpu.PrefetchScalarGridSpec(
-            num_scalar_prefetch=2,
-            grid=(segs,),
-            in_specs=[
-                pl.BlockSpec((SEG, width), ROW),
-                pl.BlockSpec((SEG, width), ROW),
-                pl.BlockSpec((SEG, width), ROW),
-                pl.BlockSpec((1, 8, SEG), lambda i, *s: (i, 0, 0)),
-                pl.BlockSpec((1, width), FIX),
-            ]
-            + [HBM] * 2,
-            out_specs=[pl.BlockSpec((SEG, width), ROW)] + [whole] * 8 + [pl.BlockSpec((8, width), FIX)],
-            scratch_shapes=[
-                pltpu.VMEM((4, tokens, width), BF),
-                pltpu.VMEM((4, tokens, width), BF),
-                pltpu.VMEM((4 * tokens, 2 * width), F32),
-                pltpu.VMEM((width, SEG), F32),
-                pltpu.SemaphoreType.DMA((2,)),
-            ],
-        ),
-        compiler_params=pltpu.CompilerParams(
-            dimension_semantics=("arbitrary",), vmem_limit_bytes=61 << 20
-        ),
-        cost_estimate=pl.CostEstimate(flops=4 * 10**9, transcendentals=0, bytes_accessed=12 << 20),
-        name="attend_backward",
-    )(place, parents, q, dos, o, lse, scale_row, keys, values)
 
 
 def gelu_parts(c):
@@ -904,19 +782,26 @@
     )(*os_pair, mixed, x, g, fc1, fc2, out_w, post, pre, wide)
 
 
-def finish(bits, *refs):
-    dq0, dq1, os0, os1, weight, pre, mid_gains, head0, head1 = refs[0:9]
-    held, came, dk1, dv1 = refs[9:13], refs[13:17], refs[17:21], refs[21:25]
-    full_hbm, du_hbm, x_hbm, dr1_hbm = refs[25:29]
-    din, grad, out_grad, small_out = refs[29:33]
-    piece, inbox, inner, grads, acc, stage, arrived, res, core_out, core_in, y_out, y_in, small, small_in = refs[33:47]
-    full, du, x, dr1, send, recv, local = refs[47:54]
+def closing(bits, parents, *refs):
+    q0, q1, os0, os1, lse0, lse1, scale_ref, weight, pre, mid_gains, shares = refs[0:11]
+    kt_hbm, vt_hbm, dos_hbm, o0_hbm, o1_hbm, full_hbm, du_hbm, x_hbm, dr1_hbm = refs[11:20]
+    din, res, small_out, ffn = refs[20:24]
+    (
+        kt, vt, dos, o, bias, dqt, contrib_k, contrib_v, dkp0, dkp1, dvp0, dvp1, inbox, inner, grads, acc, stage,
+        arrived, core_out, core_in, y_out, y_in, small, small_in, big, x, dr1, send, recv, local,
+    ) = refs[24:]
     shard = lax.axis_index("tensor")
     index = lax.axis_index("dp")
     near, far = other(shard, 1), other(shard, 2)
     rows, model = x.shape[1], x.shape[2]
-    tokens, width = dq0.shape
-    dqs = (dq0, dq1)
+    tokens, width = q0.shape
+    heads = width // HEAD_DIM
+    per = tokens // SEG
+    member, tree = index % 4, index // 4
+    trees = parents.shape[0] // (MICRO * SEGS)
+    qs, lses, os_hbm = (q0, q1), (lse0, lse1), (o0_hbm, o1_hbm)
+    dkp, dvp = (dkp0, dkp1), (dvp0, dvp1)
+    slots = DEPTH + 1
 
     def bit_of(mask):
         return (index // mask) % 2
@@ -927,15 +812,19 @@
     used = [0]
     pending = []
 
-    def remote(src, dst, target):
+    def prepare(src, dst, target):
         i = used[0]
         used[0] += 1
         copy = pltpu.make_async_remote_copy(
             src_ref=src, dst_ref=dst, send_sem=send.at[i], recv_sem=recv.at[i],
             device_id=target, device_id_type=pl.DeviceIdType.MESH,
         )
+        pending.append(copy)
+        return copy
+
+    def remote(src, dst, target):
+        copy = prepare(src, dst, target)
         copy.start()
-        pending.append(copy)
         return copy
 
     fetched = [0]
@@ -957,72 +846,187 @@
     targets = [{"tensor": near}, {"tensor": far}] + [dp_peer(mask) for mask in bits]
     for target in targets:
         pl.semaphore_signal(barrier, inc=1, device_id=target, device_id_type=pl.DeviceIdType.MESH)
-    mine1 = (dk1[0], dk1[1], dv1[0], dv1[2])
-    in_came = [fetch(came[i], inbox.at[0, i]) for i in range(4)]
-    got = [[fetch(src, piece.at[0, i]) for i, src in enumerate(held)]]
-    in_full = [fetch(full_hbm, full)]
-    got.append([fetch(src, piece.at[1, i]) for i, src in enumerate(mine1)])
-    in_rest = [fetch(du_hbm, du), fetch(x_hbm, x), fetch(dr1_hbm, dr1)]
+
+    def fetch_tree(m):
+        return [
+            fetch(kt_hbm.at[m], kt), fetch(vt_hbm.at[m], vt), fetch(dos_hbm.at[m], dos), fetch(os_hbm[m], o)
+        ]
+
+    count = shares.shape[0] // 2
+    group = ffn.shape[2]
+    lines = group // 2 ** len(bits)
+    base = 0
+    for step, mask in enumerate(bits):
+        base = base + bit_of(mask) * (group // 2 ** (step + 1))
+    base = pl.multiple_of(base, 16)
+    cut = max(1, count // 2)
+    parts = [(k, at) for k in range(2) for at in range(0, count, cut)]
+    in_share = [
+        fetch(shares.at[pl.ds(k * count + at, cut)], ffn.at[k, pl.ds(at, cut), pl.ds(base, lines), :])
+        for k, at in parts
+    ]
+    in_tree = fetch_tree(0)
+    in_du = fetch(du_hbm, big)
     pl.semaphore_wait(barrier, len(targets))
-
-    def first_sends():
+    gathers = []
+    size = lines
+    for mask in bits[::-1]:
+        rows_at = pl.ds(pl.multiple_of(base, 16), size)
+        level = []
+        for k, at in parts:
+            where = ffn.at[k, pl.ds(at, cut), rows_at, :]
+            level.append(prepare(where, where, dp_peer(mask)))
+        gathers.append(level)
+        base, size = base - bit_of(mask) * size, 2 * size
+    events = {}
+    for level in range(1, len(bits)):
+        for part in range(len(parts)):
+            turn = (1, 4, 8, 11)[part] if level < len(bits) - 1 else (7, 10, 14, 18)[part]
+            events.setdefault(min(23, turn), []).append((level, part))
+
+    def gather_turn(step, slot):
+        for turn, moves in sorted(events.items()):
+
+            @pl.when(step * 6 + slot == turn)
+            def _():
+                for level, part in moves:
+                    gathers[level - 1][part].wait_recv()
+                    gathers[level][part].start()
+
+    def attend_back(m, step):
+        seg = member * per + xor4(step, shard)
+        steps_up, found = climb(parents, (m * trees + tree) * SEGS, seg)
+        here = pl.ds(pl.multiple_of(step * SEG, SEG), SEG)
+        grad_out = dos[here, :]
+        cross = grad_out * o[here, :]
+        small[4, :, 0:width] += jnp.sum(cross.reshape(SEG // 8, 8, width), axis=0)
+        scale = scale_ref[...]
+        go = (grad_out * scale).astype(BF)
+        cross_t = jnp.transpose(cross * scale)
+        lane = lax.broadcasted_iota(jnp.int32, (SEG, width), 1) // HEAD_DIM
+        q = qs[m][here, :] * BF(HEAD_DIM ** -0.5)
+        zero = jnp.zeros_like(q)
+        q_heads = [jnp.where(lane == h, q, zero) for h in range(heads)]
+        g_heads = [jnp.where(lane == h, go, zero) for h in range(heads)]
+        deltas = [
+            jnp.sum(cross_t[h * HEAD_DIM:(h + 1) * HEAD_DIM], axis=0, keepdims=True) for h in range(heads)
+        ]
+        tops = lses[m][step]
+        dqt[...] = jnp.zeros_like(dqt)
+
+        def slot_block(slot):
+            here_slot = slot == DEPTH
+            source = seg
+            for j in range(DEPTH):
+                source = jnp.where(slot == j, found[j], source)
+            at = 4 * xor4(lax.div(source, 4), member) + xor4(lax.rem(source, 4), shard)
+            key_row = lax.broadcasted_iota(jnp.int32, (SEG, SEG), 0)
+            query_col = lax.broadcasted_iota(jnp.int32, (SEG, SEG), 1)
+            last = jnp.where(here_slot, 0, jnp.where(slot < steps_up, SEG, -SEG))
+            bias[...] = jnp.where(key_row <= query_col + last, 0.0, NEGATIVE)
+            k = kt[at]
+            v = vt[at]
+            k_t = jnp.transpose(k)
+            dk = jnp.zeros((SEG, width), F32)
+            dv = jnp.zeros((SEG, width), F32)
+            for h in range(heads):
+                p = jnp.exp(mm(k, q_heads[h], NT) + bias[...] - tops[h:h + 1, :])
+                dv += mm(p.astype(BF), g_heads[h])
+                dp = mm(v, g_heads[h], NT)
+                ds = (p * (dp - deltas[h])).astype(BF)
+                dk += mm(ds, q_heads[h])
+                dqt[pl.ds(h * HEAD_DIM, HEAD_DIM), :] += mm(k_t[h * HEAD_DIM:(h + 1) * HEAD_DIM], ds)
+            contrib_k[step * slots + slot] = dk.astype(BF)
+            contrib_v[step * slots + slot] = dv.astype(BF)
+            if m == 0:
+                gather_turn(step, slot)
+
+        each(slots, slot_block)
+        grads[m, here, 0:width] = (jnp.transpose(dqt[...]) * HEAD_DIM ** -0.5).astype(BF)
+
+    def combine(m, r):
+        def one(line):
+            seg = xor4(jnp.int32(r), member) * per + xor4(line, shard)
+            dk = jnp.zeros((SEG, width), F32)
+            dv = jnp.zeros((SEG, width), F32)
+            for step in range(4):
+                own = member * per + other(shard, step)
+                steps_up, found = climb(parents, (m * trees + tree) * SEGS, own)
+                at = jnp.where(seg == own, step * slots + DEPTH, 4 * slots)
+                for j in range(DEPTH):
+                    hit = jnp.logical_and(found[j] == seg, j < steps_up)
+                    at = jnp.where(hit, step * slots + j, at)
+                dk = dk + contrib_k[at].astype(F32)
+                dv = dv + contrib_v[at].astype(F32)
+            dkp[m][4 * r + line] = dk.astype(BF)
+            dvp[m][4 * r + line] = dv.astype(BF)
+
+        each(4, one)
+
+    def piece(ref, r):
+        return ref.at[pl.ds(4 * r, 4)]
+
+    def first_sends(m):
+        combine(m, 3)
+        copies = [
+            remote(piece(dkp[m], 3), inbox.at[m, 0], dp_peer(2)),
+            remote(piece(dvp[m], 3), inbox.at[m, 1], dp_peer(1)),
+        ]
+        combine(m, 2)
+        copies.append(remote(piece(dkp[m], 2), inbox.at[m, 2], dp_peer(2)))
+        combine(m, 1)
+        copies.append(remote(piece(dvp[m], 1), inbox.at[m, 3], dp_peer(1)))
+        combine(m, 0)
+        return copies
+
+    def second_pair(m):
         return [
-            remote(dk1[3], inbox.at[1, 0], dp_peer(2)),
-            remote(dv1[3], inbox.at[1, 1], dp_peer(1)),
-            remote(dk1[2], inbox.at[1, 2], dp_peer(2)),
-            remote(dv1[1], inbox.at[1, 3], dp_peer(1)),
+            prepare(inner.at[m, 0], inbox.at[m, 4], dp_peer(1)),
+            prepare(inner.at[m, 1], inbox.at[m, 5], dp_peer(2)),
         ]
 
-    class Here:
-        def __init__(self, copy):
-            self.copy = copy
-
-        def wait_recv(self):
-            self.copy.wait()
-
-    def add_rows(out, terms):
+    def second_sends(m, first, second):
+        for i, own in enumerate((piece(dkp[m], 1), piece(dvp[m], 2))):
+            first[i].wait_recv()
+
+            def one(n):
+                inner[m, i, n] = (own[n].astype(F32) + inbox[m, i, n].astype(F32)).astype(BF)
+
+            each(4, one)
+            second[i].start()
+
+    def own_rows(m, kind, own, slots_in):
         def one(n):
-            total = terms[0][tile(n), :].astype(F32)
-            for term in terms[1:]:
-                total = total + term[tile(n), :].astype(F32)
-            out[tile(n), :] = total.astype(out.dtype)
-
-        each(tokens // SEG, one)
-
-    def second_sends(m, first):
-        for copy in got[m]:
-            copy.wait()
-        first[0].wait_recv()
-        add_rows(inner.at[m, 0], [piece.at[m, 1], inbox.at[m, 0]])
-        one = remote(inner.at[m, 0], inbox.at[m, 4], dp_peer(1))
-        first[1].wait_recv()
-        add_rows(inner.at[m, 1], [piece.at[m, 3], inbox.at[m, 1]])
-        two = remote(inner.at[m, 1], inbox.at[m, 5], dp_peer(2))
-        return one, two
+            total = own[n].astype(F32)
+            for i in slots_in:
+                total = total + inbox[m, i, n].astype(F32)
+            grads[m, tile(n), kind * width:(kind + 1) * width] = total.astype(BF)
+
+        each(4, one)
 
     def own_key(m, first, second):
         first[2].wait_recv()
         second[0].wait_recv()
-        add_rows(grads.at[m, :, width:2 * width], [piece.at[m, 0], inbox.at[m, 2], inbox.at[m, 4]])
+        own_rows(m, 1, piece(dkp[m], 0), (2, 4))
 
     def own_value(m, first, second):
         first[3].wait_recv()
         second[1].wait_recv()
-        add_rows(grads.at[m, :, 2 * width:3 * width], [piece.at[m, 2], inbox.at[m, 3], inbox.at[m, 5]])
+        own_rows(m, 2, piece(dvp[m], 0), (3, 5))
 
     def out_rows(n):
-        acc[3, tile(n), :] = mm(du[0, :, tile(n)], os0[...], TN) + mm(du[1, :, tile(n)], os1[...], TN)
+        acc[3, tile(n), :] = mm(big[0, :, tile(n)], os0[...], TN) + mm(big[1, :, tile(n)], os1[...], TN)
 
     def weight_rows(m, kind):
         cols = slice(kind * width, (kind + 1) * width)
 
         def one(n):
-            part = mm(full[m, :, tile(n)], grads[m, :, cols], TN)
+            part = mm(big[m, :, tile(n)], grads[m, :, cols], TN)
             acc[kind, tile(n), :] = part if m == 0 else acc[kind, tile(n), :] + part
 
         each(model // SEG, one)
 
-    def input_rows(m):
+    def input_rows(m, old):
         def block(r, out):
             def one(n):
                 part = jnp.zeros((rows, SEG), F32)
@@ -1036,16 +1040,19 @@
 
             each(model // SEG, one)
 
-        block(3, core_out.at[m, 0])
-        hop3 = remote(core_out.at[m, 0], core_in.at[m, 0], {"tensor": near})
-        block(1, core_out.at[m, 1])
-        hop1 = remote(core_out.at[m, 1], core_in.at[m, 1], {"tensor": near})
+        for copy in old:
+            copy.wait_send()
+            pending[:] = [kept for kept in pending if kept is not copy]
+        block(3, core_out.at[0])
+        hop3 = remote(core_out.at[0], core_in.at[m, 0], {"tensor": near})
         block(2, din.at[m])
         hop3.wait_recv()
-        y_out[m] = (din[m] + core_in[m, 0].astype(F32)).astype(BF)
-        hop = remote(y_out.at[m], y_in.at[m], {"tensor": far})
+        y_out[...] = (din[m] + core_in[m, 0].astype(F32)).astype(BF)
+        hop = remote(y_out, y_in.at[m], {"tensor": far})
+        block(1, core_out.at[1])
+        hop1 = remote(core_out.at[1], core_in.at[m, 1], {"tensor": near})
         block(0, din.at[m])
-        return hop1, hop
+        return hop1, hop, hop3
 
     chunk = 32
 
@@ -1112,45 +1119,66 @@
                     self.back = True
                     self.gather_send()
 
-    for m in range(MICRO):
-        grads[m, :, 0:width] = dqs[m][...]
     small[...] = jnp.zeros_like(small)
     small[1:4] = mid_gains[...].reshape(3, 8, model)
-    small[4, :, 0:width] = head0[...] + head1[...]
-
-    first0 = [Here(copy) for copy in in_came]
-    second0 = second_sends(0, first0)
-    first1 = first_sends()
-    for copy in in_full:
+    contrib_k[4 * slots] = jnp.zeros((SEG, width), BF)
+    contrib_v[4 * slots] = jnp.zeros((SEG, width), BF)
+    for copy, part in zip(in_share, gathers[0]):
         copy.wait()
+        part.start()
+    in_du.wait()
+    query, mixer, key, value = [Chain(kind) for kind in (0, 3, 1, 2)]
+    each(model // SEG, out_rows)
+    mixer.reduce_send()
+    in_full = fetch(full_hbm, big)
+    in_rest = [fetch(x_hbm, x), fetch(dr1_hbm, dr1)]
+    for copy in in_tree:
+        copy.wait()
+
+    each(4, lambda step: attend_back(0, step))
+    in_tree = fetch_tree(1)
+    first0 = first_sends(0)
+    second0 = second_pair(0)
+    mixer.go()
+    for copy in in_tree:
+        copy.wait()
+
+    def back1(step):
+        attend_back(1, step)
+
+        @pl.when(step == 1)
+        def _():
+            second_sends(0, first0, second0)
+
+    each(4, back1)
+    first1 = first_sends(1)
+    second1 = second_pair(1)
+    mixer.go()
+    in_full.wait()
     weight_rows(0, 0)
     weight_rows(1, 0)
-    query, mixer, key, value = [Chain(kind) for kind in (0, 3, 1, 2)]
     query.reduce_send()
+    own_key(0, first0, second0)
+    own_value(0, first0, second0)
     for copy in in_rest:
         copy.wait()
-    each(model // SEG, out_rows)
-    mixer.reduce_send()
-    own_key(0, first0, second0)
-    own_value(0, first0, second0)
-    hops0 = input_rows(0)
+    hops0 = input_rows(0, ())
+    second_sends(1, first1, second1)
     weight_rows(0, 1)
     weight_rows(0, 2)
-    second1 = second_sends(1, first1)
     query.go()
     mixer.go()
     input_norms(0, hops0)
     query.go()
-    mixer.go()
     own_key(1, first1, second1)
     weight_rows(1, 1)
     key.reduce_send()
     own_value(1, first1, second1)
     weight_rows(1, 2)
     value.reduce_send()
-    hops1 = input_rows(1)
     query.go()
     mixer.go()
+    hops1 = input_rows(1, hops0)
     key.go()
     value.go()
     query.go()
@@ -1186,61 +1214,70 @@
                 chain.go()
     small_out[...] = small[2 + len(bits)]
 
-    def widen(n):
-        for kind in range(3):
-            grad[kind, tile(n), :] = res[kind, tile(n), :].astype(F32)
-        out_grad[:, tile(n)] = jnp.transpose(res[3, tile(n), :].astype(F32))
-
-    each(model // SEG, widen)
+    for copy in gathers[-1]:
+        copy.wait_recv()
     for copy in pending:
         copy.wait_send()
 
 
-def finish_call(dqs, held, came, dk1, dv1, full, os_pair, du, x, dr1, weight, pre, mid_gains, heads):
+def closing_call(parents, qs, os_pair, lses, scale_row, weight, pre, mid_gains, kt, vt, dos, outs, full, du, x, dr1, shares):
     micro, rows, model = x.shape
-    tokens, width = dqs[0].shape
-    bits = tuple(2**b for b in range(lax.axis_size("dp").bit_length() - 1))
+    tokens, width = qs[0].shape
+    size = lax.axis_size("dp")
+    bits = tuple(2**b for b in range(size.bit_length() - 1))
     vmem = pl.BlockSpec(memory_space=pltpu.VMEM)
+    count, lines = shares.shape[0], shares.shape[1]
+    slots = DEPTH + 1
+    segs = pltpu.VMEM((4 * tokens // SEG, SEG, width), BF)
     return pl.pallas_call(
-        partial(finish, bits),
+        partial(closing, bits),
         out_shape=(
             jax.ShapeDtypeStruct((micro, rows, model), F32),
-            jax.ShapeDtypeStruct((3, model, width), F32),
-            jax.ShapeDtypeStruct((width, model), F32),
+            jax.ShapeDtypeStruct((4, model, width), BF),
             jax.ShapeDtypeStruct((8, model), F32),
+            jax.ShapeDtypeStruct((2, count // 2, lines * size, model), BF),
         ),
-        in_specs=[vmem] * 9 + [HBM] * 20,
-        out_specs=(vmem,) * 4,
+        in_specs=[pl.BlockSpec(memory_space=pltpu.SMEM)] + [vmem] * 11 + [HBM] * 9,
+        out_specs=(vmem, vmem, vmem, HBM),
         scratch_shapes=[
-            pltpu.VMEM((micro, 4, tokens, width), BF),
-            pltpu.VMEM((micro, 6, tokens, width), BF),
-            pltpu.VMEM((micro, 2, tokens, width), BF),
+            segs,
+            segs,
+            pltpu.VMEM((tokens, width), F32),
+            pltpu.VMEM((tokens, width), F32),
+            pltpu.VMEM((SEG, SEG), F32),
+            pltpu.VMEM((width, SEG), F32),
+            pltpu.VMEM((4 * slots + 1, SEG, width), BF),
+            pltpu.VMEM((4 * slots + 1, SEG, width), BF),
+            segs,
+            segs,
+            segs,
+            segs,
+            pltpu.VMEM((micro, 6, tokens // SEG, SEG, width), BF),
+            pltpu.VMEM((micro, 2, tokens // SEG, SEG, width), BF),
             pltpu.VMEM((micro, tokens, 3 * width), BF),
             pltpu.VMEM((4, model, width), F32),
             pltpu.VMEM((4, model, width), BF),
             pltpu.VMEM((4, model, width), BF),
-            pltpu.VMEM((4, model, width), BF),
+            pltpu.VMEM((2, rows, model), BF),
             pltpu.VMEM((micro, 2, rows, model), BF),
-            pltpu.VMEM((micro, 2, rows, model), BF),
-            pltpu.VMEM((micro, rows, model), BF),
+            pltpu.VMEM((rows, model), BF),
             pltpu.VMEM((micro, rows, model), BF),
             pltpu.VMEM((3 + len(bits) + 2, 8, model), F32),
             pltpu.VMEM((2 + len(bits), 8, model), F32),
             pltpu.VMEM((micro, tokens, model), BF),
-            pltpu.VMEM((micro, tokens, model), BF),
             pltpu.VMEM((micro, rows, model), BF),
             pltpu.VMEM((micro, rows, model), F32),
-            pltpu.SemaphoreType.DMA((24 + 9 * len(bits),)),
-            pltpu.SemaphoreType.DMA((24 + 9 * len(bits),)),
+            pltpu.SemaphoreType.DMA((28 + 14 * len(bits),)),
+            pltpu.SemaphoreType.DMA((28 + 14 * len(bits),)),
             pltpu.SemaphoreType.DMA((20,)),
         ],
         compiler_params=pltpu.CompilerParams(
-            collective_id=1, has_side_effects=True, vmem_limit_bytes=61 << 20
+            collective_id=1, has_side_effects=True, vmem_limit_bytes=62 << 20
         ),
-        cost_estimate=pl.CostEstimate(flops=60 * 10**9, transcendentals=0, bytes_accessed=30 << 20),
-        name="finish",
+        cost_estimate=pl.CostEstimate(flops=120 * 10**9, transcendentals=0, bytes_accessed=30 << 20),
+        name="closing",
     )(
-        *dqs, *os_pair, weight, pre, mid_gains, *heads, *held, *came, *dk1, *dv1, full, du, x, dr1
+        parents, *qs, *os_pair, *lses, scale_row, weight, pre, mid_gains, shares, kt, vt, dos, *outs, full, du, x, dr1
     )
 
 
@@ -1258,25 +1295,15 @@
     ffn_norm_gain,
     fc2_weight,
 ):
-    trees = parent.shape[1]
-    group = lax.axis_size("dp") // trees
-    member = lax.axis_index("dp") % group
-    tree_index = lax.axis_index("dp") // group
-    shard = lax.axis_index("tensor")
-    row_count = block_input.shape[1]
     tokens = cotangent.shape[1]
     width = qkv_weight.shape[2]
     parents = parent.reshape(-1)
     scale_row = jnp.repeat(head_scale, HEAD_DIM)[None, :]
 
-    def place(micro):
-        return jnp.stack([(micro * trees + tree_index) * SEGS, member, shard]).astype(jnp.int32)
-
     q0, q1, o0, o1, os0, os1, lse0, lse1, mixed, full1, keys, values = opening_call(
         parents, block_input, pre_attn_gain[None], qkv_weight, scale_row, out_weight
     )
     full1 = full1.reshape(MICRO, tokens, -1)
-    keys, values = [tree.reshape(MICRO, 4, tokens, width) for tree in (keys, values)]
     du, dos, dr1, f_own, f_far, mid_gains, shares = middle_call(
         (os0, os1),
         mixed,
@@ -1289,44 +1316,36 @@
         pre_ffn_gain[None],
         ffn_norm_gain[None],
     )
-    count, lines, model = shares.shape
-    whole = lax.all_gather(shares, "dp", axis=0)
     f_got = swap(f_far, "tensor", 2)
     outputs = (f_own + f_got.astype(F32)).astype(BF)
-    backs = [
-        attention_grad(m, place(m), parents, q, dos[m], o, lse, scale_row, keys, values)
-        for m, (q, o, lse) in enumerate(((q0, o0, lse0), (q1, o1, lse1)))
-    ]
-    dk0, dv0 = backs[0][1:5], backs[0][5:9]
-    came = (swap(dk0[3], "dp", 2), swap(dv0[3], "dp", 1), swap(dk0[2], "dp", 2), swap(dv0[1], "dp", 1))
-    din, qkv_grad, out_grad, small = finish_call(
-        [b[0] for b in backs],
-        (dk0[0], dk0[1], dv0[0], dv0[2]),
-        came,
-        backs[1][1:5],
-        backs[1][5:9],
+    din, narrow, small, whole = closing_call(
+        parents,
+        (q0, q1),
+        (os0, os1),
+        (lse0, lse1),
+        scale_row,
+        qkv_weight,
+        pre_attn_gain[None],
+        mid_gains,
+        keys,
+        values,
+        dos,
+        (o0, o1),
         full1,
-        (os0, os1),
         du,
         block_input,
         dr1,
-        qkv_weight,
-        pre_attn_gain[None],
-        mid_gains,
-        [b[9] for b in backs],
+        shares,
     )
     head_grad = small[4, 0:width].reshape(-1, HEAD_DIM).sum(-1)
-    levels = lax.axis_size("dp").bit_length() - 1
-    whole = whole.reshape((2,) * levels + (2, count // 2, lines, model))
-    whole = jnp.transpose(whole, (levels, levels + 1) + tuple(range(levels))[::-1] + (levels + 2, levels + 3))
-    whole = whole.reshape(2, -1, model)
+    whole = whole.reshape(2, -1, whole.shape[-1])
     return (
         outputs,
         din,
         small[0],
-        qkv_grad,
+        narrow[0:3].astype(F32),
         head_grad,
-        out_grad,
+        narrow[3].T.astype(F32),
         small[1],
         small[2],
         whole[0].astype(F32),

time: 495 us -> 475 us (0.960)
  the two profiles are of different devices: /device:TPU:0 before, /device:TPU:22 now
where the time goes in v4:
time: 475 us; the launch traced here: 468 us
  Pallas kernels  444 us (93%)
  other arithmetic  11.2 us (2%)
  local copies, waits for them, and re-layouts  9.25 us (2%)
    pallas_call x1, Pallas kernels, closing_call(): pl.pallas_call(partial(closing, bits), out_shape=(jax.ShapeDtypeStruct((m...  204 us
    pallas_call x1, Pallas kernels, middle_call(): pl.pallas_call(partial(middle, bits), out_shape=(wide_rows, jax.ShapeDtyp...  150 us
    pallas_call x1, Pallas kernels, opening_call(): pl.pallas_call(opening, out_shape=(narrow, narrow, narrow_wide, narrow_wi...  90 us
  transfers between devices with their start and end apart: 1, of which 0 were waited for; matrix products, arithmetic and copies ran while one was open for 3% of the time, Pallas kernels for 44%

profile of v4, /device:TPU:22, one launch (start us, length us, event | category | flops | bytes accessed | tf_op | source)
XLA Modules:
  0.0 467.7 jit_solution(3221361795668921238)
XLA Ops:
  0.6 1.3 reshape.39.parents
  1.9 0.7 broadcast_in_dim.17
  2.6 0.6 broadcast_in_dim_reshape.3.scale_ref.refs_6_
  3.3 90.0 %opening.1 = (bf16[1024,256]{1,0:T(8,128)(2,1)}, bf16[1024,256]{1,0:T(8,128)(2,1)}, f32[1024,256]{1,0:T(8,128)}, f32[1024,256]{1,0:T(8,128)}, bf16[1024,256]{1,0...) custom-call(s32[64]{0:T(128)} %reshape.39.parents, ...), custom_call_target="tpu_custom_call" | custom-call | flops 60000002048 | bytes 20971520 | tf_op jit(solution)/shard_map/opening/pallas_call | solution.py:280
  93.3 149.9 %middle.1 = (bf16[2,1024,1024]{2,1,0:T(8,128)(2,1)}, f32[2,1024,256]{2,1,0:T(8,128)}, f32[2,256,1024]{2,1,0:T(8,128)}, f32[2,256,1024]{2,1,0:T(8,128)}, bf16[2,2...) custom-call(bf16[1024,256]{1,0:T(8,128)(2,1)} %get-tuple-element.34.os0.refs_2_, ...), custom_call_target="tpu_custom_call" | custom-call | flops 99999997952 | bytes 41943040 | tf_op jit(solution)/shard_map/middle/pallas_call | solution.py:741
  243.2 2.3 collective-permute-start
  245.5 204.1 %closing.1 = (f32[2,256,1024]{2,1,0:T(8,128)}, bf16[4,1024,256]{2,1,0:T(8,128)(2,1)}, f32[8,1024]{1,0:T(8,128)}, bf16[2,4,256,1024]{3,2,1,0:T(8,128)(2,1)}) custom-call(s32[64]{0:T(128)} %reshape.39.parents, bf16[1024,256]{1,0:T(8,128)(2,1)} %get-tuple-element.39.refs_0_, bf16[1024,256]{1,0:T(8,128)(2,1)} %get-tuple-element.40.refs_1_, ...), custom_call_target="tpu_custom_call" | custom-call | flops 120000004096 | bytes 31457280 | tf_op jit(solution)/shard_map/closing/pallas_call | solution.py:1232
  449.7 0.0 copy-start.2
  449.7 3.3 slice_convert_fusion
  453.0 1.1 convert_bitcast_fusion
  454.1 0.0 copy-done.2
  454.2 0.1 reshape_squeeze.3
  454.3 1.3 copy.23
  455.6 0.6 reduce_sum.9
  456.2 0.6 fusion.1
  456.8 2.7 fusion
  459.5 0.0 copy-start
  459.5 4.7 %bitcast_convert_fusion = (f32[1024,1024]{1,0:T(8,128)}, f32[1024,1024]{1,0:T(8,128)}) fusion(bf16[1,4,256,1024]{3,2,1,0:T(8,128)(2,1)S(1)} %get-tuple-element.68, bf16[1,4,256,1024]{3,2,1,0:T(8,128)(2,1)S(1)} %get-tuple-element.69), kind=kLoop, calls=%fused_computation | loop fusion | flops 2097152 | bytes 12582912 | tf_op jit(solution)/shard_map/convert_element_type | solution.py:1353
  464.2 0.0 collective-permute-done
  464.2 0.0 copy-done
  464.2 0.0 copy-start.1
  464.2 1.4 add_convert_fusion
  465.6 0.6 copy-done.1
  466.2 1.3 copy.25
  (1 shorter events, 0.0 us)
Async XLA Ops:
  243.2 221.0 %collective-permute-start = (bf16[2,256,1024]{2,1,0:T(8,128)(2,1)}, bf16[2,256,1024]{2,1,0:T(8,128)(2,1)S(1)}, u32[]{:S(2)}, u32[]{:S(2)}) collective-permute-start(bf16[2,256,1024]{2,1,0:T(8,128)(2,1)} %get-tuple-element.38), channel_id=1, source_target_pairs={{0,2},{1,3},{2,0},{3,1},{4,6},{5,7},{6,4},{7,5},{8,10},{9,11},{10,... | collective-permute-start | bytes 3145736 | tf_op jit(solution)/shard_map/ppermute | solution.py:31
  449.7 4.5 copy-start.2
  459.5 4.7 %copy-start = (f32[2,256,1024]{2,1,0:T(8,128)S(1)}, f32[2,256,1024]{2,1,0:T(8,128)}, u32[]{:S(2)}) copy-start(f32[2,256,1024]{2,1,0:T(8,128)} %get-tuple-element.37) | copy-start | bytes 6291460
  464.2 2.0 copy-start.1

commit v5 on v4

--- a/solution.py
+++ b/solution.py
@@ -388,11 +388,14 @@
     def first_hop(kind, m, block, out):
         block(3, core_out.at[m, 0])
         hop3 = remote(core_out.at[m, 0], core_in.at[kind, m, 0], 1)
+        block(2, None)
+        hop3.wait_recv()
+        add_far(kind, m)
+        far_hop = remote(y_out.at[m], y_in.at[kind, m], 2)
         block(1, core_out.at[m, 1])
         hop1 = remote(core_out.at[m, 1], core_in.at[kind, m, 1], 1)
-        block(2, None)
         block(0, out)
-        return hop3, hop1
+        return hop3, hop1, far_hop
 
     chunk = 32
 
@@ -416,10 +419,6 @@
 
         return block
 
-    hops = first_hop(0, 1, mixed_block(), nu.at[1])
-    hops[0].wait_recv()
-    add_far(0, 1)
-    far_hop = remote(y_out.at[1], y_in.at[0, 1], 2)
     def project_grad(m):
         for r in range(4):
             got_g[m][r].wait()
@@ -438,10 +437,10 @@
         inverse = lax.rsqrt(jnp.mean(center * center, axis=-1, keepdims=True) + EPSILON)
         return center * inverse, inverse
 
-    def forward_norms(m):
+    def forward_norms(m, hops=None):
         if m:
             hops[1].wait_recv()
-            far_hop.wait_recv()
+            hops[2].wait_recv()
 
         def one(at):
             mixed, inverse = norm_two(m, at, own_sum(0, m, nu[m, at], at) if m else mixed0[at, :])
@@ -544,6 +543,7 @@
 
     forward_norms(0)
     far0, near0 = spread(0, full)
+    hops = first_hop(0, 1, mixed_block(), nu.at[1])
     got_fc2.wait()
     project_grad(0)
     got_fc1.wait()
@@ -551,26 +551,23 @@
     near0.wait_recv()
     ffn_forward(0, 1)
     project_grad(1)
-    forward_norms(1)
-    far1, near1 = spread(1, full)
-    ffn_forward(1, 0)
     far0.wait_recv()
     cross0 = remote(full.at[0, 2], full.at[0, 3], 1)
     ffn_forward(0, 2)
     cross0.wait_recv()
     ffn_forward(0, 3)
     stats0 = send_stats(0)
+    forward_norms(1, hops)
+    far1, near1 = spread(1, full)
+    ffn_forward(1, 0)
     near1.wait_recv()
     ffn_forward(1, 1)
+    for copy in stats0:
+        copy.wait_recv()
+    hop_a = first_hop(1, 0, grad_block(0), dr1.at[0])
     far1.wait_recv()
     cross1 = remote(full.at[1, 2], full.at[1, 3], 1)
     ffn_forward(1, 2)
-    for copy in stats0:
-        copy.wait_recv()
-    hop_a = first_hop(1, 0, grad_block(0), dr1.at[0])
-    hop_a[0].wait_recv()
-    add_far(1, 0)
-    far_a = remote(y_out.at[0], y_in.at[1, 0], 2)
     cross1.wait_recv()
     ffn_forward(1, 3)
     stats1 = send_stats(1)
@@ -589,12 +586,9 @@
     first_grad(0)
     for copy in stats1:
         copy.wait_recv()
-    reuse(hops, far_hop)
+    reuse(hops)
     hop_b = first_hop(1, 1, grad_block(1), dr1.at[1])
-    hop_b[0].wait_recv()
-    add_far(1, 1)
-    far_b = remote(y_out.at[1], y_in.at[1, 1], 2)
-    backward_norms(0, hop_a[1], far_a)
+    backward_norms(0, hop_a[1], hop_a[2])
     du_far0, du_near0 = spread(0, du)
     first_grad(1)
     group = hidden // (shares.shape[0] // 2)
@@ -604,6 +598,7 @@
             self.number, self.which = number, number // (hidden // group)
             self.start = (number % (hidden // group)) * group
             self.base, self.size, self.at, self.step = self.start, group, self.start, 0
+            self.back = False
 
         def send(self):
             mask = bits[self.step]
@@ -635,17 +630,37 @@
                     self.which, pl.ds(pl.multiple_of(where + i * 16, 16), 16), :
                 ].astype(F32)
                 if last:
-                    shares[self.number, pl.ds(pl.multiple_of(i * 16, 16), 16), :] = total.astype(BF)
+                    at = self.start + base - self.first + i * 16
+                    staged[self.which, pl.ds(pl.multiple_of(at, 16), 16), :] = total.astype(BF)
                 else:
                     act[self.which, mine, :] = total
 
             each(self.size // 16, one)
             self.at += self.size
+            if self.step == 1:
+                self.first = base
+
+        def gather(self):
+            self.step -= 1
+            mask = bits[self.step]
+            at = pl.ds(pl.multiple_of(self.start + self.base - self.first, 16), self.size)
+            self.copy = remote(staged.at[self.which, at, :], staged.at[self.which, at, :], dp_peer(mask))
+            self.base, self.size = self.base - bit_of(mask) * self.size, 2 * self.size
 
         def go(self):
-            self.wait()
-            if self.step < len(bits):
+            if self.back:
+                self.copy.wait_recv()
+            else:
+                self.wait()
+                self.back = self.step == len(bits)
+            if not self.back:
+                reuse(self.copy)
                 self.send()
+            elif self.which == 0 and self.step > 1:
+                self.gather()
+            else:
+                half = group // 2
+                store(staged.at[self.which, pl.ds(self.start, half), :], shares.at[self.number])
 
     chains = [Chain(i) for i in range(shares.shape[0])]
     half_chains = len(chains) // 2
@@ -656,7 +671,7 @@
     for i, chain in enumerate(chains[half_chains:]):
         each(per_chain, lambda n: second_grad(n + i * per_chain))
         chain.send()
-    backward_norms(1, hop_b[1], far_b)
+    backward_norms(1, hop_b[1], hop_b[2])
     du_far1, du_near1 = spread(1, du)
 
     def ffn_out(m, hop_old):
@@ -684,9 +699,9 @@
 
     todo = [
         chains[turn - level]
-        for turn in range(len(chains) + len(bits) - 1)
-        for level in range(len(bits))
-        if 0 <= turn - level < len(chains)
+        for turn in range(len(chains) + 2 * len(bits) - 2)
+        for level in range(2 * len(bits) - 1)
+        if 0 <= turn - level < (half_chains if level >= len(bits) else len(chains))
     ]
 
     def advance(count):
@@ -746,10 +761,10 @@
             own, own,
             jax.ShapeDtypeStruct((micro, rows, model), BF),
             jax.ShapeDtypeStruct((24, model), F32),
-            jax.ShapeDtypeStruct((count, group // size, model), BF),
+            jax.ShapeDtypeStruct((count, group // 2, model), BF),
         ),
         in_specs=[vmem, vmem, vmem, vmem, HBM, HBM, HBM, vmem, vmem, vmem, vmem],
-        out_specs=(HBM, vmem, vmem, vmem, vmem, vmem, vmem),
+        out_specs=(HBM, vmem, vmem, vmem, vmem, vmem, HBM),
         scratch_shapes=[
             pltpu.VMEM((model, hidden), BF),
             pltpu.VMEM((hidden, model), BF),
@@ -770,9 +785,9 @@
             pltpu.VMEM((4, rows, 128), F32),
             pltpu.VMEM((128, rows), F32),
             pltpu.VMEM((2, hidden, model), BF),
-            pltpu.SemaphoreType.DMA((40 + count * len(bits),)),
-            pltpu.SemaphoreType.DMA((40 + count * len(bits),)),
-            pltpu.SemaphoreType.DMA((20,)),
+            pltpu.SemaphoreType.DMA((40 + 2 * count * len(bits),)),
+            pltpu.SemaphoreType.DMA((40 + 2 * count * len(bits),)),
+            pltpu.SemaphoreType.DMA((20 + count,)),
         ],
         compiler_params=pltpu.CompilerParams(
             collective_id=0, has_side_effects=True, vmem_limit_bytes=61 << 20
@@ -783,8 +798,8 @@
 
 
 def closing(bits, parents, *refs):
-    q0, q1, os0, os1, lse0, lse1, scale_ref, weight, pre, mid_gains, shares = refs[0:11]
-    kt_hbm, vt_hbm, dos_hbm, o0_hbm, o1_hbm, full_hbm, du_hbm, x_hbm, dr1_hbm = refs[11:20]
+    q0, q1, os0, os1, lse0, lse1, scale_ref, weight, pre, mid_gains = refs[0:10]
+    shares, kt_hbm, vt_hbm, dos_hbm, o0_hbm, o1_hbm, full_hbm, du_hbm, x_hbm, dr1_hbm = refs[10:20]
     din, res, small_out, ffn = refs[20:24]
     (
         kt, vt, dos, o, bias, dqt, contrib_k, contrib_v, dkp0, dkp1, dvp0, dvp1, inbox, inner, grads, acc, stage,
@@ -852,36 +867,48 @@
             fetch(kt_hbm.at[m], kt), fetch(vt_hbm.at[m], vt), fetch(dos_hbm.at[m], dos), fetch(os_hbm[m], o)
         ]
 
-    count = shares.shape[0] // 2
-    group = ffn.shape[2]
-    lines = group // 2 ** len(bits)
-    base = 0
-    for step, mask in enumerate(bits):
-        base = base + bit_of(mask) * (group // 2 ** (step + 1))
-    base = pl.multiple_of(base, 16)
+    count, half = shares.shape[0] // 2, shares.shape[1]
+    lines = 2 * half // 2 ** len(bits)
+    base = bit_of(bits[0]) * half
+    inside = 0
+    for step, mask in enumerate(bits[1:]):
+        inside = inside + bit_of(mask) * (half // 2 ** (step + 1))
     cut = max(1, count // 2)
-    parts = [(k, at) for k in range(2) for at in range(0, count, cut)]
+    parts = list(range(0, count, cut))
+    whole_half = pl.ds(pl.multiple_of(base, 16), half)
+    own_lines = pl.ds(pl.multiple_of(base + inside, 16), lines)
+    inside_lines = pl.ds(pl.multiple_of(inside, 16), lines)
     in_share = [
-        fetch(shares.at[pl.ds(k * count + at, cut)], ffn.at[k, pl.ds(at, cut), pl.ds(base, lines), :])
-        for k, at in parts
+        fetch(shares.at[pl.ds(count + at, cut), inside_lines, :], ffn.at[1, pl.ds(at, cut), own_lines, :])
+        for at in parts
     ]
     in_tree = fetch_tree(0)
     in_du = fetch(du_hbm, big)
+    in_share.append(fetch(shares.at[pl.ds(0, count)], ffn.at[0, :, whole_half, :]))
     pl.semaphore_wait(barrier, len(targets))
+    ready = [
+        remote(shares.at[pl.ds(at, cut)], ffn.at[0, pl.ds(at, cut), whole_half, :], dp_peer(bits[0]))
+        for at in parts
+    ]
     gathers = []
-    size = lines
+    size, base = lines, base + inside
     for mask in bits[::-1]:
         rows_at = pl.ds(pl.multiple_of(base, 16), size)
         level = []
-        for k, at in parts:
-            where = ffn.at[k, pl.ds(at, cut), rows_at, :]
-            level.append(prepare(where, where, dp_peer(mask)))
+        for at in parts:
+            where = ffn.at[1, pl.ds(at, cut), rows_at, :]
+            source = where if gathers else shares.at[pl.ds(count + at, cut), inside_lines, :]
+            level.append(prepare(source, where, dp_peer(mask)))
+        if not gathers:
+            for copy in level:
+                copy.start()
         gathers.append(level)
         base, size = base - bit_of(mask) * size, 2 * size
+
     events = {}
     for level in range(1, len(bits)):
         for part in range(len(parts)):
-            turn = (1, 4, 8, 11)[part] if level < len(bits) - 1 else (7, 10, 14, 18)[part]
+            turn = (2, 6)[part] if level < len(bits) - 1 else (8, 13)[part]
             events.setdefault(min(23, turn), []).append((level, part))
 
     def gather_turn(step, slot):
@@ -890,6 +917,8 @@
             @pl.when(step * 6 + slot == turn)
             def _():
                 for level, part in moves:
+                    if level == 1:
+                        in_share[part].wait()
                     gathers[level - 1][part].wait_recv()
                     gathers[level][part].start()
 
@@ -1073,12 +1102,13 @@
         each(rows // chunk, one)
 
     class Chain:
-        def __init__(self, kind):
+        def __init__(self, kind, order):
+            self.order = order
             self.kind, self.base, self.size, self.at, self.step = kind, 0, model, 0, 0
             self.copy, self.back, self.done = None, False, False
 
         def reduce_send(self):
-            mask = bits[self.step]
+            mask = self.order[self.step]
             half = self.size // 2
             out = pl.ds(pl.multiple_of(self.base + (1 - bit_of(mask)) * half, 16), half)
             slot = pl.ds(self.at, half)
@@ -1099,7 +1129,7 @@
 
         def gather_send(self):
             self.step -= 1
-            mask = bits[self.step]
+            mask = self.order[self.step]
             mine = pl.ds(pl.multiple_of(self.base, 16), self.size)
             self.copy = remote(res.at[self.kind, mine, :], res.at[self.kind, mine, :], dp_peer(mask))
             self.base, self.size = self.base - bit_of(mask) * self.size, 2 * self.size
@@ -1123,11 +1153,9 @@
     small[1:4] = mid_gains[...].reshape(3, 8, model)
     contrib_k[4 * slots] = jnp.zeros((SEG, width), BF)
     contrib_v[4 * slots] = jnp.zeros((SEG, width), BF)
-    for copy, part in zip(in_share, gathers[0]):
-        copy.wait()
-        part.start()
     in_du.wait()
-    query, mixer, key, value = [Chain(kind) for kind in (0, 3, 1, 2)]
+    turned = bits[1:] + bits[:1]
+    query, mixer, key, value = [Chain(*a) for a in ((0, bits), (3, turned), (1, bits), (2, turned))]
     each(model // SEG, out_rows)
     mixer.reduce_send()
     in_full = fetch(full_hbm, big)
@@ -1214,8 +1242,9 @@
                 chain.go()
     small_out[...] = small[2 + len(bits)]
 
-    for copy in gathers[-1]:
+    for copy in ready + gathers[-1]:
         copy.wait_recv()
+    in_share[-1].wait()
     for copy in pending:
         copy.wait_send()
 
@@ -1226,7 +1255,7 @@
     size = lax.axis_size("dp")
     bits = tuple(2**b for b in range(size.bit_length() - 1))
     vmem = pl.BlockSpec(memory_space=pltpu.VMEM)
-    count, lines = shares.shape[0], shares.shape[1]
+    count, half = shares.shape[0], shares.shape[1]
     slots = DEPTH + 1
     segs = pltpu.VMEM((4 * tokens // SEG, SEG, width), BF)
     return pl.pallas_call(
@@ -1235,9 +1264,9 @@
             jax.ShapeDtypeStruct((micro, rows, model), F32),
             jax.ShapeDtypeStruct((4, model, width), BF),
             jax.ShapeDtypeStruct((8, model), F32),
-            jax.ShapeDtypeStruct((2, count // 2, lines * size, model), BF),
+            jax.ShapeDtypeStruct((2, count // 2, 2 * half, model), BF),
         ),
-        in_specs=[pl.BlockSpec(memory_space=pltpu.SMEM)] + [vmem] * 11 + [HBM] * 9,
+        in_specs=[pl.BlockSpec(memory_space=pltpu.SMEM)] + [vmem] * 10 + [HBM] * 10,
         out_specs=(vmem, vmem, vmem, HBM),
         scratch_shapes=[
             segs,

time: 475 us -> 454 us (0.956)
  the two profiles are of different devices: /device:TPU:22 before, /device:TPU:0 now
where the time goes in v5:
time: 454 us; the launch traced here: 447 us
  Pallas kernels  425 us (94%)
  other arithmetic  11.2 us (2%)
  local copies, waits for them, and re-layouts  9.25 us (2%)
    pallas_call x1, Pallas kernels, closing_call(): pl.pallas_call(partial(closing, bits), out_shape=(jax.ShapeDtypeStruct((m...  176 us
    pallas_call x1, Pallas kernels, middle_call(): pl.pallas_call(partial(middle, bits), out_shape=(wide_rows, jax.ShapeDtyp...  157 us
    pallas_call x1, Pallas kernels, opening_call(): pl.pallas_call(opening, out_shape=(narrow, narrow, narrow_wide, narrow_wi...  92.5 us
  transfers between devices with their start and end apart: 1, of which 0 were waited for; matrix products, arithmetic and copies ran while one was open for 3% of the time, Pallas kernels for 39%

profile of v5, /device:TPU:0, one launch (start us, length us, event | category | flops | bytes accessed | tf_op | source)
XLA Modules:
  0.0 446.7 jit_solution(13907529073925984003)
XLA Ops:
  0.6 1.3 reshape.39.parents
  1.9 0.7 broadcast_in_dim.17
  2.6 0.6 broadcast_in_dim_reshape.3.scale_ref.refs_6_
  3.3 92.5 %opening.1 = (bf16[1024,256]{1,0:T(8,128)(2,1)}, bf16[1024,256]{1,0:T(8,128)(2,1)}, f32[1024,256]{1,0:T(8,128)}, f32[1024,256]{1,0:T(8,128)}, bf16[1024,256]{1,0...) custom-call(s32[64]{0:T(128)} %reshape.39.parents, ...), custom_call_target="tpu_custom_call" | custom-call | flops 60000002048 | bytes 20971520 | tf_op jit(solution)/shard_map/opening/pallas_call | solution.py:280
  95.8 156.5 %middle.1 = (bf16[2,1024,1024]{2,1,0:T(8,128)(2,1)}, f32[2,1024,256]{2,1,0:T(8,128)}, f32[2,256,1024]{2,1,0:T(8,128)}, f32[2,256,1024]{2,1,0:T(8,128)}, bf16[2,2...) custom-call(bf16[1024,256]{1,0:T(8,128)(2,1)} %get-tuple-element.34.os0.refs_2_, ...), custom_call_target="tpu_custom_call" | custom-call | flops 99999997952 | bytes 41943040 | tf_op jit(solution)/shard_map/middle/pallas_call | solution.py:756
  252.3 0.7 collective-permute-start
  253.1 175.6 %closing.1 = (f32[2,256,1024]{2,1,0:T(8,128)}, bf16[4,1024,256]{2,1,0:T(8,128)(2,1)}, f32[8,1024]{1,0:T(8,128)}, bf16[2,4,256,1024]{3,2,1,0:T(8,128)(2,1)}) custom-call(s32[64]{0:T(128)} %reshape.39.parents, bf16[1024,256]{1,0:T(8,128)(2,1)} %get-tuple-element.39.refs_0_, bf16[1024,256]{1,0:T(8,128)(2,1)} %get-tuple-element.40.refs_1_, ...), custom_call_target="tpu_custom_call" | custom-call | flops 120000004096 | bytes 31457280 | tf_op jit(solution)/shard_map/closing/pallas_call | solution.py:1261
  428.6 0.0 copy-start.2
  428.6 3.3 slice_convert_fusion
  432.0 1.1 convert_bitcast_fusion
  433.1 0.0 copy-done.2
  433.1 0.1 reshape_squeeze.3
  433.2 1.3 copy.23
  434.5 0.6 reduce_sum.9
  435.2 0.6 fusion.1
  435.8 2.7 fusion
  438.4 0.0 copy-start
  438.4 4.7 %bitcast_convert_fusion = (f32[1024,1024]{1,0:T(8,128)}, f32[1024,1024]{1,0:T(8,128)}) fusion(bf16[1,4,256,1024]{3,2,1,0:T(8,128)(2,1)S(1)} %get-tuple-element.68, bf16[1,4,256,1024]{3,2,1,0:T(8,128)(2,1)S(1)} %get-tuple-element.69), kind=kLoop, calls=%fused_computation | loop fusion | flops 2097152 | bytes 12582912 | tf_op jit(solution)/shard_map/convert_element_type | solution.py:1382
  443.2 0.0 collective-permute-done
  443.2 0.0 copy-done
  443.2 0.0 copy-start.1
  443.2 1.4 add_convert_fusion
  444.5 0.6 copy-done.1
  445.1 1.3 copy.25
  (1 shorter events, 0.0 us)
Async XLA Ops:
  252.3 190.8 %collective-permute-start = (bf16[2,256,1024]{2,1,0:T(8,128)(2,1)}, bf16[2,256,1024]{2,1,0:T(8,128)(2,1)S(1)}, u32[]{:S(2)}, u32[]{:S(2)}) collective-permute-start(bf16[2,256,1024]{2,1,0:T(8,128)(2,1)} %get-tuple-element.38), channel_id=1, source_target_pairs={{0,2},{1,3},{2,0},{3,1},{4,6},{5,7},{6,4},{7,5},{8,10},{9,11},{10,... | collective-permute-start | bytes 3145736 | tf_op jit(solution)/shard_map/ppermute | solution.py:31
  428.6 4.5 %copy-start.2 = (f32[8,1024]{1,0:T(8,128)S(1)}, f32[8,1024]{1,0:T(8,128)}, u32[]{:S(2)}) copy-start(f32[8,1024]{1,0:T(8,128)} %get-tuple-element.54) | copy-start | bytes 98308
  438.4 4.7 %copy-start = (f32[2,256,1024]{2,1,0:T(8,128)S(1)}, f32[2,256,1024]{2,1,0:T(8,128)}, u32[]{:S(2)}) copy-start(f32[2,256,1024]{2,1,0:T(8,128)} %get-tuple-element.37) | copy-start | bytes 6291460
  443.2 2.0 copy-start.1

commit v6 on v5

--- a/solution.py
+++ b/solution.py
@@ -593,6 +593,8 @@
     first_grad(1)
     group = hidden // (shares.shape[0] // 2)
 
+    line = min(32, group // 2 ** len(bits))
+
     class Chain:
         def __init__(self, number):
             self.number, self.which = number, number // (hidden // group)
@@ -607,12 +609,12 @@
             where = self.at
 
             def one(i):
-                src = pl.ds(pl.multiple_of(away + i * 16, 16), 16)
-                staged[self.which, pl.ds(pl.multiple_of(where + i * 16, 16), 16), :] = act[
+                src = pl.ds(pl.multiple_of(away + i * line, line), line)
+                staged[self.which, pl.ds(pl.multiple_of(where + i * line, line), line), :] = act[
                     self.which, src, :
                 ].astype(BF)
 
-            each(half // 16, one)
+            each(half // line, one)
             slot = pl.ds(where, half)
             self.copy = remote(
                 staged.at[self.which, slot, :], arrived.at[self.which, slot, :], dp_peer(mask)
@@ -625,17 +627,17 @@
             base, where, last = self.base, self.at, self.step == len(bits)
 
             def one(i):
-                mine = pl.ds(pl.multiple_of(base + i * 16, 16), 16)
+                mine = pl.ds(pl.multiple_of(base + i * line, line), line)
                 total = act[self.which, mine, :] + arrived[
-                    self.which, pl.ds(pl.multiple_of(where + i * 16, 16), 16), :
+                    self.which, pl.ds(pl.multiple_of(where + i * line, line), line), :
                 ].astype(F32)
                 if last:
-                    at = self.start + base - self.first + i * 16
-                    staged[self.which, pl.ds(pl.multiple_of(at, 16), 16), :] = total.astype(BF)
+                    at = self.start + base - self.first + i * line
+                    staged[self.which, pl.ds(pl.multiple_of(at, line), line), :] = total.astype(BF)
                 else:
                     act[self.which, mine, :] = total
 
-            each(self.size // 16, one)
+            each(self.size // line, one)
             self.at += self.size
             if self.step == 1:
                 self.first = base

time: 454 us -> 454 us (level)
  no operation moved by 1% of the time
where the time goes in v6:
time: 454 us; the launch traced here: 446 us
  Pallas kernels  424 us (93%)
  other arithmetic  11.2 us (2%)
  local copies, waits for them, and re-layouts  9.25 us (2%)
    pallas_call x1, Pallas kernels, closing_call(): pl.pallas_call(partial(closing, bits), out_shape=(jax.ShapeDtypeStruct((m...  175 us
    pallas_call x1, Pallas kernels, middle_call(): pl.pallas_call(partial(middle, bits), out_shape=(wide_rows, jax.ShapeDtyp...  156 us
    pallas_call x1, Pallas kernels, opening_call(): pl.pallas_call(opening, out_shape=(narrow, narrow, narrow_wide, narrow_wi...  92.5 us
  transfers between devices with their start and end apart: 1, of which 0 were waited for; matrix products, arithmetic and copies ran while one was open for 3% of the time, Pallas kernels for 39%

profile of v6, /device:TPU:0, one launch (start us, length us, event | category | flops | bytes accessed | tf_op | source)
XLA Modules:
  0.0 446.3 jit_solution(6553765347571089429)
XLA Ops:
  0.6 1.3 reshape.39.parents
  1.9 0.7 broadcast_in_dim.17
  2.6 0.6 broadcast_in_dim_reshape.3.scale_ref.refs_6_
  3.3 92.5 %opening.1 = (bf16[1024,256]{1,0:T(8,128)(2,1)}, bf16[1024,256]{1,0:T(8,128)(2,1)}, f32[1024,256]{1,0:T(8,128)}, f32[1024,256]{1,0:T(8,128)}, bf16[1024,256]{1,0...) custom-call(s32[64]{0:T(128)} %reshape.39.parents, ...), custom_call_target="tpu_custom_call" | custom-call | flops 60000002048 | bytes 20971520 | tf_op jit(solution)/shard_map/opening/pallas_call | solution.py:280
  95.8 156.3 %middle.1 = (bf16[2,1024,1024]{2,1,0:T(8,128)(2,1)}, f32[2,1024,256]{2,1,0:T(8,128)}, f32[2,256,1024]{2,1,0:T(8,128)}, f32[2,256,1024]{2,1,0:T(8,128)}, bf16[2,2...) custom-call(bf16[1024,256]{1,0:T(8,128)(2,1)} %get-tuple-element.34.os0.refs_2_, ...), custom_call_target="tpu_custom_call" | custom-call | flops 99999997952 | bytes 41943040 | tf_op jit(solution)/shard_map/middle/pallas_call | solution.py:758
  252.0 0.8 collective-permute-start
  252.9 175.5 %closing.1 = (f32[2,256,1024]{2,1,0:T(8,128)}, bf16[4,1024,256]{2,1,0:T(8,128)(2,1)}, f32[8,1024]{1,0:T(8,128)}, bf16[2,4,256,1024]{3,2,1,0:T(8,128)(2,1)}) custom-call(s32[64]{0:T(128)} %reshape.39.parents, bf16[1024,256]{1,0:T(8,128)(2,1)} %get-tuple-element.39.refs_0_, bf16[1024,256]{1,0:T(8,128)(2,1)} %get-tuple-element.40.refs_1_, ...), custom_call_target="tpu_custom_call" | custom-call | flops 120000004096 | bytes 31457280 | tf_op jit(solution)/shard_map/closing/pallas_call | solution.py:1263
  428.3 0.0 copy-start.2
  428.3 3.3 slice_convert_fusion
  431.7 1.1 convert_bitcast_fusion
  432.8 0.0 copy-done.2
  432.8 0.1 reshape_squeeze.3
  432.9 1.3 copy.23
  434.2 0.6 reduce_sum.9
  434.8 0.6 fusion.1
  435.5 2.7 fusion
  438.1 0.0 copy-start
  438.1 4.7 %bitcast_convert_fusion = (f32[1024,1024]{1,0:T(8,128)}, f32[1024,1024]{1,0:T(8,128)}) fusion(bf16[1,4,256,1024]{3,2,1,0:T(8,128)(2,1)S(1)} %get-tuple-element.68, bf16[1,4,256,1024]{3,2,1,0:T(8,128)(2,1)S(1)} %get-tuple-element.69), kind=kLoop, calls=%fused_computation | loop fusion | flops 2097152 | bytes 12582912 | tf_op jit(solution)/shard_map/convert_element_type | solution.py:1384
  442.8 0.0 collective-permute-done
  442.9 0.0 copy-done
  442.9 0.0 copy-start.1
  442.9 1.4 add_convert_fusion
  444.2 0.6 copy-done.1
  444.8 1.3 copy.25
  (1 shorter events, 0.0 us)
Async XLA Ops:
  252.0 190.8 %collective-permute-start = (bf16[2,256,1024]{2,1,0:T(8,128)(2,1)}, bf16[2,256,1024]{2,1,0:T(8,128)(2,1)S(1)}, u32[]{:S(2)}, u32[]{:S(2)}) collective-permute-start(bf16[2,256,1024]{2,1,0:T(8,128)(2,1)} %get-tuple-element.38), channel_id=1, source_target_pairs={{0,2},{1,3},{2,0},{3,1},{4,6},{5,7},{6,4},{7,5},{8,10},{9,11},{10,... | collective-permute-start | bytes 3145736 | tf_op jit(solution)/shard_map/ppermute | solution.py:31
  428.3 4.5 %copy-start.2 = (f32[8,1024]{1,0:T(8,128)S(1)}, f32[8,1024]{1,0:T(8,128)}, u32[]{:S(2)}) copy-start(f32[8,1024]{1,0:T(8,128)} %get-tuple-element.54) | copy-start | bytes 98308
  438.1 4.7 %copy-start = (f32[2,256,1024]{2,1,0:T(8,128)S(1)}, f32[2,256,1024]{2,1,0:T(8,128)}, u32[]{:S(2)}) copy-start(f32[2,256,1024]{2,1,0:T(8,128)} %get-tuple-element.37) | copy-start | bytes 6291460
  442.9 2.0 copy-start.1
